TPU v7x, 512 devices: a whole 4x8x8 slice. The times are simulated.
512 devices in a mesh: dp: 8 (over z_lo, core), ctx: 64 (over z_hi, y, x).
Axes of the slice: x: 4, y: 8, z: 8 (z_hi: 2, z_lo: 4; z = z_hi * 4 + z_lo), core: 2. Of those that a mesh axis runs over, the one named last changes fastest.
Arguments:
- queries: bfloat16 [32768, 4096], P(('dp', 'ctx')), parts along dimension 0, as said below
- keys: bfloat16 [32768, 512], P(('dp', 'ctx')), parts along dimension 0, as said below
- values: bfloat16 [32768, 512], P(('dp', 'ctx')), parts along dimension 0, may hold values from -6 to 6
Outputs:
- attended: bfloat16 [32768, 4096], P(('dp', 'ctx')), parts along dimension 0
There are 8 independent parts, one for each index of `dp`. A program takes and returns all parts, laid end to end along the dimension named above; each array names one. Nothing has to cross between parts.
Inputs may be any that keep to these rules, and one draw needn't show every extreme that they name: `queries`: entries lie between -310 / sqrt(128) and 310 / sqrt(128). `keys`: entries lie between -6 and 6.
All inputs are finite; a program needn't handle non-finite values.
Results may differ from a plain program's by a relative error of at most 0.0035.
Values may be sent and summed in bfloat16 or wider, within the bound.
No kernel may reach another device: no remote copies, remote signals or barrier semaphores. Data moves between devices by JAX's collectives and lax.ppermute only.
A program may use at most 128 MiB of HBM per device.

v0:
```python
import math

import jax
import jax.numpy as jnp
from jax import lax
from jax.sharding import PartitionSpec as P

QH = 32
KVH = 4
HD = 128


def fresh_state(length, group_size):
    return (
        jnp.zeros((length, KVH, group_size, HD), jnp.float32),
        jnp.full((KVH, group_size, length), -1e30, jnp.float32),
        jnp.zeros((KVH, group_size, length), jnp.float32),
    )


def absorb(carry_state, query_block, query_pos, key_piece, value_piece):
    summed, running_max, denominator = carry_state
    key_heads = key_piece.reshape(key_piece.shape[0], KVH, HD)
    value_heads = value_piece.reshape(value_piece.shape[0], KVH, HD)
    scores = jnp.einsum(
        "tkgd,skd->kgts", query_block, key_heads, preferred_element_type=jnp.float32
    )
    scores = scores * (1.0 / math.sqrt(HD))
    key_pos = jnp.arange(key_heads.shape[0], dtype=jnp.int32)
    scores = jnp.where(key_pos[None, :] <= query_pos[:, None], scores, -jnp.inf)
    new_max = jnp.maximum(running_max, scores.max(-1))
    weights = jnp.exp(scores - new_max[..., None])
    denominator = weights.sum(-1)
    mixed_values = jnp.einsum(
        "kgts,skd->tkgd",
        weights.astype(jnp.bfloat16),
        value_heads,
        preferred_element_type=jnp.float32,
    )
    summed = mixed_values
    return (summed, new_max, denominator)


def guarded(carry_state, query_block, query_pos, key_piece, value_piece, offset):
    return lax.cond(
        offset <= query_pos[-1],
        lambda kept: absorb(kept, query_block, query_pos, key_piece, value_piece),
        lambda kept: kept,
        carry_state,
    )


def finish(carry_state):
    summed, running_max, denominator = carry_state
    result = summed / jnp.transpose(denominator, (2, 0, 1))[..., None]
    return result.reshape(summed.shape[0], QH * HD).astype(jnp.bfloat16)


def local(queries, keys, values):
    local_rows = queries.shape[0]
    my_index = lax.axis_index("ctx")
    group_size = QH // KVH
    own_pos = my_index * local_rows + jnp.arange(local_rows, dtype=jnp.int32)
    query_sets = ((queries.reshape(local_rows, KVH, group_size, HD), own_pos),)
    initial = tuple((fresh_state(entry[1].shape[0], group_size) for entry in query_sets))
    pieces = (
        lax.all_gather(keys, "ctx", axis=0, tiled=True),
        lax.all_gather(values, "ctx", axis=0, tiled=True),
    )
    offset = jnp.int32(0)
    states = tuple(
        (
            guarded(
                initial[number],
                query_sets[number][0],
                query_sets[number][1],
                pieces[0],
                pieces[1],
                offset,
            )
            for number in range(len(query_sets))
        )
    )
    return finish(states[0])


def solution(mesh):
    in_specs = (P(("dp", "ctx"), None), P(("dp", "ctx"), None), P(("dp", "ctx"), None))
    out_specs = P(("dp", "ctx"), None)
    return jax.shard_map(local, mesh=mesh, in_specs=in_specs, out_specs=out_specs, check_vma=False)
```

profile of v0, /device:TPU:4, one launch (start us, length us, event | category | flops | bytes accessed | tf_op | source)
XLA Modules:
  0.0 402.2 jit_solution(12471639932094628450)
XLA Ops:
  6.5 0.0 all-gather.3.cloned.1.call-start
  6.5 0.7 all-gather.3.cloned.1.call-update
  7.3 0.0 all-gather.5.cloned.1.call-start
  7.3 0.7 all-gather.5.cloned.1.call-update
  8.0 0.6 slice.3
  9.3 164.9 %all-gather.3.cloned.1.call-done = bf16[4096,512]{1,0:T(8,128)(2,1)} async-done(((bf16[64,512]{1,0:T(8,128)(2,1)}), bf16[4096,512]{1,0:T(8,128)(2,1)}) %all-gather.3.cloned.1.call-update) | async-done | bytes 4194320 | tf_op jit(solution)/shard_map/all_gather | solution.py:67
  174.1 156.1 %all-gather.5.cloned.1.call-done = bf16[4096,512]{1,0:T(8,128)(2,1)} async-done(((bf16[64,512]{1,0:T(8,128)(2,1)}), bf16[4096,512]{1,0:T(8,128)(2,1)}) %all-gather.5.cloned.1.call-update) | async-done | bytes 4194320 | tf_op jit(solution)/shard_map/all_gather | solution.py:68
  330.3 63.4 %conditional.1 = (f32[64,4,8,128]{3,0,2,1:T(8,128)S(1)}, f32[4,8,64]{2,1,0:T(8,128)S(1)}) conditional(s32[]{:T(128)} %bitcast.4, () %tuple.13, (s32[64]{0:T(128)S(1)}, bf16[4096,512]{1,0:T(8,128)(2,1)}, bf16[64,4096]{1,0:T(8,128)(2,1)}, bf16[4096,512]{1,0:T(8,128)(2,1)}) %tuple.14), branch_computations={%region_0.0_spmd, %region_1.4_spmd} | conditional | flops 4387502080 | bytes 129548560 | solution.py:45
  330.3 0.2 iota_compare_fusion
  330.5 6.9 %reshape.18 = bf16[4096,4,128]{2,1,0:T(4,128)(2,1)} reshape(bf16[4096,512]{1,0:T(8,128)(2,1)} %get-tuple-element.15) | data formatting | bytes 8388608 | tf_op jit(solution)/shard_map/cond/branch_1_fun/reshape | solution.py:23
  337.4 1.1 copy.15
  338.5 16.7 %fusion.2 = (f32[4,8,64]{2,1,0:T(8,128)S(1)}, f32[4,4096,64,8]{1,2,3,0:T(8,128)}) fusion(pred[64,4096]{1,0:T(8,128)(4,1)S(1)} %iota_compare_fusion, bf16[64,4,8,128]{3,2,1,0:T(8,128)(2,1)S(1)} %bitcast.27, bf16[4096,4,128,1]{2,1,0,3:T(4,128)(2,1)} %bitcast.25), kind=kOutput, calls=%fused_computation.4 | convolution fusion | flops 2172647424 | bytes 38543360 | tf_op jit(solution)/shard_map/cond/branch_1_fun/tkgd,skd->kgts/dot_general | solution.py:25
  355.2 15.4 %fusion = f32[4,8,64]{2,1,0:T(8,128)S(1)} fusion(f32[4,4096,64,8]{1,2,3,0:T(8,128)} %get-tuple-element.25, f32[4,8,64]{2,1,0:T(8,128)S(1)} %broadcast_maximum_fusion, pred[64,4096]{1,0:T(8,128)(4,1)S(1)} %iota_compare_fusion), kind=kLoop, calls=%fused_computation.2 | loop fusion | flops 33552384 | bytes 33832960 | tf_op jit(solution)/shard_map/cond/branch_1_fun/reduce_sum | solution.py:33
  370.5 6.9 %reshape.20 = bf16[4096,4,128]{2,1,0:T(4,128)(2,1)} reshape(bf16[4096,512]{1,0:T(8,128)(2,1)} %get-tuple-element.17) | data formatting | bytes 8388608 | tf_op jit(solution)/shard_map/cond/branch_1_fun/reshape | solution.py:24
  377.4 16.3 %fusion.9 = f32[64,4,8,128]{3,0,2,1:T(8,128)S(1)} fusion(bf16[4096,4,128,1]{2,1,0,3:T(4,128)(2,1)} %bitcast.26, f32[4,4096,64,8]{1,2,3,0:T(8,128)} %get-tuple-element.25, f32[4,8,64]{2,1,0:T(8,128)S(1)} %broadcast_maximum_fusion, pred[64,4096]{1,0:T(8,128)(4,1)S(1)} %iota_compare_fusion), kind=kOutput, calls=%fused_computation.10 | convolution fusion | flops 2181038080 | bytes 39067648 | tf_op jit(solution)/shard_map/cond/branch_1_fun/kgts,skd->tkgd/dot_general | solution.py:34
  393.7 0.3 divide_convert_fusion
  394.0 0.3 copy.8
  394.4 1.0 copy.30
  (2 shorter events, 0.0 us)
Async XLA Ops:
  6.5 167.6 %all-gather.3.cloned.1.call-start = ((), (), s32[]{:S(2)}) async-start(), calls=%async_computation | async-start | bytes 4259840 | tf_op jit(solution)/shard_map/all_gather | solution.py:67
  7.3 323.0 %all-gather.5.cloned.1.call-start = ((), (), s32[]{:S(2)}) async-start(), calls=%async_computation.1 | async-start | bytes 4259840 | tf_op jit(solution)/shard_map/all_gather | solution.py:68
Sparse Core Ops, SparseCore 0:
  11.8 162.2 all-gather.2
  178.7 151.5 all-gather.4
where the time goes:
time: 403 us; the launch traced here: 402 us
  waiting for transfers between devices  322 us (80%)
  matrix products  32.9 us (8%)
  local copies, waits for them, and re-layouts  16.8 us (4%)
  other arithmetic  15.9 us (4%)
  between operations  14.1 us (3%)
    all_gather x1, waiting for transfers between devices, local(): lax.all_gather(keys, 'ctx', axis=0, tiled=True)  165 us
    all_gather x1, waiting for transfers between devices, local(): lax.all_gather(values, 'ctx', axis=0, tiled=True)  156 us
    dot_general x1, matrix products, absorb(): jnp.einsum('tkgd,skd->kgts', query_block, key_heads, preferred_element_ty...  16.7 us
    dot_general x1, matrix products, absorb(): jnp.einsum('kgts,skd->tkgd', weights.astype(jnp.bfloat16), value_heads, p...  16.3 us
    reduce_sum x1, other arithmetic, absorb(): denominator = weights.sum(-1)  15.4 us
  transfers between devices with their start and end apart: 2, of which 2 were waited for; matrix products, arithmetic and copies ran while one was open for 0% of the time, Pallas kernels for 0%

commit v1 on v0

v1 whole, which is shorter than its diff:
```python
import functools
import math

import jax
import jax.numpy as jnp
from jax import lax
from jax.experimental import pallas as pl
from jax.experimental.pallas import tpu as pltpu
from jax.sharding import PartitionSpec as P

QH = 32
KVH = 4
HD = 128
GROUP = QH // KVH
NZ, NY, NX = 2, 8, 4
ROWS = 256
SCALE = math.log2(math.e) / math.sqrt(HD)
NEG = -1e30
QK = (((1,), (1,)), ((), ()))
UNROLL = 4


def index(z, y, x):
    return z * (NY * NX) + y * NX + x


X_GROUPS = [[index(z, y, x) for x in range(NX)] for z in range(NZ) for y in range(NY)]
Z_GROUPS = [[index(z, y, x) for z in range(NZ)] for y in range(NY) for x in range(NX)]


def ring(step):
    return [
        (index(z, y, x), index(z, (y + step) % NY, x))
        for z in range(NZ)
        for y in range(NY)
        for x in range(NX)
    ]


def columns(head):
    return pl.ds(pl.multiple_of(head * HD, HD), HD)


def lane_sums(weights):
    total = weights[:, :HD]
    for at in range(HD, weights.shape[1], HD):
        total = total + weights[:, at : at + HD]
    return total


def own_kernel(place, x_ref, kv_ref, acc_ref, max_ref, sum_ref):
    def head(j, carry):
        cols = columns(j)
        scores = lax.dot_general(
            x_ref[:, cols], kv_ref[:, :HD], QK, preferred_element_type=jnp.float32
        )
        row = lax.broadcasted_iota(jnp.int32, scores.shape, 0)
        col = lax.broadcasted_iota(jnp.int32, scores.shape, 1)
        scores = jnp.where(col <= row + place[0] * ROWS, scores, NEG)
        peak = jnp.max(scores, axis=1, keepdims=True) * SCALE
        weights = jnp.exp2(scores * SCALE - peak)
        sum_ref[:, cols] = lane_sums(weights)
        acc_ref[:, cols] = jnp.dot(
            weights.astype(jnp.bfloat16),
            kv_ref[:, HD:],
            preferred_element_type=jnp.float32,
        )
        max_ref[:, cols] = jnp.broadcast_to(peak, (ROWS, HD))
        return carry

    lax.fori_loop(0, GROUP, head, 0, unroll=UNROLL)


def absorb(n, x_ref, kv_ref, acc_in, max_in, sum_in, acc_ref, max_ref, sum_ref):
    def head(j, carry):
        cols = columns(j)
        scores = lax.dot_general(
            x_ref[:, cols], kv_ref[:n, :HD], QK, preferred_element_type=jnp.float32
        )
        old = max_in[:, cols]
        peak = jnp.maximum(old, jnp.max(scores, axis=1, keepdims=True) * SCALE)
        keep = jnp.exp2(old - peak)
        weights = jnp.exp2(scores * SCALE - jnp.tile(peak, (1, n // HD)))
        sum_ref[:, cols] = sum_in[:, cols] * keep + lane_sums(weights)
        acc_ref[:, cols] = acc_in[:, cols] * keep + jnp.dot(
            weights.astype(jnp.bfloat16),
            kv_ref[:n, HD:],
            preferred_element_type=jnp.float32,
        )
        max_ref[:, cols] = peak
        return carry

    lax.fori_loop(0, GROUP, head, 0, unroll=UNROLL)


def absorb_if_needed(shift, place, x_ref, kv_ref, ins, outs):
    z, y = place[0], place[1]
    source = lax.rem(y - shift + NY, NY)
    before = source < y

    @pl.when(jnp.logical_and(z == 1, before))
    def _():
        absorb(2 * ROWS, x_ref, kv_ref, *ins, *outs)

    @pl.when(jnp.logical_and(z == 1, jnp.logical_not(before)))
    def _():
        absorb(ROWS, x_ref, kv_ref, *ins, *outs)

    @pl.when(jnp.logical_and(z == 0, before))
    def _():
        absorb(ROWS, x_ref, kv_ref, *ins, *outs)


def more_kernel(shift, place, x_ref, kv_ref, a_in, m_in, s_in, a_out, m_out, s_out):
    absorb_if_needed(
        shift, place, x_ref, kv_ref, (a_in, m_in, s_in), (a_out, m_out, s_out)
    )


def last_kernel(
    shift, place, x_ref, kv_ref, a_in, m_in, s_in, o_ref, a_out, m_out, s_out
):
    absorb_if_needed(
        shift, place, x_ref, kv_ref, (a_in, m_in, s_in), (a_out, m_out, s_out)
    )

    def head(j, carry):
        cols = columns(j)
        total = jnp.sum(s_out[:, cols], axis=1, keepdims=True)
        o_ref[:, cols] = (a_out[:, cols] / total).astype(jnp.bfloat16)
        return carry

    lax.fori_loop(0, GROUP, head, 0, unroll=UNROLL)


VMEM = pl.BlockSpec(memory_space=pltpu.VMEM)
SMEM = pl.BlockSpec(memory_space=pltpu.SMEM)
STATE = [jax.ShapeDtypeStruct((ROWS, GROUP * HD), jnp.float32)] * 3
PARAMS = pltpu.CompilerParams(vmem_limit_bytes=24 << 20)
COST = pl.CostEstimate(
    flops=4 * ROWS * GROUP * 2 * ROWS * HD,
    bytes_accessed=8 << 20,
    transcendentals=ROWS * GROUP * 2 * ROWS,
)


def own_block(place, x, kv):
    return pl.pallas_call(
        own_kernel,
        out_shape=STATE,
        in_specs=[SMEM, VMEM, VMEM],
        out_specs=[VMEM] * 3,
        compiler_params=PARAMS,
        cost_estimate=COST,
        name="own_block",
    )(place, x, kv)


def more_block(shift, place, x, kv, state):
    return pl.pallas_call(
        functools.partial(more_kernel, shift),
        out_shape=STATE,
        in_specs=[SMEM] + [VMEM] * 5,
        out_specs=[VMEM] * 3,
        input_output_aliases={3: 0, 4: 1, 5: 2},
        compiler_params=PARAMS,
        cost_estimate=COST,
        name="more_block",
    )(place, x, kv, *state)


def last_block(shift, place, x, kv, state):
    return pl.pallas_call(
        functools.partial(last_kernel, shift),
        out_shape=[jax.ShapeDtypeStruct((ROWS, GROUP * HD), jnp.bfloat16)] + STATE,
        in_specs=[SMEM] + [VMEM] * 5,
        out_specs=[VMEM] * 4,
        input_output_aliases={3: 1, 4: 2, 5: 3},
        compiler_params=PARAMS,
        cost_estimate=COST,
        name="last_block",
    )(place, x, kv, *state)[0]


def local(queries, keys, values):
    rows = queries.shape[0]
    me = lax.axis_index("ctx")
    place = jnp.stack([me // (NY * NX), (me // NX) % NY]).astype(jnp.int32)
    by_head = jnp.concatenate(
        [
            queries.reshape(rows, KVH, GROUP * HD),
            keys.reshape(rows, KVH, HD),
            values.reshape(rows, KVH, HD),
        ],
        axis=2,
    ).transpose(1, 0, 2)
    x = lax.all_to_all(by_head, "ctx", 0, 0, axis_index_groups=X_GROUPS, tiled=True)
    x = x.reshape(ROWS, (GROUP + 2) * HD)
    kv = lax.all_gather(
        x[:, GROUP * HD :], "ctx", axis=0, tiled=True, axis_index_groups=Z_GROUPS
    )
    x = x[:, : GROUP * HD]
    up = down = kv
    arrived = []
    for step in range(1, NY // 2):
        up = lax.ppermute(up, "ctx", ring(1))
        down = lax.ppermute(down, "ctx", ring(-1))
        arrived += [(step, up), (-step, down)]
    up = lax.ppermute(up, "ctx", ring(1))
    state = own_block(place, x, kv)
    for shift, block in arrived:
        state = more_block(shift, place, x, block, state)
    out = last_block(NY // 2, place, x, up, state)
    out = lax.all_to_all(
        out.reshape(NX, rows, GROUP * HD),
        "ctx",
        0,
        0,
        axis_index_groups=X_GROUPS,
        tiled=True,
    )
    return out.transpose(1, 0, 2).reshape(rows, QH * HD)


def solution(mesh):
    spec = P(("dp", "ctx"), None)
    return jax.shard_map(
        local, mesh=mesh, in_specs=(spec,) * 3, out_specs=spec, check_vma=False
    )
```

time: 403 us -> 97.3 us (0.24)
  the two profiles are of different devices: /device:TPU:4 before, /device:TPU:440 now
where the time goes in v1:
time: 97.3 us; the launch traced here: 96.9 us
  blocking collectives  36.6 us (38%)
  Pallas kernels  28.2 us (29%)
  starting transfers between devices  23.6 us (24%)
  waiting for transfers between devices  6.14 us (6%)
  local copies, waits for them, and re-layouts  2.04 us (2%)
    pallas_call x6, Pallas kernels, more_block(): pl.pallas_call(functools.partial(more_kernel, shift), out_shape=STATE, in...  21 us
    ppermute x4, starting transfers between devices, local(): up = lax.ppermute(up, 'ctx', ring(1))  15.3 us
    all_to_all x1, blocking collectives, local(): lax.all_to_all(by_head, 'ctx', 0, 0, axis_index_groups=X_GROUPS, tiled=True)  15 us
    all_gather x1, blocking collectives, local(): lax.all_gather(x[:, GROUP * HD:], 'ctx', axis=0, tiled=True, axis_index_g...  11.1 us
    all_to_all x1, blocking collectives, local(): lax.all_to_all(out.reshape(NX, rows, GROUP * HD), 'ctx', 0, 0, axis_index...  10.5 us
    ppermute x3, starting transfers between devices, local(): down = lax.ppermute(down, 'ctx', ring(-1))  8.27 us
    ppermute x4, waiting for transfers between devices, local(): up = lax.ppermute(up, 'ctx', ring(1))  6.13 us
    pallas_call x1, Pallas kernels, last_block(): pl.pallas_call(functools.partial(last_kernel, shift), out_shape=[jax.Shap...  3.9 us
  transfers between devices with their start and end apart: 7, of which 2 were waited for; matrix products, arithmetic and copies ran while one was open for 0% of the time, Pallas kernels for 25%

profile of v1, /device:TPU:440, one launch (start us, length us, event | category | flops | bytes accessed | tf_op | source)
XLA Modules:
  0.0 96.9 jit_solution(7049172607434830866)
XLA Ops:
  0.0 0.0 copy-start
  0.0 0.0 copy-start.1
  0.0 1.1 %copy.36 = bf16[8,4,8,1024]{3,2,0,1:T(8,128)(2,1)S(1)} copy(bf16[8,4,8,1024]{3,2,1,0:T(8,128)(2,1)} %bitcast.28) | data formatting | bytes 1048576 | tf_op jit(solution)/shard_map/reshape | solution.py:191
  1.1 0.0 copy-done
  1.1 0.0 copy-done.1
  1.2 0.1 maximum_bitcast_fusion
  1.2 15.0 %all_to_all.10 = bf16[4,64,1280]{2,1,0:T(8,128)(2,1)S(1)} all-to-all(bf16[4,64,1280]{2,1,0:T(8,128)(2,1)S(1)} %maximum_bitcast_fusion), channel_id=1, replica_groups={{0,1,2,3},{4,5,6,7},{8,9,10,11},{12,13,14,15},{16,17,18,19},{20,21,22,2..., dimensions={0} | all-to-all | bytes 1310720 | tf_op jit(solution)/shard_map/all_to_all | solution.py:197
  16.2 11.1 %all_gather.3.kv_ref = bf16[512,256]{1,0:T(8,128)(2,1)S(1)} all-gather(bf16[256,256]{1,0:T(8,128)(2,1)S(1)} %slice.9), channel_id=1, replica_groups={{0,32},{1,33},{2,34},{3,35},{4,36},{5,37},{6,38},{7,39},{8,40},{9,41},{..., dimensions={0}, use_global_device_ids=true | all-gather | bytes 393216 | tf_op jit(solution)/shard_map/all_gather | solution.py:199
  27.3 1.9 %collective-permute-start = (bf16[512,256]{1,0:T(8,128)(2,1)S(1)}, bf16[512,256]{1,0:T(8,128)(2,1)S(1)}, u32[]{:S(2)}, u32[]{:S(2)}) collective-permute-start(bf16[512,256]{1,0:T(8,128)(2,1)S(1)} %all_gather.3.kv_ref), channel_id=1, source_target_pairs={{0,4},{1,5},{2,6},{3,7},{4,8},{5,9},{6,10},{7,11},{8,12},{9,13},{1... | collective-permute-start | bytes 786440 | tf_op jit(solution)/shard_map/ppermute | solution.py:206
  29.2 3.9 %collective-permute-start.4 = (bf16[512,256]{1,0:T(8,128)(2,1)S(1)}, bf16[512,256]{1,0:T(8,128)(2,1)S(1)}, u32[]{:S(2)}, u32[]{:S(2)}) collective-permute-start(bf16[512,256]{1,0:T(8,128)(2,1)S(1)} %all_gather.3.kv_ref), channel_id=1, source_target_pairs={{0,28},{1,29},{2,30},{3,31},{4,0},{5,1},{6,2},{7,3},{8,4},{9,5},{1... | collective-permute-start | bytes 786440 | tf_op jit(solution)/shard_map/ppermute | solution.py:207
  33.2 3.5 %collective-permute-done.kv_ref = bf16[512,256]{1,0:T(8,128)(2,1)S(1)} collective-permute-done((bf16[512,256]{1,0:T(8,128)(2,1)S(1)}, bf16[512,256]{1,0:T(8,128)(2,1)S(1)}, u32[]{:S(2)}, u32[]{:S(2)}) %collective-permute-start) | collective-permute-done | bytes 262176 | tf_op jit(solution)/shard_map/ppermute | solution.py:206
  36.7 3.4 %collective-permute-start.1 = (bf16[512,256]{1,0:T(8,128)(2,1)S(1)}, bf16[512,256]{1,0:T(8,128)(2,1)S(1)}, u32[]{:S(2)}, u32[]{:S(2)}) collective-permute-start(bf16[512,256]{1,0:T(8,128)(2,1)S(1)} %collective-permute-done.kv_ref), channel_id=1, source_target_pairs={{0,4},{1,5},{2,6},{3,7},{4,8},{5,9},{6,10},{7,11},{8,12},{9,13},{1... | collective-permute-start | bytes 786440 | tf_op jit(solution)/shard_map/ppermute | solution.py:206
  40.1 0.0 collective-permute-done.4.kv_ref
  40.1 2.4 %collective-permute-start.5 = (bf16[512,256]{1,0:T(8,128)(2,1)S(1)}, bf16[512,256]{1,0:T(8,128)(2,1)S(1)}, u32[]{:S(2)}, u32[]{:S(2)}) collective-permute-start(bf16[512,256]{1,0:T(8,128)(2,1)S(1)} %collective-permute-done.4.kv_ref), channel_id=1, source_target_pairs={{0,28},{1,29},{2,30},{3,31},{4,0},{5,1},{6,2},{7,3},{8,4},{9,5},{1... | collective-permute-start | bytes 786440 | tf_op jit(solution)/shard_map/ppermute | solution.py:207
  42.5 2.6 %collective-permute-done.1.kv_ref = bf16[512,256]{1,0:T(8,128)(2,1)S(1)} collective-permute-done((bf16[512,256]{1,0:T(8,128)(2,1)S(1)}, bf16[512,256]{1,0:T(8,128)(2,1)S(1)}, u32[]{:S(2)}, u32[]{:S(2)}) %collective-permute-start.1) | collective-permute-done | bytes 262176 | tf_op jit(solution)/shard_map/ppermute | solution.py:206
  45.2 4.9 %collective-permute-start.2 = (bf16[512,256]{1,0:T(8,128)(2,1)S(1)}, bf16[512,256]{1,0:T(8,128)(2,1)S(1)}, u32[]{:S(2)}, u32[]{:S(2)}) collective-permute-start(bf16[512,256]{1,0:T(8,128)(2,1)S(1)} %collective-permute-done.1.kv_ref), channel_id=1, source_target_pairs={{0,4},{1,5},{2,6},{3,7},{4,8},{5,9},{6,10},{7,11},{8,12},{9,13},{1... | collective-permute-start | bytes 786440 | tf_op jit(solution)/shard_map/ppermute | solution.py:206
  50.1 0.1 pad_add_fusion.place
  50.2 0.1 slice.8.x_ref
  50.2 0.0 collective-permute-done.5.kv_ref
  50.2 1.9 %collective-permute-start.6 = (bf16[512,256]{1,0:T(8,128)(2,1)S(1)}, bf16[512,256]{1,0:T(8,128)(2,1)S(1)}, u32[]{:S(2)}, u32[]{:S(2)}) collective-permute-start(bf16[512,256]{1,0:T(8,128)(2,1)S(1)} %collective-permute-done.5.kv_ref), channel_id=1, source_target_pairs={{0,28},{1,29},{2,30},{3,31},{4,0},{5,1},{6,2},{7,3},{8,4},{9,5},{1... | collective-permute-start | bytes 786440 | tf_op jit(solution)/shard_map/ppermute | solution.py:207
  52.2 3.3 %own_block.1 = (f32[256,1024]{1,0:T(8,128)S(1)}, f32[256,1024]{1,0:T(8,128)S(1)}, f32[256,1024]{1,0:T(8,128)S(1)}) custom-call(s32[2]{0:T(128)S(1)} %pad_add_fusion.place, bf16[256,1024]{1,0:T(8,128)(2,1)S(1)} %slice.8.x_ref, bf16[512,256]{1,0:T(8,128)(2,1)S(1)} %all_gather.3.kv_ref), custom_call_target="tpu_custom_call" | custom-call | flops 536870912 | bytes 8388608 | tf_op jit(solution)/shard_map/own_block/pallas_call | solution.py:148
  55.5 0.0 collective-permute-done.2.kv_ref
  55.5 5.1 %collective-permute-start.3 = (bf16[512,256]{1,0:T(8,128)(2,1)S(1)}, bf16[512,256]{1,0:T(8,128)(2,1)S(1)}, u32[]{:S(2)}, u32[]{:S(2)}) collective-permute-start(bf16[512,256]{1,0:T(8,128)(2,1)S(1)} %collective-permute-done.2.kv_ref), channel_id=1, source_target_pairs={{0,4},{1,5},{2,6},{3,7},{4,8},{5,9},{6,10},{7,11},{8,12},{9,13},{1... | collective-permute-start | bytes 786440 | tf_op jit(solution)/shard_map/ppermute | solution.py:209
  60.6 3.5 %more_block.6 = (f32[256,1024]{1,0:T(8,128)S(1)}, f32[256,1024]{1,0:T(8,128)S(1)}, f32[256,1024]{1,0:T(8,128)S(1)}) custom-call(s32[2]{0:T(128)S(1)} %pad_add_fusion.place, bf16[256,1024]{1,0:T(8,128)(2,1)S(1)} %slice.8.x_ref, bf16[512,256]{1,0:T(8,128)(2,1)S(1)} %collective-permute-done.kv_ref, ...), custom_call_target="tpu_custom_call", output_to_operand_aliasing={{0}: (3, {}), {1}: (4, {}), {2}: (5, {})} | custom-call | flops 536870912 | bytes 8388608 | tf_op jit(solution)/shard_map/more_block/pallas_call | solution.py:160
  64.1 3.5 %more_block.7 = (f32[256,1024]{1,0:T(8,128)S(1)}, f32[256,1024]{1,0:T(8,128)S(1)}, f32[256,1024]{1,0:T(8,128)S(1)}) custom-call(s32[2]{0:T(128)S(1)} %pad_add_fusion.place, bf16[256,1024]{1,0:T(8,128)(2,1)S(1)} %slice.8.x_ref, bf16[512,256]{1,0:T(8,128)(2,1)S(1)} %collective-permute-done.4.kv_ref, ...), custom_call_target="tpu_custom_call", output_to_operand_aliasing={{0}: (3, {}), {1}: (4, {}), {2}: (5, {})} | custom-call | flops 536870912 | bytes 8388608 | tf_op jit(solution)/shard_map/more_block/pallas_call | solution.py:160
  67.5 3.5 %more_block.8 = (f32[256,1024]{1,0:T(8,128)S(1)}, f32[256,1024]{1,0:T(8,128)S(1)}, f32[256,1024]{1,0:T(8,128)S(1)}) custom-call(s32[2]{0:T(128)S(1)} %pad_add_fusion.place, bf16[256,1024]{1,0:T(8,128)(2,1)S(1)} %slice.8.x_ref, bf16[512,256]{1,0:T(8,128)(2,1)S(1)} %collective-permute-done.1.kv_ref, ...), custom_call_target="tpu_custom_call", output_to_operand_aliasing={{0}: (3, {}), {1}: (4, {}), {2}: (5, {})} | custom-call | flops 536870912 | bytes 8388608 | tf_op jit(solution)/shard_map/more_block/pallas_call | solution.py:160
  71.0 3.6 %more_block.9 = (f32[256,1024]{1,0:T(8,128)S(1)}, f32[256,1024]{1,0:T(8,128)S(1)}, f32[256,1024]{1,0:T(8,128)S(1)}) custom-call(s32[2]{0:T(128)S(1)} %pad_add_fusion.place, bf16[256,1024]{1,0:T(8,128)(2,1)S(1)} %slice.8.x_ref, bf16[512,256]{1,0:T(8,128)(2,1)S(1)} %collective-permute-done.5.kv_ref, ...), custom_call_target="tpu_custom_call", output_to_operand_aliasing={{0}: (3, {}), {1}: (4, {}), {2}: (5, {})} | custom-call | flops 536870912 | bytes 8388608 | tf_op jit(solution)/shard_map/more_block/pallas_call | solution.py:160
  74.7 3.5 %more_block.10 = (f32[256,1024]{1,0:T(8,128)S(1)}, f32[256,1024]{1,0:T(8,128)S(1)}, f32[256,1024]{1,0:T(8,128)S(1)}) custom-call(s32[2]{0:T(128)S(1)} %pad_add_fusion.place, bf16[256,1024]{1,0:T(8,128)(2,1)S(1)} %slice.8.x_ref, bf16[512,256]{1,0:T(8,128)(2,1)S(1)} %collective-permute-done.2.kv_ref, ...), custom_call_target="tpu_custom_call", output_to_operand_aliasing={{0}: (3, {}), {1}: (4, {}), {2}: (5, {})} | custom-call | flops 536870912 | bytes 8388608 | tf_op jit(solution)/shard_map/more_block/pallas_call | solution.py:160
  78.1 0.0 collective-permute-done.6.kv_ref
  78.1 3.5 %more_block.11 = (f32[256,1024]{1,0:T(8,128)S(1)}, f32[256,1024]{1,0:T(8,128)S(1)}, f32[256,1024]{1,0:T(8,128)S(1)}) custom-call(s32[2]{0:T(128)S(1)} %pad_add_fusion.place, bf16[256,1024]{1,0:T(8,128)(2,1)S(1)} %slice.8.x_ref, bf16[512,256]{1,0:T(8,128)(2,1)S(1)} %collective-permute-done.6.kv_ref, ...), custom_call_target="tpu_custom_call", output_to_operand_aliasing={{0}: (3, {}), {1}: (4, {}), {2}: (5, {})} | custom-call | flops 536870912 | bytes 8388608 | tf_op jit(solution)/shard_map/more_block/pallas_call | solution.py:160
  81.6 0.0 collective-permute-done.3.kv_ref
  81.6 3.9 %last_block.1 = (bf16[256,1024]{1,0:T(8,128)(2,1)S(1)}, f32[256,1024]{1,0:T(8,128)S(1)}, f32[256,1024]{1,0:T(8,128)S(1)}, f32[256,1024]{1,0:T(8,128)S(1)}) custom-call(s32[2]{0:T(128)S(1)} %pad_add_fusion.place, bf16[256,1024]{1,0:T(8,128)(2,1)S(1)} %slice.8.x_ref, ...), custom_call_target="tpu_custom_call", output_to_operand_aliasing={{1}: (3, {}), {2}: (4, {}), {3}: (5, {})} | custom-call | flops 536870912 | bytes 8388608 | tf_op jit(solution)/shard_map/last_block/pallas_call | solution.py:173
  85.6 10.5 %all_to_all.11 = bf16[4,64,1024]{2,1,0:T(8,128)(2,1)S(1)} all-to-all(bf16[4,64,1024]{2,1,0:T(8,128)(2,1)S(1)} %bitcast.23), channel_id=1, replica_groups={{0,1,2,3},{4,5,6,7},{8,9,10,11},{12,13,14,15},{16,17,18,19},{20,21,22,2..., dimensions={0} | all-to-all | bytes 1048576 | tf_op jit(solution)/shard_map/all_to_all | solution.py:214
  96.0 0.8 copy.32
  (2 shorter events, 0.0 us)
Async XLA Ops:
  0.0 1.1 %copy-start = (bf16[64,512]{1,0:T(8,128)(2,1)S(1)}, bf16[64,512]{1,0:T(8,128)(2,1)}, u32[]{:S(2)}) copy-start(bf16[64,512]{1,0:T(8,128)(2,1)} %param.4) | copy-start | bytes 196612
  0.0 1.1 %copy-start.1 = (bf16[64,512]{1,0:T(8,128)(2,1)S(1)}, bf16[64,512]{1,0:T(8,128)(2,1)}, u32[]{:S(2)}) copy-start(bf16[64,512]{1,0:T(8,128)(2,1)} %param.5) | copy-start | bytes 196612
  27.3 9.3 %collective-permute-start = (bf16[512,256]{1,0:T(8,128)(2,1)S(1)}, bf16[512,256]{1,0:T(8,128)(2,1)S(1)}, u32[]{:S(2)}, u32[]{:S(2)}) collective-permute-start(bf16[512,256]{1,0:T(8,128)(2,1)S(1)} %all_gather.3.kv_ref), channel_id=1, source_target_pairs={{0,4},{1,5},{2,6},{3,7},{4,8},{5,9},{6,10},{7,11},{8,12},{9,13},{1... | collective-permute-start | bytes 786440 | tf_op jit(solution)/shard_map/ppermute | solution.py:206
  29.2 10.8 %collective-permute-start.4 = (bf16[512,256]{1,0:T(8,128)(2,1)S(1)}, bf16[512,256]{1,0:T(8,128)(2,1)S(1)}, u32[]{:S(2)}, u32[]{:S(2)}) collective-permute-start(bf16[512,256]{1,0:T(8,128)(2,1)S(1)} %all_gather.3.kv_ref), channel_id=1, source_target_pairs={{0,28},{1,29},{2,30},{3,31},{4,0},{5,1},{6,2},{7,3},{8,4},{9,5},{1... | collective-permute-start | bytes 786440 | tf_op jit(solution)/shard_map/ppermute | solution.py:207
  36.7 8.5 %collective-permute-start.1 = (bf16[512,256]{1,0:T(8,128)(2,1)S(1)}, bf16[512,256]{1,0:T(8,128)(2,1)S(1)}, u32[]{:S(2)}, u32[]{:S(2)}) collective-permute-start(bf16[512,256]{1,0:T(8,128)(2,1)S(1)} %collective-permute-done.kv_ref), channel_id=1, source_target_pairs={{0,4},{1,5},{2,6},{3,7},{4,8},{5,9},{6,10},{7,11},{8,12},{9,13},{1... | collective-permute-start | bytes 786440 | tf_op jit(solution)/shard_map/ppermute | solution.py:206
  40.1 10.1 %collective-permute-start.5 = (bf16[512,256]{1,0:T(8,128)(2,1)S(1)}, bf16[512,256]{1,0:T(8,128)(2,1)S(1)}, u32[]{:S(2)}, u32[]{:S(2)}) collective-permute-start(bf16[512,256]{1,0:T(8,128)(2,1)S(1)} %collective-permute-done.4.kv_ref), channel_id=1, source_target_pairs={{0,28},{1,29},{2,30},{3,31},{4,0},{5,1},{6,2},{7,3},{8,4},{9,5},{1... | collective-permute-start | bytes 786440 | tf_op jit(solution)/shard_map/ppermute | solution.py:207
  45.2 10.3 %collective-permute-start.2 = (bf16[512,256]{1,0:T(8,128)(2,1)S(1)}, bf16[512,256]{1,0:T(8,128)(2,1)S(1)}, u32[]{:S(2)}, u32[]{:S(2)}) collective-permute-start(bf16[512,256]{1,0:T(8,128)(2,1)S(1)} %collective-permute-done.1.kv_ref), channel_id=1, source_target_pairs={{0,4},{1,5},{2,6},{3,7},{4,8},{5,9},{6,10},{7,11},{8,12},{9,13},{1... | collective-permute-start | bytes 786440 | tf_op jit(solution)/shard_map/ppermute | solution.py:206
  50.2 27.9 %collective-permute-start.6 = (bf16[512,256]{1,0:T(8,128)(2,1)S(1)}, bf16[512,256]{1,0:T(8,128)(2,1)S(1)}, u32[]{:S(2)}, u32[]{:S(2)}) collective-permute-start(bf16[512,256]{1,0:T(8,128)(2,1)S(1)} %collective-permute-done.5.kv_ref), channel_id=1, source_target_pairs={{0,28},{1,29},{2,30},{3,31},{4,0},{5,1},{6,2},{7,3},{8,4},{9,5},{1... | collective-permute-start | bytes 786440 | tf_op jit(solution)/shard_map/ppermute | solution.py:207
  55.5 26.2 %collective-permute-start.3 = (bf16[512,256]{1,0:T(8,128)(2,1)S(1)}, bf16[512,256]{1,0:T(8,128)(2,1)S(1)}, u32[]{:S(2)}, u32[]{:S(2)}) collective-permute-start(bf16[512,256]{1,0:T(8,128)(2,1)S(1)} %collective-permute-done.2.kv_ref), channel_id=1, source_target_pairs={{0,4},{1,5},{2,6},{3,7},{4,8},{5,9},{6,10},{7,11},{8,12},{9,13},{1... | collective-permute-start | bytes 786440 | tf_op jit(solution)/shard_map/ppermute | solution.py:209

commit v2 on v1

--- a/solution.py
+++ b/solution.py
@@ -17,7 +17,6 @@
 SCALE = math.log2(math.e) / math.sqrt(HD)
 NEG = -1e30
 QK = (((1,), (1,)), ((), ()))
-UNROLL = 4
 
 
 def index(z, y, x):
@@ -37,10 +36,6 @@
     ]
 
 
-def columns(head):
-    return pl.ds(pl.multiple_of(head * HD, HD), HD)
-
-
 def lane_sums(weights):
     total = weights[:, :HD]
     for at in range(HD, weights.shape[1], HD):
@@ -48,15 +43,31 @@
     return total
 
 
+def scores_of(j, n, x_ref, kv_ref):
+    return lax.dot_general(
+        x_ref[:, j * HD : (j + 1) * HD],
+        kv_ref[:n, :HD],
+        QK,
+        preferred_element_type=jnp.float32,
+    )
+
+
+def per_head(n, x_ref, kv_ref, finish):
+    scores = scores_of(0, n, x_ref, kv_ref)
+    for j in range(GROUP):
+        ahead = scores_of(j + 1, n, x_ref, kv_ref) if j + 1 < GROUP else None
+        finish(slice(j * HD, (j + 1) * HD), scores)
+        scores = ahead
+
+
 def own_kernel(place, x_ref, kv_ref, acc_ref, max_ref, sum_ref):
-    def head(j, carry):
-        cols = columns(j)
-        scores = lax.dot_general(
-            x_ref[:, cols], kv_ref[:, :HD], QK, preferred_element_type=jnp.float32
-        )
-        row = lax.broadcasted_iota(jnp.int32, scores.shape, 0)
-        col = lax.broadcasted_iota(jnp.int32, scores.shape, 1)
-        scores = jnp.where(col <= row + place[0] * ROWS, scores, NEG)
+    shape = (ROWS, 2 * ROWS)
+    row = lax.broadcasted_iota(jnp.int32, shape, 0)
+    col = lax.broadcasted_iota(jnp.int32, shape, 1)
+    seen = col <= row + place[0] * ROWS
+
+    def finish(cols, scores):
+        scores = jnp.where(seen, scores, NEG)
         peak = jnp.max(scores, axis=1, keepdims=True) * SCALE
         weights = jnp.exp2(scores * SCALE - peak)
         sum_ref[:, cols] = lane_sums(weights)
@@ -66,17 +77,12 @@
             preferred_element_type=jnp.float32,
         )
         max_ref[:, cols] = jnp.broadcast_to(peak, (ROWS, HD))
-        return carry
-
-    lax.fori_loop(0, GROUP, head, 0, unroll=UNROLL)
+
+    per_head(2 * ROWS, x_ref, kv_ref, finish)
 
 
 def absorb(n, x_ref, kv_ref, acc_in, max_in, sum_in, acc_ref, max_ref, sum_ref):
-    def head(j, carry):
-        cols = columns(j)
-        scores = lax.dot_general(
-            x_ref[:, cols], kv_ref[:n, :HD], QK, preferred_element_type=jnp.float32
-        )
+    def finish(cols, scores):
         old = max_in[:, cols]
         peak = jnp.maximum(old, jnp.max(scores, axis=1, keepdims=True) * SCALE)
         keep = jnp.exp2(old - peak)
@@ -88,25 +94,19 @@
             preferred_element_type=jnp.float32,
         )
         max_ref[:, cols] = peak
-        return carry
-
-    lax.fori_loop(0, GROUP, head, 0, unroll=UNROLL)
+
+    per_head(n, x_ref, kv_ref, finish)
 
 
 def absorb_if_needed(shift, place, x_ref, kv_ref, ins, outs):
     z, y = place[0], place[1]
-    source = lax.rem(y - shift + NY, NY)
-    before = source < y
-
-    @pl.when(jnp.logical_and(z == 1, before))
+    before = (lax.rem(y - shift + NY, NY) < y).astype(jnp.int32)
+
+    @pl.when(z + before == 2)
     def _():
         absorb(2 * ROWS, x_ref, kv_ref, *ins, *outs)
 
-    @pl.when(jnp.logical_and(z == 1, jnp.logical_not(before)))
-    def _():
-        absorb(ROWS, x_ref, kv_ref, *ins, *outs)
-
-    @pl.when(jnp.logical_and(z == 0, before))
+    @pl.when(z + before == 1)
     def _():
         absorb(ROWS, x_ref, kv_ref, *ins, *outs)
 
@@ -123,14 +123,10 @@
     absorb_if_needed(
         shift, place, x_ref, kv_ref, (a_in, m_in, s_in), (a_out, m_out, s_out)
     )
-
-    def head(j, carry):
-        cols = columns(j)
+    for j in range(GROUP):
+        cols = slice(j * HD, (j + 1) * HD)
         total = jnp.sum(s_out[:, cols], axis=1, keepdims=True)
         o_ref[:, cols] = (a_out[:, cols] / total).astype(jnp.bfloat16)
-        return carry
-
-    lax.fori_loop(0, GROUP, head, 0, unroll=UNROLL)
 
 
 VMEM = pl.BlockSpec(memory_space=pltpu.VMEM)
@@ -200,16 +196,18 @@
         x[:, GROUP * HD :], "ctx", axis=0, tiled=True, axis_index_groups=Z_GROUPS
     )
     x = x[:, : GROUP * HD]
-    up = down = kv
-    arrived = []
+    up = lax.ppermute(kv, "ctx", ring(1))
+    down = lax.ppermute(kv, "ctx", ring(-1))
+    state = own_block(place, x, kv)
     for step in range(1, NY // 2):
-        up = lax.ppermute(up, "ctx", ring(1))
-        down = lax.ppermute(down, "ctx", ring(-1))
-        arrived += [(step, up), (-step, down)]
-    up = lax.ppermute(up, "ctx", ring(1))
-    state = own_block(place, x, kv)
-    for shift, block in arrived:
-        state = more_block(shift, place, x, block, state)
+        up, state = lax.optimization_barrier((up, state))
+        next_up = lax.ppermute(up, "ctx", ring(1))
+        state = more_block(step, place, x, up, state)
+        if step + 1 < NY // 2:
+            down, state = lax.optimization_barrier((down, state))
+            next_down = lax.ppermute(down, "ctx", ring(-1))
+        state = more_block(-step, place, x, down, state)
+        up, down = next_up, next_down
     out = last_block(NY // 2, place, x, up, state)
     out = lax.all_to_all(
         out.reshape(NX, rows, GROUP * HD),

time: 97.3 us -> 86.3 us (0.89)
  the two profiles are of different devices: /device:TPU:440 before, /device:TPU:384 now
where the time goes in v2:
time: 86.3 us; the launch traced here: 85.9 us
  blocking collectives  36.6 us (42%)
  starting transfers between devices  24.2 us (28%)
  Pallas kernels  18.2 us (21%)
  waiting for transfers between devices  4.57 us (5%)
  local copies, waits for them, and re-layouts  2.04 us (2%)
    all_to_all x1, blocking collectives, local(): lax.all_to_all(by_head, 'ctx', 0, 0, axis_index_groups=X_GROUPS, tiled=True)  15 us
    pallas_call x6, Pallas kernels, more_block(): pl.pallas_call(functools.partial(more_kernel, shift), out_shape=STATE, in...  13.2 us
    ppermute x2, starting transfers between devices, local(): next_down = lax.ppermute(down, 'ctx', ring(-1))  11.2 us
    all_gather x1, blocking collectives, local(): lax.all_gather(x[:, GROUP * HD:], 'ctx', axis=0, tiled=True, axis_index_g...  11.1 us
    all_to_all x1, blocking collectives, local(): lax.all_to_all(out.reshape(NX, rows, GROUP * HD), 'ctx', 0, 0, axis_index...  10.5 us
    ppermute x3, starting transfers between devices, local(): next_up = lax.ppermute(up, 'ctx', ring(1))  5.75 us
    ppermute x1, starting transfers between devices, local(): down = lax.ppermute(kv, 'ctx', ring(-1))  3.81 us
    ppermute x1, starting transfers between devices, local(): up = lax.ppermute(kv, 'ctx', ring(1))  3.47 us
  transfers between devices with their start and end apart: 7, of which 2 were waited for; matrix products, arithmetic and copies ran while one was open for 0% of the time, Pallas kernels for 18%

profile of v2, /device:TPU:384, one launch (start us, length us, event | category | flops | bytes accessed | tf_op | source)
XLA Modules:
  0.0 85.9 jit_solution(16930224649688138599)
XLA Ops:
  0.0 0.0 copy-start
  0.0 0.0 copy-start.1
  0.0 1.1 %copy.36 = bf16[8,4,8,1024]{3,2,0,1:T(8,128)(2,1)S(1)} copy(bf16[8,4,8,1024]{3,2,1,0:T(8,128)(2,1)} %bitcast.28) | data formatting | bytes 1048576 | tf_op jit(solution)/shard_map/reshape | solution.py:187
  1.1 0.0 copy-done
  1.1 0.0 copy-done.1
  1.2 0.1 maximum_bitcast_fusion
  1.2 15.0 %all_to_all.10 = bf16[4,64,1280]{2,1,0:T(8,128)(2,1)S(1)} all-to-all(bf16[4,64,1280]{2,1,0:T(8,128)(2,1)S(1)} %maximum_bitcast_fusion), channel_id=1, replica_groups={{0,1,2,3},{4,5,6,7},{8,9,10,11},{12,13,14,15},{16,17,18,19},{20,21,22,2..., dimensions={0} | all-to-all | bytes 1310720 | tf_op jit(solution)/shard_map/all_to_all | solution.py:193
  16.2 11.1 %all_gather.3.kv_ref = bf16[512,256]{1,0:T(8,128)(2,1)S(1)} all-gather(bf16[256,256]{1,0:T(8,128)(2,1)S(1)} %slice.9), channel_id=1, replica_groups={{0,32},{1,33},{2,34},{3,35},{4,36},{5,37},{6,38},{7,39},{8,40},{9,41},{..., dimensions={0}, use_global_device_ids=true | all-gather | bytes 393216 | tf_op jit(solution)/shard_map/all_gather | solution.py:195
  27.3 3.5 %collective-permute-start = (bf16[512,256]{1,0:T(8,128)(2,1)S(1)}, bf16[512,256]{1,0:T(8,128)(2,1)S(1)}, u32[]{:S(2)}, u32[]{:S(2)}) collective-permute-start(bf16[512,256]{1,0:T(8,128)(2,1)S(1)} %all_gather.3.kv_ref), channel_id=1, source_target_pairs={{0,4},{1,5},{2,6},{3,7},{4,8},{5,9},{6,10},{7,11},{8,12},{9,13},{1... | collective-permute-start | bytes 786440 | tf_op jit(solution)/shard_map/ppermute | solution.py:199
  30.8 3.8 %collective-permute-start.2 = (bf16[512,256]{1,0:T(8,128)(2,1)S(1)}, bf16[512,256]{1,0:T(8,128)(2,1)S(1)}, u32[]{:S(2)}, u32[]{:S(2)}) collective-permute-start(bf16[512,256]{1,0:T(8,128)(2,1)S(1)} %all_gather.3.kv_ref), channel_id=1, source_target_pairs={{0,28},{1,29},{2,30},{3,31},{4,0},{5,1},{6,2},{7,3},{8,4},{9,5},{1... | collective-permute-start | bytes 786440 | tf_op jit(solution)/shard_map/ppermute | solution.py:200
  34.7 0.1 pad_add_fusion.place
  34.7 0.1 slice.8.x_ref
  34.8 2.2 %own_block.1 = (f32[256,1024]{1,0:T(8,128)S(1)}, f32[256,1024]{1,0:T(8,128)S(1)}, f32[256,1024]{1,0:T(8,128)S(1)}) custom-call(s32[2]{0:T(128)S(1)} %pad_add_fusion.place, bf16[256,1024]{1,0:T(8,128)(2,1)S(1)} %slice.8.x_ref, bf16[512,256]{1,0:T(8,128)(2,1)S(1)} %all_gather.3.kv_ref), custom_call_target="tpu_custom_call" | custom-call | flops 536870912 | bytes 8388608 | tf_op jit(solution)/shard_map/own_block/pallas_call | solution.py:144
  37.0 1.4 %collective-permute-done.kv_ref = bf16[512,256]{1,0:T(8,128)(2,1)S(1)} collective-permute-done((bf16[512,256]{1,0:T(8,128)(2,1)S(1)}, bf16[512,256]{1,0:T(8,128)(2,1)S(1)}, u32[]{:S(2)}, u32[]{:S(2)}) %collective-permute-start) | collective-permute-done | bytes 262176 | tf_op jit(solution)/shard_map/ppermute | solution.py:199
  38.4 1.9 %collective-permute-start.1 = (bf16[512,256]{1,0:T(8,128)(2,1)S(1)}, bf16[512,256]{1,0:T(8,128)(2,1)S(1)}, u32[]{:S(2)}, u32[]{:S(2)}) collective-permute-start(bf16[512,256]{1,0:T(8,128)(2,1)S(1)} %collective-permute-done.kv_ref), channel_id=1, source_target_pairs={{0,4},{1,5},{2,6},{3,7},{4,8},{5,9},{6,10},{7,11},{8,12},{9,13},{1... | collective-permute-start | bytes 786440 | tf_op jit(solution)/shard_map/ppermute | solution.py:204
  40.3 2.2 %more_block.6 = (f32[256,1024]{1,0:T(8,128)S(1)}, f32[256,1024]{1,0:T(8,128)S(1)}, f32[256,1024]{1,0:T(8,128)S(1)}) custom-call(s32[2]{0:T(128)S(1)} %pad_add_fusion.place, bf16[256,1024]{1,0:T(8,128)(2,1)S(1)} %slice.8.x_ref, bf16[512,256]{1,0:T(8,128)(2,1)S(1)} %collective-permute-done.kv_ref, ...), custom_call_target="tpu_custom_call", output_to_operand_aliasing={{0}: (3, {}), {1}: (4, {}), {2}: (5, {})} | custom-call | flops 536870912 | bytes 8388608 | tf_op jit(solution)/shard_map/more_block/pallas_call | solution.py:156
  42.5 0.0 collective-permute-done.2.kv_ref
  42.5 5.6 %collective-permute-start.4 = (bf16[512,256]{1,0:T(8,128)(2,1)S(1)}, bf16[512,256]{1,0:T(8,128)(2,1)S(1)}, u32[]{:S(2)}, u32[]{:S(2)}) collective-permute-start(bf16[512,256]{1,0:T(8,128)(2,1)S(1)} %collective-permute-done.2.kv_ref), channel_id=1, source_target_pairs={{0,28},{1,29},{2,30},{3,31},{4,0},{5,1},{6,2},{7,3},{8,4},{9,5},{1... | collective-permute-start | bytes 786440 | tf_op jit(solution)/shard_map/ppermute | solution.py:208
  48.1 2.2 %more_block.7 = (f32[256,1024]{1,0:T(8,128)S(1)}, f32[256,1024]{1,0:T(8,128)S(1)}, f32[256,1024]{1,0:T(8,128)S(1)}) custom-call(s32[2]{0:T(128)S(1)} %pad_add_fusion.place, bf16[256,1024]{1,0:T(8,128)(2,1)S(1)} %slice.8.x_ref, bf16[512,256]{1,0:T(8,128)(2,1)S(1)} %collective-permute-done.2.kv_ref, ...), custom_call_target="tpu_custom_call", output_to_operand_aliasing={{0}: (3, {}), {1}: (4, {}), {2}: (5, {})} | custom-call | flops 536870912 | bytes 8388608 | tf_op jit(solution)/shard_map/more_block/pallas_call | solution.py:156
  50.3 0.0 collective-permute-done.1.kv_ref
  50.3 1.9 %collective-permute-start.3 = (bf16[512,256]{1,0:T(8,128)(2,1)S(1)}, bf16[512,256]{1,0:T(8,128)(2,1)S(1)}, u32[]{:S(2)}, u32[]{:S(2)}) collective-permute-start(bf16[512,256]{1,0:T(8,128)(2,1)S(1)} %collective-permute-done.1.kv_ref), channel_id=1, source_target_pairs={{0,4},{1,5},{2,6},{3,7},{4,8},{5,9},{6,10},{7,11},{8,12},{9,13},{1... | collective-permute-start | bytes 786440 | tf_op jit(solution)/shard_map/ppermute | solution.py:204
  52.2 2.3 %more_block.8 = (f32[256,1024]{1,0:T(8,128)S(1)}, f32[256,1024]{1,0:T(8,128)S(1)}, f32[256,1024]{1,0:T(8,128)S(1)}) custom-call(s32[2]{0:T(128)S(1)} %pad_add_fusion.place, bf16[256,1024]{1,0:T(8,128)(2,1)S(1)} %slice.8.x_ref, bf16[512,256]{1,0:T(8,128)(2,1)S(1)} %collective-permute-done.1.kv_ref, ...), custom_call_target="tpu_custom_call", output_to_operand_aliasing={{0}: (3, {}), {1}: (4, {}), {2}: (5, {})} | custom-call | flops 536870912 | bytes 8388608 | tf_op jit(solution)/shard_map/more_block/pallas_call | solution.py:156
  54.5 0.0 collective-permute-done.4.kv_ref
  54.6 5.6 %collective-permute-start.6 = (bf16[512,256]{1,0:T(8,128)(2,1)S(1)}, bf16[512,256]{1,0:T(8,128)(2,1)S(1)}, u32[]{:S(2)}, u32[]{:S(2)}) collective-permute-start(bf16[512,256]{1,0:T(8,128)(2,1)S(1)} %collective-permute-done.4.kv_ref), channel_id=1, source_target_pairs={{0,28},{1,29},{2,30},{3,31},{4,0},{5,1},{6,2},{7,3},{8,4},{9,5},{1... | collective-permute-start | bytes 786440 | tf_op jit(solution)/shard_map/ppermute | solution.py:208
  60.2 2.2 %more_block.9 = (f32[256,1024]{1,0:T(8,128)S(1)}, f32[256,1024]{1,0:T(8,128)S(1)}, f32[256,1024]{1,0:T(8,128)S(1)}) custom-call(s32[2]{0:T(128)S(1)} %pad_add_fusion.place, bf16[256,1024]{1,0:T(8,128)(2,1)S(1)} %slice.8.x_ref, bf16[512,256]{1,0:T(8,128)(2,1)S(1)} %collective-permute-done.4.kv_ref, ...), custom_call_target="tpu_custom_call", output_to_operand_aliasing={{0}: (3, {}), {1}: (4, {}), {2}: (5, {})} | custom-call | flops 536870912 | bytes 8388608 | tf_op jit(solution)/shard_map/more_block/pallas_call | solution.py:156
  62.3 0.0 collective-permute-done.3.kv_ref
  62.3 1.9 %collective-permute-start.5 = (bf16[512,256]{1,0:T(8,128)(2,1)S(1)}, bf16[512,256]{1,0:T(8,128)(2,1)S(1)}, u32[]{:S(2)}, u32[]{:S(2)}) collective-permute-start(bf16[512,256]{1,0:T(8,128)(2,1)S(1)} %collective-permute-done.3.kv_ref), channel_id=1, source_target_pairs={{0,4},{1,5},{2,6},{3,7},{4,8},{5,9},{6,10},{7,11},{8,12},{9,13},{1... | collective-permute-start | bytes 786440 | tf_op jit(solution)/shard_map/ppermute | solution.py:204
  64.3 2.2 %more_block.10 = (f32[256,1024]{1,0:T(8,128)S(1)}, f32[256,1024]{1,0:T(8,128)S(1)}, f32[256,1024]{1,0:T(8,128)S(1)}) custom-call(s32[2]{0:T(128)S(1)} %pad_add_fusion.place, bf16[256,1024]{1,0:T(8,128)(2,1)S(1)} %slice.8.x_ref, bf16[512,256]{1,0:T(8,128)(2,1)S(1)} %collective-permute-done.3.kv_ref, ...), custom_call_target="tpu_custom_call", output_to_operand_aliasing={{0}: (3, {}), {1}: (4, {}), {2}: (5, {})} | custom-call | flops 536870912 | bytes 8388608 | tf_op jit(solution)/shard_map/more_block/pallas_call | solution.py:156
  66.4 0.0 collective-permute-done.6.kv_ref
  66.5 2.2 %more_block.11 = (f32[256,1024]{1,0:T(8,128)S(1)}, f32[256,1024]{1,0:T(8,128)S(1)}, f32[256,1024]{1,0:T(8,128)S(1)}) custom-call(s32[2]{0:T(128)S(1)} %pad_add_fusion.place, bf16[256,1024]{1,0:T(8,128)(2,1)S(1)} %slice.8.x_ref, bf16[512,256]{1,0:T(8,128)(2,1)S(1)} %collective-permute-done.6.kv_ref, ...), custom_call_target="tpu_custom_call", output_to_operand_aliasing={{0}: (3, {}), {1}: (4, {}), {2}: (5, {})} | custom-call | flops 536870912 | bytes 8388608 | tf_op jit(solution)/shard_map/more_block/pallas_call | solution.py:156
  68.6 3.2 %collective-permute-done.5.kv_ref = bf16[512,256]{1,0:T(8,128)(2,1)S(1)} collective-permute-done((bf16[512,256]{1,0:T(8,128)(2,1)S(1)}, bf16[512,256]{1,0:T(8,128)(2,1)S(1)}, u32[]{:S(2)}, u32[]{:S(2)}) %collective-permute-start.5) | collective-permute-done | bytes 262176 | tf_op jit(solution)/shard_map/ppermute | solution.py:204
  71.8 2.7 %last_block.1 = (bf16[256,1024]{1,0:T(8,128)(2,1)S(1)}, f32[256,1024]{1,0:T(8,128)S(1)}, f32[256,1024]{1,0:T(8,128)S(1)}, f32[256,1024]{1,0:T(8,128)S(1)}) custom-call(s32[2]{0:T(128)S(1)} %pad_add_fusion.place, bf16[256,1024]{1,0:T(8,128)(2,1)S(1)} %slice.8.x_ref, ...), custom_call_target="tpu_custom_call", output_to_operand_aliasing={{1}: (3, {}), {2}: (4, {}), {3}: (5, {})} | custom-call | flops 536870912 | bytes 8388608 | tf_op jit(solution)/shard_map/last_block/pallas_call | solution.py:169
  74.6 10.5 %all_to_all.11 = bf16[4,64,1024]{2,1,0:T(8,128)(2,1)S(1)} all-to-all(bf16[4,64,1024]{2,1,0:T(8,128)(2,1)S(1)} %bitcast.23), channel_id=1, replica_groups={{0,1,2,3},{4,5,6,7},{8,9,10,11},{12,13,14,15},{16,17,18,19},{20,21,22,2..., dimensions={0} | all-to-all | bytes 1048576 | tf_op jit(solution)/shard_map/all_to_all | solution.py:212
  85.0 0.8 copy.32
  (2 shorter events, 0.0 us)
Async XLA Ops:
  0.0 1.1 %copy-start = (bf16[64,512]{1,0:T(8,128)(2,1)S(1)}, bf16[64,512]{1,0:T(8,128)(2,1)}, u32[]{:S(2)}) copy-start(bf16[64,512]{1,0:T(8,128)(2,1)} %param.4) | copy-start | bytes 196612
  0.0 1.1 %copy-start.1 = (bf16[64,512]{1,0:T(8,128)(2,1)S(1)}, bf16[64,512]{1,0:T(8,128)(2,1)}, u32[]{:S(2)}) copy-start(bf16[64,512]{1,0:T(8,128)(2,1)} %param.5) | copy-start | bytes 196612
  27.3 11.1 %collective-permute-start = (bf16[512,256]{1,0:T(8,128)(2,1)S(1)}, bf16[512,256]{1,0:T(8,128)(2,1)S(1)}, u32[]{:S(2)}, u32[]{:S(2)}) collective-permute-start(bf16[512,256]{1,0:T(8,128)(2,1)S(1)} %all_gather.3.kv_ref), channel_id=1, source_target_pairs={{0,4},{1,5},{2,6},{3,7},{4,8},{5,9},{6,10},{7,11},{8,12},{9,13},{1... | collective-permute-start | bytes 786440 | tf_op jit(solution)/shard_map/ppermute | solution.py:199
  30.8 11.6 %collective-permute-start.2 = (bf16[512,256]{1,0:T(8,128)(2,1)S(1)}, bf16[512,256]{1,0:T(8,128)(2,1)S(1)}, u32[]{:S(2)}, u32[]{:S(2)}) collective-permute-start(bf16[512,256]{1,0:T(8,128)(2,1)S(1)} %all_gather.3.kv_ref), channel_id=1, source_target_pairs={{0,28},{1,29},{2,30},{3,31},{4,0},{5,1},{6,2},{7,3},{8,4},{9,5},{1... | collective-permute-start | bytes 786440 | tf_op jit(solution)/shard_map/ppermute | solution.py:200
  38.4 11.9 %collective-permute-start.1 = (bf16[512,256]{1,0:T(8,128)(2,1)S(1)}, bf16[512,256]{1,0:T(8,128)(2,1)S(1)}, u32[]{:S(2)}, u32[]{:S(2)}) collective-permute-start(bf16[512,256]{1,0:T(8,128)(2,1)S(1)} %collective-permute-done.kv_ref), channel_id=1, source_target_pairs={{0,4},{1,5},{2,6},{3,7},{4,8},{5,9},{6,10},{7,11},{8,12},{9,13},{1... | collective-permute-start | bytes 786440 | tf_op jit(solution)/shard_map/ppermute | solution.py:204
  42.5 12.1 %collective-permute-start.4 = (bf16[512,256]{1,0:T(8,128)(2,1)S(1)}, bf16[512,256]{1,0:T(8,128)(2,1)S(1)}, u32[]{:S(2)}, u32[]{:S(2)}) collective-permute-start(bf16[512,256]{1,0:T(8,128)(2,1)S(1)} %collective-permute-done.2.kv_ref), channel_id=1, source_target_pairs={{0,28},{1,29},{2,30},{3,31},{4,0},{5,1},{6,2},{7,3},{8,4},{9,5},{1... | collective-permute-start | bytes 786440 | tf_op jit(solution)/shard_map/ppermute | solution.py:208
  50.3 12.1 %collective-permute-start.3 = (bf16[512,256]{1,0:T(8,128)(2,1)S(1)}, bf16[512,256]{1,0:T(8,128)(2,1)S(1)}, u32[]{:S(2)}, u32[]{:S(2)}) collective-permute-start(bf16[512,256]{1,0:T(8,128)(2,1)S(1)} %collective-permute-done.1.kv_ref), channel_id=1, source_target_pairs={{0,4},{1,5},{2,6},{3,7},{4,8},{5,9},{6,10},{7,11},{8,12},{9,13},{1... | collective-permute-start | bytes 786440 | tf_op jit(solution)/shard_map/ppermute | solution.py:204
  54.6 11.9 %collective-permute-start.6 = (bf16[512,256]{1,0:T(8,128)(2,1)S(1)}, bf16[512,256]{1,0:T(8,128)(2,1)S(1)}, u32[]{:S(2)}, u32[]{:S(2)}) collective-permute-start(bf16[512,256]{1,0:T(8,128)(2,1)S(1)} %collective-permute-done.4.kv_ref), channel_id=1, source_target_pairs={{0,28},{1,29},{2,30},{3,31},{4,0},{5,1},{6,2},{7,3},{8,4},{9,5},{1... | collective-permute-start | bytes 786440 | tf_op jit(solution)/shard_map/ppermute | solution.py:208
  62.3 9.5 %collective-permute-start.5 = (bf16[512,256]{1,0:T(8,128)(2,1)S(1)}, bf16[512,256]{1,0:T(8,128)(2,1)S(1)}, u32[]{:S(2)}, u32[]{:S(2)}) collective-permute-start(bf16[512,256]{1,0:T(8,128)(2,1)S(1)} %collective-permute-done.3.kv_ref), channel_id=1, source_target_pairs={{0,4},{1,5},{2,6},{3,7},{4,8},{5,9},{6,10},{7,11},{8,12},{9,13},{1... | collective-permute-start | bytes 786440 | tf_op jit(solution)/shard_map/ppermute | solution.py:204

commit v3 on v2

v3 whole, which is shorter than its diff:
```python
import functools
import math

import jax
import jax.numpy as jnp
from jax import lax
from jax.experimental import pallas as pl
from jax.experimental.pallas import tpu as pltpu
from jax.sharding import PartitionSpec as P

QH = 32
KVH = 4
HD = 128
GROUP = QH // KVH
NZ, NY, NX = 2, 8, 4
ROWS = 256
SCALE = math.log2(math.e) / math.sqrt(HD)
NEG = -1e30
HIDE = 1e30
QK = (((1,), (1,)), ((), ()))


def index(z, y, x):
    return z * (NY * NX) + y * NX + x


X_GROUPS = [[index(z, y, x) for x in range(NX)] for z in range(NZ) for y in range(NY)]
Z_UP = [(index(0, y, x), index(1, y, x)) for y in range(NY) for x in range(NX)]


def ring(step):
    return [
        (index(z, y, x), index(z, (y + step) % NY, x))
        for z in range(NZ)
        for y in range(NY)
        for x in range(NX)
    ]


def lane_sums(weights):
    total = weights[:, :HD]
    for at in range(HD, weights.shape[1], HD):
        total = total + weights[:, at : at + HD]
    return total


def joined(blocks, column):
    return jnp.concatenate(
        [
            block[:, at + column : at + column + HD]
            for block in blocks
            for at in (0, 2 * HD)
        ],
        axis=0,
    )


def per_head(x_ref, blocks, finish):
    def scores_of(j):
        return lax.dot_general(
            x_ref[:, j * HD : (j + 1) * HD],
            joined(blocks, 0),
            QK,
            preferred_element_type=jnp.float32,
        )

    scores = scores_of(0)
    for j in range(GROUP):
        ahead = scores_of(j + 1) if j + 1 < GROUP else None
        finish(slice(j * HD, (j + 1) * HD), scores)
        scores = ahead


def mixed(weights, blocks):
    return jnp.dot(
        weights.astype(jnp.bfloat16),
        joined(blocks, HD),
        preferred_element_type=jnp.float32,
    )


def own_kernel(place, x_ref, kv_ref, acc_ref, max_ref, sum_ref):
    shape = (ROWS, 2 * ROWS)
    row = lax.broadcasted_iota(jnp.int32, shape, 0)
    col = lax.broadcasted_iota(jnp.int32, shape, 1)
    seen = col <= row + place[0] * ROWS

    def finish(cols, scores):
        scores = jnp.where(seen, scores, NEG)
        peak = jnp.max(scores, axis=1, keepdims=True) * SCALE
        weights = jnp.exp2(scores * SCALE - peak)
        sum_ref[:, cols] = lane_sums(weights)
        acc_ref[:, cols] = mixed(weights, [kv_ref])
        max_ref[:, cols] = jnp.broadcast_to(peak, (ROWS, HD))

    per_head(x_ref, [kv_ref], finish)


def absorb(shifts, place, x_ref, blocks, ins, outs, done=None):
    z, y = place[0], place[1]
    hidden = []
    for shift in shifts:
        before = (lax.rem(y - shift + NY, NY) < y).astype(jnp.int32)
        hidden.append(jnp.where(z + before >= 1, 0.0, HIDE))
        hidden.append(jnp.where(z + before == 2, 0.0, HIDE))
    acc_in, max_in, sum_in = ins
    acc_ref, max_ref, sum_ref = outs

    def finish(cols, scores):
        old = max_in[:, cols]
        top = None
        for c, gap in enumerate(hidden):
            left = scores[:, c * ROWS : c * ROWS + HD]
            right = scores[:, c * ROWS + HD : (c + 1) * ROWS]
            here = jnp.maximum(left, right) * SCALE - gap
            top = here if top is None else jnp.maximum(top, here)
        peak = jnp.maximum(old, jnp.max(top, axis=1, keepdims=True))
        keep = jnp.exp2(old - peak)
        base = jnp.concatenate([peak + gap for gap in hidden for _ in (0, 1)], axis=1)
        weights = jnp.exp2(scores * SCALE - base)
        total = sum_in[:, cols] * keep + lane_sums(weights)
        acc = acc_in[:, cols] * keep + mixed(weights, blocks)
        if done is None:
            sum_ref[:, cols] = total
            acc_ref[:, cols] = acc
            max_ref[:, cols] = peak
        else:
            total = jnp.sum(total, axis=1, keepdims=True)
            done[:, cols] = (acc / total).astype(jnp.bfloat16)

    per_head(x_ref, blocks, finish)


def pair_kernel(step, place, x_ref, up_ref, down_ref, a, m, s, a_out, m_out, s_out):
    absorb(
        (step, -step), place, x_ref, [up_ref, down_ref], (a, m, s), (a_out, m_out, s_out)
    )


def last_kernel(step, place, x_ref, up_ref, a, m, s, o_ref):
    absorb((step,), place, x_ref, [up_ref], (a, m, s), (None,) * 3, o_ref)


VMEM = pl.BlockSpec(memory_space=pltpu.VMEM)
SMEM = pl.BlockSpec(memory_space=pltpu.SMEM)
STATE = [jax.ShapeDtypeStruct((ROWS, GROUP * HD), jnp.float32)] * 3
PARAMS = pltpu.CompilerParams(vmem_limit_bytes=32 << 20)


def cost(blocks):
    pairs = ROWS * GROUP * 2 * ROWS * blocks
    return pl.CostEstimate(
        flops=4 * pairs * HD, bytes_accessed=8 << 20, transcendentals=pairs
    )


def own_block(place, x, kv):
    return pl.pallas_call(
        own_kernel,
        out_shape=STATE,
        in_specs=[SMEM, VMEM, VMEM],
        out_specs=[VMEM] * 3,
        compiler_params=PARAMS,
        cost_estimate=cost(1),
        name="own_block",
    )(place, x, kv)


def pair_block(step, place, x, up, down, state):
    return pl.pallas_call(
        functools.partial(pair_kernel, step),
        out_shape=STATE,
        in_specs=[SMEM] + [VMEM] * 6,
        out_specs=[VMEM] * 3,
        input_output_aliases={4: 0, 5: 1, 6: 2},
        compiler_params=PARAMS,
        cost_estimate=cost(2),
        name="pair_block",
    )(place, x, up, down, *state)


def last_block(step, place, x, up, state):
    return pl.pallas_call(
        functools.partial(last_kernel, step),
        out_shape=jax.ShapeDtypeStruct((ROWS, GROUP * HD), jnp.bfloat16),
        in_specs=[SMEM] + [VMEM] * 5,
        out_specs=VMEM,
        compiler_params=PARAMS,
        cost_estimate=cost(1),
        name="last_block",
    )(place, x, up, *state)


def local(queries, keys, values):
    rows = queries.shape[0]
    me = lax.axis_index("ctx")
    z, y = me // (NY * NX), (me // NX) % NY
    place = jnp.stack([z, y]).astype(jnp.int32)
    own = jnp.concatenate(
        [keys.reshape(rows, KVH, HD), values.reshape(rows, KVH, HD)], axis=2
    )
    first = lax.ppermute(own, "ctx", Z_UP)
    first = jnp.where(z == 0, own, first)
    by_head = jnp.concatenate(
        [queries.reshape(rows, KVH, GROUP * HD), first, own], axis=2
    ).transpose(1, 0, 2)
    x = lax.all_to_all(by_head, "ctx", 0, 0, axis_index_groups=X_GROUPS, tiled=True)
    x = x.reshape(ROWS, (GROUP + 4) * HD)
    kv = x[:, GROUP * HD :]
    x = x[:, : GROUP * HD]
    up = lax.ppermute(kv, "ctx", ring(1))
    down = lax.ppermute(kv, "ctx", ring(-1))
    state = own_block(place, x, kv)
    for step in range(1, NY // 2):
        up, state = lax.optimization_barrier((up, state))
        next_up = lax.ppermute(up, "ctx", ring(1))
        if step + 1 < NY // 2:
            next_down = lax.ppermute(down, "ctx", ring(-1))
        state = pair_block(step, place, x, up, down, state)
        up, down = next_up, next_down
    out = last_block(NY // 2, place, x, up, state)
    out = lax.all_to_all(
        out.reshape(NX, rows, GROUP * HD),
        "ctx",
        0,
        0,
        axis_index_groups=X_GROUPS,
        tiled=True,
    )
    return out.transpose(1, 0, 2).reshape(rows, QH * HD)


def solution(mesh):
    spec = P(("dp", "ctx"), None)
    return jax.shard_map(
        local, mesh=mesh, in_specs=(spec,) * 3, out_specs=spec, check_vma=False
    )
```

time: 86.3 us -> 90.3 us (1.046)
  the two profiles are of different devices: /device:TPU:384 before, /device:TPU:128 now
where the time goes in v3:
time: 90.3 us; the launch traced here: 89.8 us
  starting transfers between devices  32.6 us (36%)
  blocking collectives  27 us (30%)
  Pallas kernels  17.9 us (20%)
  waiting for transfers between devices  8.11 us (9%)
  local copies, waits for them, and re-layouts  3.72 us (4%)
    all_to_all x1, blocking collectives, local(): lax.all_to_all(by_head, 'ctx', 0, 0, axis_index_groups=X_GROUPS, tiled=True)  16.6 us
    pallas_call x3, Pallas kernels, pair_block(): pl.pallas_call(functools.partial(pair_kernel, step), out_shape=STATE, in_...  13 us
    all_to_all x1, blocking collectives, local(): lax.all_to_all(out.reshape(NX, rows, GROUP * HD), 'ctx', 0, 0, axis_index...  10.5 us
    ppermute x2, starting transfers between devices, local(): next_down = lax.ppermute(down, 'ctx', ring(-1))  10.3 us
    ppermute x1, starting transfers between devices, local(): first = lax.ppermute(own, 'ctx', Z_UP)  9.12 us
    ppermute x3, starting transfers between devices, local(): next_up = lax.ppermute(up, 'ctx', ring(1))  5.93 us
    ppermute x1, waiting for transfers between devices, local(): first = lax.ppermute(own, 'ctx', Z_UP)  4.37 us
    ppermute x1, starting transfers between devices, local(): down = lax.ppermute(kv, 'ctx', ring(-1))  3.81 us
  transfers between devices with their start and end apart: 8, of which 3 were waited for; matrix products, arithmetic and copies ran while one was open for 1% of the time, Pallas kernels for 17%

profile of v3, /device:TPU:128, one launch (start us, length us, event | category | flops | bytes accessed | tf_op | source)
XLA Modules:
  0.0 89.8 jit_solution(2724612225037317972)
XLA Ops:
  0.0 0.0 copy-start
  0.0 0.0 copy-start.1
  0.0 0.8 copy-done
  0.9 0.9 constant_dynamic-update-slice_fusion
  1.7 9.1 %collective-permute-start = (bf16[64,4,256]{2,0,1:T(8,128)(2,1)S(1)}, bf16[64,4,256]{2,0,1:T(8,128)(2,1)S(1)}, u32[]{:S(2)}, u32[]{:S(2)}) collective-permute-start(bf16[64,4,256]{2,0,1:T(8,128)(2,1)S(1)} %constant_dynamic-update-slice_fusion), channel_id=1, source_target_pairs={{0,32},{1,33},{2,34},{3,35},{4,36},{5,37},{6,38},{7,39},{8,40},{9,... | collective-permute-start | bytes 393224 | tf_op jit(solution)/shard_map/ppermute | solution.py:202
  10.9 1.1 %copy.30 = bf16[8,4,8,1024]{3,2,0,1:T(8,128)(2,1)S(1)} copy(bf16[8,4,8,1024]{3,2,1,0:T(8,128)(2,1)} %bitcast.36) | data formatting | bytes 1048576 | tf_op jit(solution)/shard_map/reshape | solution.py:205
  12.0 0.0 copy-done.1
  12.0 4.4 %collective-permute-done = bf16[64,4,256]{2,0,1:T(8,128)(2,1)S(1)} collective-permute-done((bf16[64,4,256]{2,0,1:T(8,128)(2,1)S(1)}, bf16[64,4,256]{2,0,1:T(8,128)(2,1)S(1)}, u32[]{:S(2)}, u32[]{:S(2)}) %collective-permute-start) | collective-permute-done | bytes 131104 | tf_op jit(solution)/shard_map/ppermute | solution.py:202
  16.4 0.1 maximum_bitcast_fusion
  16.5 16.6 %all_to_all.10 = bf16[4,64,1536]{2,1,0:T(8,128)(2,1)S(1)} all-to-all(bf16[4,64,1536]{2,1,0:T(8,128)(2,1)S(1)} %maximum_bitcast_fusion), channel_id=1, replica_groups={{0,1,2,3},{4,5,6,7},{8,9,10,11},{12,13,14,15},{16,17,18,19},{20,21,22,2..., dimensions={0} | all-to-all | bytes 1572864 | tf_op jit(solution)/shard_map/all_to_all | solution.py:207
  33.1 3.5 %collective-permute-start.1 = (bf16[256,512]{1,0:T(8,128)(2,1)S(1)}, bf16[256,512]{1,0:T(8,128)(2,1)S(1)}, u32[]{:S(2)}, u32[]{:S(2)}) collective-permute-start(bf16[256,512]{1,0:T(8,128)(2,1)S(1)} %slice.9.kv_ref), channel_id=1, source_target_pairs={{0,4},{1,5},{2,6},{3,7},{4,8},{5,9},{6,10},{7,11},{8,12},{9,13},{1... | collective-permute-start | bytes 786440 | tf_op jit(solution)/shard_map/ppermute | solution.py:211
  36.6 3.8 %collective-permute-start.3 = (bf16[256,512]{1,0:T(8,128)(2,1)S(1)}, bf16[256,512]{1,0:T(8,128)(2,1)S(1)}, u32[]{:S(2)}, u32[]{:S(2)}) collective-permute-start(bf16[256,512]{1,0:T(8,128)(2,1)S(1)} %slice.9.kv_ref), channel_id=1, source_target_pairs={{0,28},{1,29},{2,30},{3,31},{4,0},{5,1},{6,2},{7,3},{8,4},{9,5},{1... | collective-permute-start | bytes 786440 | tf_op jit(solution)/shard_map/ppermute | solution.py:212
  40.4 0.1 pad_add_fusion.place
  40.5 2.2 %own_block.1 = (f32[256,1024]{1,0:T(8,128)S(1)}, f32[256,1024]{1,0:T(8,128)S(1)}, f32[256,1024]{1,0:T(8,128)S(1)}) custom-call(s32[2]{0:T(128)S(1)} %pad_add_fusion.place, bf16[256,1024]{1,0:T(8,128)(2,1)S(1)} %slice.8.x_ref, bf16[256,512]{1,0:T(8,128)(2,1)S(1)} %slice.9.kv_ref), custom_call_target="tpu_custom_call" | custom-call | flops 536870912 | bytes 8388608 | tf_op jit(solution)/shard_map/own_block/pallas_call | solution.py:158
  42.8 0.7 collective-permute-done.1.up_ref
  43.5 1.9 %collective-permute-start.2 = (bf16[256,512]{1,0:T(8,128)(2,1)S(1)}, bf16[256,512]{1,0:T(8,128)(2,1)S(1)}, u32[]{:S(2)}, u32[]{:S(2)}) collective-permute-start(bf16[256,512]{1,0:T(8,128)(2,1)S(1)} %collective-permute-done.1.up_ref), channel_id=1, source_target_pairs={{0,4},{1,5},{2,6},{3,7},{4,8},{5,9},{6,10},{7,11},{8,12},{9,13},{1... | collective-permute-start | bytes 786440 | tf_op jit(solution)/shard_map/ppermute | solution.py:216
  45.4 0.0 collective-permute-done.3.down_ref
  45.4 5.1 %collective-permute-start.5 = (bf16[256,512]{1,0:T(8,128)(2,1)S(1)}, bf16[256,512]{1,0:T(8,128)(2,1)S(1)}, u32[]{:S(2)}, u32[]{:S(2)}) collective-permute-start(bf16[256,512]{1,0:T(8,128)(2,1)S(1)} %collective-permute-done.3.down_ref), channel_id=1, source_target_pairs={{0,28},{1,29},{2,30},{3,31},{4,0},{5,1},{6,2},{7,3},{8,4},{9,5},{1... | collective-permute-start | bytes 786440 | tf_op jit(solution)/shard_map/ppermute | solution.py:218
  50.5 4.3 %pair_block.3 = (f32[256,1024]{1,0:T(8,128)S(1)}, f32[256,1024]{1,0:T(8,128)S(1)}, f32[256,1024]{1,0:T(8,128)S(1)}) custom-call(s32[2]{0:T(128)S(1)} %pad_add_fusion.place, bf16[256,1024]{1,0:T(8,128)(2,1)S(1)} %slice.8.x_ref, bf16[256,512]{1,0:T(8,128)(2,1)S(1)} %collective-permute-done.1.up_ref, ...), custom_call_target="tpu_custom_call", output_to_operand_aliasing={{0}: (4, {}), {1}: (5, {}), {2}: (6, {})} | custom-call | flops 1073741824 | bytes 8388608 | tf_op jit(solution)/shard_map/pair_block/pallas_call | solution.py:170
  54.8 0.0 collective-permute-done.2.up_ref
  54.9 1.9 %collective-permute-start.4 = (bf16[256,512]{1,0:T(8,128)(2,1)S(1)}, bf16[256,512]{1,0:T(8,128)(2,1)S(1)}, u32[]{:S(2)}, u32[]{:S(2)}) collective-permute-start(bf16[256,512]{1,0:T(8,128)(2,1)S(1)} %collective-permute-done.2.up_ref), channel_id=1, source_target_pairs={{0,4},{1,5},{2,6},{3,7},{4,8},{5,9},{6,10},{7,11},{8,12},{9,13},{1... | collective-permute-start | bytes 786440 | tf_op jit(solution)/shard_map/ppermute | solution.py:216
  56.8 0.0 collective-permute-done.5.down_ref
  56.8 5.1 %collective-permute-start.7 = (bf16[256,512]{1,0:T(8,128)(2,1)S(1)}, bf16[256,512]{1,0:T(8,128)(2,1)S(1)}, u32[]{:S(2)}, u32[]{:S(2)}) collective-permute-start(bf16[256,512]{1,0:T(8,128)(2,1)S(1)} %collective-permute-done.5.down_ref), channel_id=1, source_target_pairs={{0,28},{1,29},{2,30},{3,31},{4,0},{5,1},{6,2},{7,3},{8,4},{9,5},{1... | collective-permute-start | bytes 786440 | tf_op jit(solution)/shard_map/ppermute | solution.py:218
  61.9 4.4 %pair_block.4 = (f32[256,1024]{1,0:T(8,128)S(1)}, f32[256,1024]{1,0:T(8,128)S(1)}, f32[256,1024]{1,0:T(8,128)S(1)}) custom-call(s32[2]{0:T(128)S(1)} %pad_add_fusion.place, bf16[256,1024]{1,0:T(8,128)(2,1)S(1)} %slice.8.x_ref, bf16[256,512]{1,0:T(8,128)(2,1)S(1)} %collective-permute-done.2.up_ref, ...), custom_call_target="tpu_custom_call", output_to_operand_aliasing={{0}: (4, {}), {1}: (5, {}), {2}: (6, {})} | custom-call | flops 1073741824 | bytes 8388608 | tf_op jit(solution)/shard_map/pair_block/pallas_call | solution.py:170
  66.3 0.0 collective-permute-done.4.up_ref
  66.3 2.1 %collective-permute-start.6 = (bf16[256,512]{1,0:T(8,128)(2,1)S(1)}, bf16[256,512]{1,0:T(8,128)(2,1)S(1)}, u32[]{:S(2)}, u32[]{:S(2)}) collective-permute-start(bf16[256,512]{1,0:T(8,128)(2,1)S(1)} %collective-permute-done.4.up_ref), channel_id=1, source_target_pairs={{0,4},{1,5},{2,6},{3,7},{4,8},{5,9},{6,10},{7,11},{8,12},{9,13},{1... | collective-permute-start | bytes 786440 | tf_op jit(solution)/shard_map/ppermute | solution.py:216
  68.4 0.0 collective-permute-done.7.down_ref
  68.4 4.3 %pair_block.5 = (f32[256,1024]{1,0:T(8,128)S(1)}, f32[256,1024]{1,0:T(8,128)S(1)}, f32[256,1024]{1,0:T(8,128)S(1)}) custom-call(s32[2]{0:T(128)S(1)} %pad_add_fusion.place, bf16[256,1024]{1,0:T(8,128)(2,1)S(1)} %slice.8.x_ref, bf16[256,512]{1,0:T(8,128)(2,1)S(1)} %collective-permute-done.4.up_ref, ...), custom_call_target="tpu_custom_call", output_to_operand_aliasing={{0}: (4, {}), {1}: (5, {}), {2}: (6, {})} | custom-call | flops 1073741824 | bytes 8388608 | tf_op jit(solution)/shard_map/pair_block/pallas_call | solution.py:170
  72.8 3.0 %collective-permute-done.6.up_ref = bf16[256,512]{1,0:T(8,128)(2,1)S(1)} collective-permute-done((bf16[256,512]{1,0:T(8,128)(2,1)S(1)}, bf16[256,512]{1,0:T(8,128)(2,1)S(1)}, u32[]{:S(2)}, u32[]{:S(2)}) %collective-permute-start.6) | collective-permute-done | bytes 262176 | tf_op jit(solution)/shard_map/ppermute | solution.py:216
  75.8 2.7 %last_block.1 = bf16[256,1024]{1,0:T(8,128)(2,1)S(1)} custom-call(s32[2]{0:T(128)S(1)} %pad_add_fusion.place, bf16[256,1024]{1,0:T(8,128)(2,1)S(1)} %slice.8.x_ref, bf16[256,512]{1,0:T(8,128)(2,1)S(1)} %collective-permute-done.6.up_ref, f32[256,1024]{1,0:T(8,128)S(1)} %get-tuple-element.50.a, f32[256,1024]{1,0:T(8,128)S(1)} %get-tuple-element.51.m, ...), custom_call_target="tpu_custom_call" | custom-call | flops 536870912 | bytes 8388608 | tf_op jit(solution)/shard_map/last_block/pallas_call | solution.py:183
  78.5 10.5 %all_to_all.11 = bf16[4,64,1024]{2,1,0:T(8,128)(2,1)S(1)} all-to-all(bf16[4,64,1024]{2,1,0:T(8,128)(2,1)S(1)} %bitcast.31), channel_id=1, replica_groups={{0,1,2,3},{4,5,6,7},{8,9,10,11},{12,13,14,15},{16,17,18,19},{20,21,22,2..., dimensions={0} | all-to-all | bytes 1048576 | tf_op jit(solution)/shard_map/all_to_all | solution.py:222
  89.0 0.8 copy.22
  (5 shorter events, 0.1 us)
Async XLA Ops:
  0.0 0.8 copy-start
  0.0 12.0 %copy-start.1 = (bf16[64,512]{1,0:T(8,128)(2,1)S(1)}, bf16[64,512]{1,0:T(8,128)(2,1)}, u32[]{:S(2)}) copy-start(bf16[64,512]{1,0:T(8,128)(2,1)} %param.5) | copy-start | bytes 196612
  1.7 14.6 %collective-permute-start = (bf16[64,4,256]{2,0,1:T(8,128)(2,1)S(1)}, bf16[64,4,256]{2,0,1:T(8,128)(2,1)S(1)}, u32[]{:S(2)}, u32[]{:S(2)}) collective-permute-start(bf16[64,4,256]{2,0,1:T(8,128)(2,1)S(1)} %constant_dynamic-update-slice_fusion), channel_id=1, source_target_pairs={{0,32},{1,33},{2,34},{3,35},{4,36},{5,37},{6,38},{7,39},{8,40},{9,... | collective-permute-start | bytes 393224 | tf_op jit(solution)/shard_map/ppermute | solution.py:202
  33.1 10.4 %collective-permute-start.1 = (bf16[256,512]{1,0:T(8,128)(2,1)S(1)}, bf16[256,512]{1,0:T(8,128)(2,1)S(1)}, u32[]{:S(2)}, u32[]{:S(2)}) collective-permute-start(bf16[256,512]{1,0:T(8,128)(2,1)S(1)} %slice.9.kv_ref), channel_id=1, source_target_pairs={{0,4},{1,5},{2,6},{3,7},{4,8},{5,9},{6,10},{7,11},{8,12},{9,13},{1... | collective-permute-start | bytes 786440 | tf_op jit(solution)/shard_map/ppermute | solution.py:211
  36.6 8.8 %collective-permute-start.3 = (bf16[256,512]{1,0:T(8,128)(2,1)S(1)}, bf16[256,512]{1,0:T(8,128)(2,1)S(1)}, u32[]{:S(2)}, u32[]{:S(2)}) collective-permute-start(bf16[256,512]{1,0:T(8,128)(2,1)S(1)} %slice.9.kv_ref), channel_id=1, source_target_pairs={{0,28},{1,29},{2,30},{3,31},{4,0},{5,1},{6,2},{7,3},{8,4},{9,5},{1... | collective-permute-start | bytes 786440 | tf_op jit(solution)/shard_map/ppermute | solution.py:212
  43.5 11.4 %collective-permute-start.2 = (bf16[256,512]{1,0:T(8,128)(2,1)S(1)}, bf16[256,512]{1,0:T(8,128)(2,1)S(1)}, u32[]{:S(2)}, u32[]{:S(2)}) collective-permute-start(bf16[256,512]{1,0:T(8,128)(2,1)S(1)} %collective-permute-done.1.up_ref), channel_id=1, source_target_pairs={{0,4},{1,5},{2,6},{3,7},{4,8},{5,9},{6,10},{7,11},{8,12},{9,13},{1... | collective-permute-start | bytes 786440 | tf_op jit(solution)/shard_map/ppermute | solution.py:216
  45.4 11.4 %collective-permute-start.5 = (bf16[256,512]{1,0:T(8,128)(2,1)S(1)}, bf16[256,512]{1,0:T(8,128)(2,1)S(1)}, u32[]{:S(2)}, u32[]{:S(2)}) collective-permute-start(bf16[256,512]{1,0:T(8,128)(2,1)S(1)} %collective-permute-done.3.down_ref), channel_id=1, source_target_pairs={{0,28},{1,29},{2,30},{3,31},{4,0},{5,1},{6,2},{7,3},{8,4},{9,5},{1... | collective-permute-start | bytes 786440 | tf_op jit(solution)/shard_map/ppermute | solution.py:218
  54.9 11.4 %collective-permute-start.4 = (bf16[256,512]{1,0:T(8,128)(2,1)S(1)}, bf16[256,512]{1,0:T(8,128)(2,1)S(1)}, u32[]{:S(2)}, u32[]{:S(2)}) collective-permute-start(bf16[256,512]{1,0:T(8,128)(2,1)S(1)} %collective-permute-done.2.up_ref), channel_id=1, source_target_pairs={{0,4},{1,5},{2,6},{3,7},{4,8},{5,9},{6,10},{7,11},{8,12},{9,13},{1... | collective-permute-start | bytes 786440 | tf_op jit(solution)/shard_map/ppermute | solution.py:216
  56.8 11.6 %collective-permute-start.7 = (bf16[256,512]{1,0:T(8,128)(2,1)S(1)}, bf16[256,512]{1,0:T(8,128)(2,1)S(1)}, u32[]{:S(2)}, u32[]{:S(2)}) collective-permute-start(bf16[256,512]{1,0:T(8,128)(2,1)S(1)} %collective-permute-done.5.down_ref), channel_id=1, source_target_pairs={{0,28},{1,29},{2,30},{3,31},{4,0},{5,1},{6,2},{7,3},{8,4},{9,5},{1... | collective-permute-start | bytes 786440 | tf_op jit(solution)/shard_map/ppermute | solution.py:218
  66.3 9.5 %collective-permute-start.6 = (bf16[256,512]{1,0:T(8,128)(2,1)S(1)}, bf16[256,512]{1,0:T(8,128)(2,1)S(1)}, u32[]{:S(2)}, u32[]{:S(2)}) collective-permute-start(bf16[256,512]{1,0:T(8,128)(2,1)S(1)} %collective-permute-done.4.up_ref), channel_id=1, source_target_pairs={{0,4},{1,5},{2,6},{3,7},{4,8},{5,9},{6,10},{7,11},{8,12},{9,13},{1... | collective-permute-start | bytes 786440 | tf_op jit(solution)/shard_map/ppermute | solution.py:216

commit v4 on v3

v4 whole, which is shorter than its diff:
```python
import functools
import math

import jax
import jax.numpy as jnp
from jax import lax
from jax.experimental import pallas as pl
from jax.experimental.pallas import tpu as pltpu
from jax.sharding import PartitionSpec as P

QH = 32
KVH = 4
HD = 128
GROUP = QH // KVH
NZ, NY, NX = 2, 8, 4
ROWS = 256
SCALE = math.log2(math.e) / math.sqrt(HD)
NEG = -1e30
QK = (((1,), (1,)), ((), ()))


def index(z, y, x):
    return z * (NY * NX) + y * NX + x


X_GROUPS = [[index(z, y, x) for x in range(NX)] for z in range(NZ) for y in range(NY)]
Z_GROUPS = [[index(z, y, x) for z in range(NZ)] for y in range(NY) for x in range(NX)]


def ring(step):
    return [
        (index(z, y, x), index(z, (y + step) % NY, x))
        for z in range(NZ)
        for y in range(NY)
        for x in range(NX)
    ]


def per_head(x_ref, keys_of, finish):
    def scores_of(j):
        return lax.dot_general(
            x_ref[:, j * HD : (j + 1) * HD],
            keys_of(),
            QK,
            preferred_element_type=jnp.float32,
        )

    scores = scores_of(0)
    for j in range(GROUP):
        ahead = scores_of(j + 1) if j + 1 < GROUP else None
        finish(slice(j * HD, (j + 1) * HD), scores)
        scores = ahead


def weigh(weights, value_scr):
    both = jnp.dot(
        weights.astype(jnp.bfloat16),
        value_scr[...],
        preferred_element_type=jnp.float32,
    )
    return both[:, :HD], both[:, HD:]


def own_kernel(place, x_ref, kv_ref, acc_ref, max_ref, sum_ref, key_scr, value_scr):
    value_scr[:, HD:] = jnp.ones((2 * ROWS, HD), jnp.bfloat16)
    key_scr[...] = kv_ref[:, :HD]
    value_scr[:, :HD] = kv_ref[:, HD:]
    shape = (ROWS, 2 * ROWS)
    row = lax.broadcasted_iota(jnp.int32, shape, 0)
    col = lax.broadcasted_iota(jnp.int32, shape, 1)
    seen = col <= row + place[0] * ROWS

    def finish(cols, scores):
        scores = jnp.where(seen, scores, NEG)
        peak = jnp.max(scores, axis=1, keepdims=True) * SCALE
        weights = jnp.exp2(scores * SCALE - peak)
        acc_ref[:, cols], sum_ref[:, cols] = weigh(weights, value_scr)
        max_ref[:, cols] = jnp.broadcast_to(peak, (ROWS, HD))

    per_head(x_ref, lambda: key_scr[...], finish)


def more_kernel(shifts, last, *refs):
    n = len(shifts)
    place, x_ref, blocks = refs[0], refs[1], refs[2 : 2 + n]
    acc_in, max_in, sum_in = refs[2 + n : 5 + n]
    outs, (key_scr, value_scr, safe_scr) = refs[5 + n : -3], refs[-3:]
    z, y = place[0], place[1]
    allowed = []
    for shift in shifts:
        before = (lax.rem(y - shift + NY, NY) < y).astype(jnp.int32)
        allowed += [z + before >= 1, z + before == 2]
    any_allowed = functools.reduce(jnp.logical_or, allowed)

    def put(c, key, value, one):
        key_scr[c * ROWS : (c + 1) * ROWS, :] = key
        value_scr[c * ROWS : (c + 1) * ROWS, :HD] = value
        value_scr[c * ROWS : (c + 1) * ROWS, HD:] = one

    @pl.when(any_allowed)
    def _():
        for c in range(2 * n - 2, -1, -2):

            @pl.when(allowed[c])
            def _(c=c):
                safe_scr[...] = blocks[c // 2][:ROWS, :HD]

        one = jnp.ones((ROWS, HD), jnp.bfloat16)
        for c in range(2 * n):
            block, at = blocks[c // 2], c % 2 * ROWS

            @pl.when(allowed[c])
            def _(c=c, block=block, at=at):
                put(c, block[at : at + ROWS, :HD], block[at : at + ROWS, HD:], one)

            @pl.when(jnp.logical_not(allowed[c]))
            def _(c=c):
                put(c, safe_scr[...], jnp.zeros_like(one), jnp.zeros_like(one))

        def finish(cols, scores):
            old = max_in[:, cols]
            peak = jnp.maximum(old, jnp.max(scores, axis=1, keepdims=True) * SCALE)
            keep = jnp.exp2(old - peak)
            weights = jnp.exp2(scores * SCALE - jnp.tile(peak, (1, 4 * n)))
            acc, total = weigh(weights, value_scr)
            acc = acc_in[:, cols] * keep + acc
            total = sum_in[:, cols] * keep + total
            if last:
                outs[0][:, cols] = (acc / total).astype(jnp.bfloat16)
            else:
                outs[0][:, cols], outs[1][:, cols], outs[2][:, cols] = acc, peak, total

        per_head(x_ref, lambda: key_scr[...], finish)

    if last:

        @pl.when(jnp.logical_not(any_allowed))
        def _():
            outs[0][...] = (acc_in[...] / sum_in[...]).astype(jnp.bfloat16)


VMEM = pl.BlockSpec(memory_space=pltpu.VMEM)
SMEM = pl.BlockSpec(memory_space=pltpu.SMEM)
STATE = [jax.ShapeDtypeStruct((ROWS, GROUP * HD), jnp.float32)] * 3
PARAMS = pltpu.CompilerParams(vmem_limit_bytes=32 << 20)


def cost(blocks):
    pairs = ROWS * GROUP * 2 * ROWS * blocks
    return pl.CostEstimate(
        flops=4 * pairs * HD, bytes_accessed=8 << 20, transcendentals=pairs
    )


def scratch(blocks):
    return [
        pltpu.VMEM((2 * ROWS * blocks, HD), jnp.bfloat16),
        pltpu.VMEM((2 * ROWS * blocks, 2 * HD), jnp.bfloat16),
    ]


def own_block(place, x, kv):
    return pl.pallas_call(
        own_kernel,
        out_shape=STATE,
        in_specs=[SMEM, VMEM, VMEM],
        out_specs=[VMEM] * 3,
        scratch_shapes=scratch(1),
        compiler_params=PARAMS,
        cost_estimate=cost(1),
        name="own_block",
    )(place, x, kv)


def more_blocks(arrived, place, x, state):
    shifts = tuple(shift for shift, _ in arrived)
    n = len(arrived)
    return pl.pallas_call(
        functools.partial(more_kernel, shifts, False),
        out_shape=STATE,
        in_specs=[SMEM] + [VMEM] * (n + 4),
        out_specs=[VMEM] * 3,
        scratch_shapes=scratch(n) + [pltpu.VMEM((ROWS, HD), jnp.bfloat16)],
        input_output_aliases={n + 2: 0, n + 3: 1, n + 4: 2},
        compiler_params=PARAMS,
        cost_estimate=cost(n),
        name="more_blocks",
    )(place, x, *[block for _, block in arrived], *state)


def last_blocks(arrived, place, x, state):
    shifts = tuple(shift for shift, _ in arrived)
    n = len(arrived)
    return pl.pallas_call(
        functools.partial(more_kernel, shifts, True),
        out_shape=[jax.ShapeDtypeStruct((ROWS, GROUP * HD), jnp.bfloat16)],
        in_specs=[SMEM] + [VMEM] * (n + 4),
        out_specs=[VMEM],
        scratch_shapes=scratch(n) + [pltpu.VMEM((ROWS, HD), jnp.bfloat16)],
        compiler_params=PARAMS,
        cost_estimate=cost(n),
        name="last_blocks",
    )(place, x, *[block for _, block in arrived], *state)[0]


def local(queries, keys, values):
    rows = queries.shape[0]
    me = lax.axis_index("ctx")
    z, y = me // (NY * NX), (me // NX) % NY
    place = jnp.stack([z, y]).astype(jnp.int32)
    by_head = jnp.concatenate(
        [
            queries.reshape(rows, KVH, GROUP * HD),
            keys.reshape(rows, KVH, HD),
            values.reshape(rows, KVH, HD),
        ],
        axis=2,
    ).transpose(1, 0, 2)
    x = lax.all_to_all(by_head, "ctx", 0, 0, axis_index_groups=X_GROUPS, tiled=True)
    x = x.reshape(ROWS, (GROUP + 2) * HD)
    kv = lax.all_gather(
        x[:, GROUP * HD :], "ctx", axis=0, tiled=True, axis_index_groups=Z_GROUPS
    )
    x = x[:, : GROUP * HD]
    got = {}
    got[1] = lax.ppermute(kv, "ctx", ring(1))
    got[-1] = lax.ppermute(kv, "ctx", ring(-1))
    state = own_block(place, x, kv)
    for step, shifts in ((1, (1,)), (2, (-1, 2)), (3, (-2, 3, -3))):
        got[step], state = lax.optimization_barrier((got[step], state))
        got[step + 1] = lax.ppermute(got[step], "ctx", ring(1))
        if step < NY // 2 - 1:
            got[-step - 1] = lax.ppermute(got[-step], "ctx", ring(-1))
        state = more_blocks([(at, got[at]) for at in shifts], place, x, state)
    out = last_blocks([(NY // 2, got[NY // 2])], place, x, state)
    out = lax.all_to_all(
        out.reshape(NX, rows, GROUP * HD),
        "ctx",
        0,
        0,
        axis_index_groups=X_GROUPS,
        tiled=True,
    )
    return out.transpose(1, 0, 2).reshape(rows, QH * HD)


def solution(mesh):
    spec = P(("dp", "ctx"), None)
    return jax.shard_map(
        local, mesh=mesh, in_specs=(spec,) * 3, out_specs=spec, check_vma=False
    )
```

time: 90.3 us -> 85.2 us (0.944)
  the two profiles are of different devices: /device:TPU:128 before, /device:TPU:96 now
where the time goes in v4:
time: 85.2 us; the launch traced here: 84.9 us
  blocking collectives  39.9 us (47%)
  starting transfers between devices  23.1 us (27%)
  Pallas kernels  18 us (21%)
  local copies, waits for them, and re-layouts  2.04 us (2%)
  waiting for transfers between devices  1.53 us (2%)
    all_to_all x1, blocking collectives, local(): lax.all_to_all(by_head, 'ctx', 0, 0, axis_index_groups=X_GROUPS, tiled=True)  15 us
    all_gather x1, blocking collectives, local(): lax.all_gather(x[:, GROUP * HD:], 'ctx', axis=0, tiled=True, axis_index_g...  14.4 us
    pallas_call x3, Pallas kernels, more_blocks(): pl.pallas_call(functools.partial(more_kernel, shifts, False), out_shape=S...  13.1 us
    all_to_all x1, blocking collectives, local(): lax.all_to_all(out.reshape(NX, rows, GROUP * HD), 'ctx', 0, 0, axis_index...  10.5 us
    ppermute x2, starting transfers between devices, local(): got[-step - 1] = lax.ppermute(got[-step], 'ctx', ring(-1))  10.3 us
    ppermute x3, starting transfers between devices, local(): got[step + 1] = lax.ppermute(got[step], 'ctx', ring(1))  5.76 us
    ppermute x1, starting transfers between devices, local(): got[-1] = lax.ppermute(kv, 'ctx', ring(-1))  4.47 us
    ppermute x1, starting transfers between devices, local(): got[1] = lax.ppermute(kv, 'ctx', ring(1))  2.57 us
  transfers between devices with their start and end apart: 7, of which 1 were waited for; matrix products, arithmetic and copies ran while one was open for 0% of the time, Pallas kernels for 18%

profile of v4, /device:TPU:96, one launch (start us, length us, event | category | flops | bytes accessed | tf_op | source)
XLA Modules:
  0.0 84.9 jit_solution(8718883118196842879)
XLA Ops:
  0.0 0.0 copy-start
  0.0 0.0 copy-start.1
  0.0 1.1 %copy.24 = bf16[8,4,8,1024]{3,2,0,1:T(8,128)(2,1)S(1)} copy(bf16[8,4,8,1024]{3,2,1,0:T(8,128)(2,1)} %bitcast.28) | data formatting | bytes 1048576 | tf_op jit(solution)/shard_map/reshape | solution.py:213
  1.1 0.0 copy-done
  1.1 0.0 copy-done.1
  1.2 0.1 maximum_bitcast_fusion
  1.2 15.0 %all_to_all.10 = bf16[4,64,1280]{2,1,0:T(8,128)(2,1)S(1)} all-to-all(bf16[4,64,1280]{2,1,0:T(8,128)(2,1)S(1)} %maximum_bitcast_fusion), channel_id=1, replica_groups={{0,1,2,3},{4,5,6,7},{8,9,10,11},{12,13,14,15},{16,17,18,19},{20,21,22,2..., dimensions={0} | all-to-all | bytes 1310720 | tf_op jit(solution)/shard_map/all_to_all | solution.py:219
  16.2 14.4 %all_gather.3.kv_ref = bf16[512,256]{1,0:T(8,128)(2,1)S(1)} all-gather(bf16[256,256]{1,0:T(8,128)(2,1)S(1)} %slice.9), channel_id=1, replica_groups={{0,32},{1,33},{2,34},{3,35},{4,36},{5,37},{6,38},{7,39},{8,40},{9,41},{..., dimensions={0}, use_global_device_ids=true | all-gather | bytes 393216 | tf_op jit(solution)/shard_map/all_gather | solution.py:221
  30.7 2.6 %collective-permute-start = (bf16[512,256]{1,0:T(8,128)(2,1)S(1)}, bf16[512,256]{1,0:T(8,128)(2,1)S(1)}, u32[]{:S(2)}, u32[]{:S(2)}) collective-permute-start(bf16[512,256]{1,0:T(8,128)(2,1)S(1)} %all_gather.3.kv_ref), channel_id=1, source_target_pairs={{0,4},{1,5},{2,6},{3,7},{4,8},{5,9},{6,10},{7,11},{8,12},{9,13},{1... | collective-permute-start | bytes 786440 | tf_op jit(solution)/shard_map/ppermute | solution.py:226
  33.3 4.5 %collective-permute-start.3 = (bf16[512,256]{1,0:T(8,128)(2,1)S(1)}, bf16[512,256]{1,0:T(8,128)(2,1)S(1)}, u32[]{:S(2)}, u32[]{:S(2)}) collective-permute-start(bf16[512,256]{1,0:T(8,128)(2,1)S(1)} %all_gather.3.kv_ref), channel_id=1, source_target_pairs={{0,28},{1,29},{2,30},{3,31},{4,0},{5,1},{6,2},{7,3},{8,4},{9,5},{1... | collective-permute-start | bytes 786440 | tf_op jit(solution)/shard_map/ppermute | solution.py:227
  37.7 0.1 pad_add_fusion.place.refs_0_
  37.8 0.1 slice.8.x_ref.refs_1_
  37.9 2.4 %own_block.1 = (f32[256,1024]{1,0:T(8,128)S(1)}, f32[256,1024]{1,0:T(8,128)S(1)}, f32[256,1024]{1,0:T(8,128)S(1)}) custom-call(s32[2]{0:T(128)S(1)} %pad_add_fusion.place.refs_0_, bf16[256,1024]{1,0:T(8,128)(2,1)S(1)} %slice.8.x_ref.refs_1_, bf16[512,256]{1,0:T(8,128)(2,1)S(1)} %all_gather.3.kv_ref), custom_call_target="tpu_custom_call" | custom-call | flops 536870912 | bytes 8388608 | tf_op jit(solution)/shard_map/own_block/pallas_call | solution.py:163
  40.3 0.0 collective-permute-done.refs_2_
  40.3 1.9 %collective-permute-start.1 = (bf16[512,256]{1,0:T(8,128)(2,1)S(1)}, bf16[512,256]{1,0:T(8,128)(2,1)S(1)}, u32[]{:S(2)}, u32[]{:S(2)}) collective-permute-start(bf16[512,256]{1,0:T(8,128)(2,1)S(1)} %collective-permute-done.refs_2_), channel_id=1, source_target_pairs={{0,4},{1,5},{2,6},{3,7},{4,8},{5,9},{6,10},{7,11},{8,12},{9,13},{1... | collective-permute-start | bytes 786440 | tf_op jit(solution)/shard_map/ppermute | solution.py:231
  42.2 0.0 collective-permute-done.3.refs_2_
  42.2 5.1 %collective-permute-start.5 = (bf16[512,256]{1,0:T(8,128)(2,1)S(1)}, bf16[512,256]{1,0:T(8,128)(2,1)S(1)}, u32[]{:S(2)}, u32[]{:S(2)}) collective-permute-start(bf16[512,256]{1,0:T(8,128)(2,1)S(1)} %collective-permute-done.3.refs_2_), channel_id=1, source_target_pairs={{0,28},{1,29},{2,30},{3,31},{4,0},{5,1},{6,2},{7,3},{8,4},{9,5},{1... | collective-permute-start | bytes 786440 | tf_op jit(solution)/shard_map/ppermute | solution.py:233
  47.4 2.8 %more_blocks.3 = (f32[256,1024]{1,0:T(8,128)S(1)}, f32[256,1024]{1,0:T(8,128)S(1)}, f32[256,1024]{1,0:T(8,128)S(1)}) custom-call(s32[2]{0:T(128)S(1)} %pad_add_fusion.place.refs_0_, bf16[256,1024]{1,0:T(8,128)(2,1)S(1)} %slice.8.x_ref.refs_1_, ...), custom_call_target="tpu_custom_call", output_to_operand_aliasing={{0}: (3, {}), {1}: (4, {}), {2}: (5, {})} | custom-call | flops 536870912 | bytes 8388608 | tf_op jit(solution)/shard_map/more_blocks/pallas_call | solution.py:178
  50.2 0.0 collective-permute-done.1.refs_3_
  50.2 1.9 %collective-permute-start.2 = (bf16[512,256]{1,0:T(8,128)(2,1)S(1)}, bf16[512,256]{1,0:T(8,128)(2,1)S(1)}, u32[]{:S(2)}, u32[]{:S(2)}) collective-permute-start(bf16[512,256]{1,0:T(8,128)(2,1)S(1)} %collective-permute-done.1.refs_3_), channel_id=1, source_target_pairs={{0,4},{1,5},{2,6},{3,7},{4,8},{5,9},{6,10},{7,11},{8,12},{9,13},{1... | collective-permute-start | bytes 786440 | tf_op jit(solution)/shard_map/ppermute | solution.py:231
  52.1 0.0 collective-permute-done.5.refs_2_
  52.1 5.1 %collective-permute-start.6 = (bf16[512,256]{1,0:T(8,128)(2,1)S(1)}, bf16[512,256]{1,0:T(8,128)(2,1)S(1)}, u32[]{:S(2)}, u32[]{:S(2)}) collective-permute-start(bf16[512,256]{1,0:T(8,128)(2,1)S(1)} %collective-permute-done.5.refs_2_), channel_id=1, source_target_pairs={{0,28},{1,29},{2,30},{3,31},{4,0},{5,1},{6,2},{7,3},{8,4},{9,5},{1... | collective-permute-start | bytes 786440 | tf_op jit(solution)/shard_map/ppermute | solution.py:233
  57.3 4.3 %more_blocks.4 = (f32[256,1024]{1,0:T(8,128)S(1)}, f32[256,1024]{1,0:T(8,128)S(1)}, f32[256,1024]{1,0:T(8,128)S(1)}) custom-call(s32[2]{0:T(128)S(1)} %pad_add_fusion.place.refs_0_, bf16[256,1024]{1,0:T(8,128)(2,1)S(1)} %slice.8.x_ref.refs_1_, ...), custom_call_target="tpu_custom_call", output_to_operand_aliasing={{0}: (4, {}), {1}: (5, {}), {2}: (6, {})} | custom-call | flops 1073741824 | bytes 8388608 | tf_op jit(solution)/shard_map/more_blocks/pallas_call | solution.py:178
  61.5 0.0 collective-permute-done.2.refs_3_
  61.6 1.9 %collective-permute-start.4 = (bf16[512,256]{1,0:T(8,128)(2,1)S(1)}, bf16[512,256]{1,0:T(8,128)(2,1)S(1)}, u32[]{:S(2)}, u32[]{:S(2)}) collective-permute-start(bf16[512,256]{1,0:T(8,128)(2,1)S(1)} %collective-permute-done.2.refs_3_), channel_id=1, source_target_pairs={{0,4},{1,5},{2,6},{3,7},{4,8},{5,9},{6,10},{7,11},{8,12},{9,13},{1... | collective-permute-start | bytes 786440 | tf_op jit(solution)/shard_map/ppermute | solution.py:231
  63.5 0.0 collective-permute-done.6.refs_4_
  63.5 6.0 %more_blocks.5 = (f32[256,1024]{1,0:T(8,128)S(1)}, f32[256,1024]{1,0:T(8,128)S(1)}, f32[256,1024]{1,0:T(8,128)S(1)}) custom-call(s32[2]{0:T(128)S(1)} %pad_add_fusion.place.refs_0_, bf16[256,1024]{1,0:T(8,128)(2,1)S(1)} %slice.8.x_ref.refs_1_, ...), custom_call_target="tpu_custom_call", output_to_operand_aliasing={{0}: (5, {}), {1}: (6, {}), {2}: (7, {})} | custom-call | flops 1610612736 | bytes 8388608 | tf_op jit(solution)/shard_map/more_blocks/pallas_call | solution.py:178
  69.5 1.5 %collective-permute-done.4.refs_2_ = bf16[512,256]{1,0:T(8,128)(2,1)S(1)} collective-permute-done((bf16[512,256]{1,0:T(8,128)(2,1)S(1)}, bf16[512,256]{1,0:T(8,128)(2,1)S(1)}, u32[]{:S(2)}, u32[]{:S(2)}) %collective-permute-start.4) | collective-permute-done | bytes 262176 | tf_op jit(solution)/shard_map/ppermute | solution.py:231
  71.0 2.5 %last_blocks.1 = bf16[256,1024]{1,0:T(8,128)(2,1)S(1)} custom-call(s32[2]{0:T(128)S(1)} %pad_add_fusion.place.refs_0_, bf16[256,1024]{1,0:T(8,128)(2,1)S(1)} %slice.8.x_ref.refs_1_, bf16[512,256]{1,0:T(8,128)(2,1)S(1)} %collective-permute-done.4.refs_2_, f32[256,1024]{1,0:T(8,128)S(1)} %get-tuple-element.50.refs_3_, ...), custom_call_target="tpu_custom_call" | custom-call | flops 536870912 | bytes 8388608 | tf_op jit(solution)/shard_map/last_blocks/pallas_call | solution.py:194
  73.5 10.5 %all_to_all.11 = bf16[4,64,1024]{2,1,0:T(8,128)(2,1)S(1)} all-to-all(bf16[4,64,1024]{2,1,0:T(8,128)(2,1)S(1)} %bitcast.23), channel_id=1, replica_groups={{0,1,2,3},{4,5,6,7},{8,9,10,11},{12,13,14,15},{16,17,18,19},{20,21,22,2..., dimensions={0} | all-to-all | bytes 1048576 | tf_op jit(solution)/shard_map/all_to_all | solution.py:236
  84.0 0.8 copy.20
  (2 shorter events, 0.0 us)
Async XLA Ops:
  0.0 1.1 %copy-start = (bf16[64,512]{1,0:T(8,128)(2,1)S(1)}, bf16[64,512]{1,0:T(8,128)(2,1)}, u32[]{:S(2)}) copy-start(bf16[64,512]{1,0:T(8,128)(2,1)} %param.4) | copy-start | bytes 196612
  0.0 1.1 %copy-start.1 = (bf16[64,512]{1,0:T(8,128)(2,1)S(1)}, bf16[64,512]{1,0:T(8,128)(2,1)}, u32[]{:S(2)}) copy-start(bf16[64,512]{1,0:T(8,128)(2,1)} %param.5) | copy-start | bytes 196612
  30.7 9.6 %collective-permute-start = (bf16[512,256]{1,0:T(8,128)(2,1)S(1)}, bf16[512,256]{1,0:T(8,128)(2,1)S(1)}, u32[]{:S(2)}, u32[]{:S(2)}) collective-permute-start(bf16[512,256]{1,0:T(8,128)(2,1)S(1)} %all_gather.3.kv_ref), channel_id=1, source_target_pairs={{0,4},{1,5},{2,6},{3,7},{4,8},{5,9},{6,10},{7,11},{8,12},{9,13},{1... | collective-permute-start | bytes 786440 | tf_op jit(solution)/shard_map/ppermute | solution.py:226
  33.3 9.0 %collective-permute-start.3 = (bf16[512,256]{1,0:T(8,128)(2,1)S(1)}, bf16[512,256]{1,0:T(8,128)(2,1)S(1)}, u32[]{:S(2)}, u32[]{:S(2)}) collective-permute-start(bf16[512,256]{1,0:T(8,128)(2,1)S(1)} %all_gather.3.kv_ref), channel_id=1, source_target_pairs={{0,28},{1,29},{2,30},{3,31},{4,0},{5,1},{6,2},{7,3},{8,4},{9,5},{1... | collective-permute-start | bytes 786440 | tf_op jit(solution)/shard_map/ppermute | solution.py:227
  40.3 9.9 %collective-permute-start.1 = (bf16[512,256]{1,0:T(8,128)(2,1)S(1)}, bf16[512,256]{1,0:T(8,128)(2,1)S(1)}, u32[]{:S(2)}, u32[]{:S(2)}) collective-permute-start(bf16[512,256]{1,0:T(8,128)(2,1)S(1)} %collective-permute-done.refs_2_), channel_id=1, source_target_pairs={{0,4},{1,5},{2,6},{3,7},{4,8},{5,9},{6,10},{7,11},{8,12},{9,13},{1... | collective-permute-start | bytes 786440 | tf_op jit(solution)/shard_map/ppermute | solution.py:231
  42.2 9.9 %collective-permute-start.5 = (bf16[512,256]{1,0:T(8,128)(2,1)S(1)}, bf16[512,256]{1,0:T(8,128)(2,1)S(1)}, u32[]{:S(2)}, u32[]{:S(2)}) collective-permute-start(bf16[512,256]{1,0:T(8,128)(2,1)S(1)} %collective-permute-done.3.refs_2_), channel_id=1, source_target_pairs={{0,28},{1,29},{2,30},{3,31},{4,0},{5,1},{6,2},{7,3},{8,4},{9,5},{1... | collective-permute-start | bytes 786440 | tf_op jit(solution)/shard_map/ppermute | solution.py:233
  50.2 11.4 %collective-permute-start.2 = (bf16[512,256]{1,0:T(8,128)(2,1)S(1)}, bf16[512,256]{1,0:T(8,128)(2,1)S(1)}, u32[]{:S(2)}, u32[]{:S(2)}) collective-permute-start(bf16[512,256]{1,0:T(8,128)(2,1)S(1)} %collective-permute-done.1.refs_3_), channel_id=1, source_target_pairs={{0,4},{1,5},{2,6},{3,7},{4,8},{5,9},{6,10},{7,11},{8,12},{9,13},{1... | collective-permute-start | bytes 786440 | tf_op jit(solution)/shard_map/ppermute | solution.py:231
  52.1 11.4 %collective-permute-start.6 = (bf16[512,256]{1,0:T(8,128)(2,1)S(1)}, bf16[512,256]{1,0:T(8,128)(2,1)S(1)}, u32[]{:S(2)}, u32[]{:S(2)}) collective-permute-start(bf16[512,256]{1,0:T(8,128)(2,1)S(1)} %collective-permute-done.5.refs_2_), channel_id=1, source_target_pairs={{0,28},{1,29},{2,30},{3,31},{4,0},{5,1},{6,2},{7,3},{8,4},{9,5},{1... | collective-permute-start | bytes 786440 | tf_op jit(solution)/shard_map/ppermute | solution.py:233
  61.6 9.5 %collective-permute-start.4 = (bf16[512,256]{1,0:T(8,128)(2,1)S(1)}, bf16[512,256]{1,0:T(8,128)(2,1)S(1)}, u32[]{:S(2)}, u32[]{:S(2)}) collective-permute-start(bf16[512,256]{1,0:T(8,128)(2,1)S(1)} %collective-permute-done.2.refs_3_), channel_id=1, source_target_pairs={{0,4},{1,5},{2,6},{3,7},{4,8},{5,9},{6,10},{7,11},{8,12},{9,13},{1... | collective-permute-start | bytes 786440 | tf_op jit(solution)/shard_map/ppermute | solution.py:231

commit v5 on v4

--- a/solution.py
+++ b/solution.py
@@ -24,7 +24,18 @@
 
 
 X_GROUPS = [[index(z, y, x) for x in range(NX)] for z in range(NZ) for y in range(NY)]
-Z_GROUPS = [[index(z, y, x) for z in range(NZ)] for y in range(NY) for x in range(NX)]
+Z_SWAP = [
+    (index(z, y, x), index(1 - z, y, x))
+    for z in range(NZ)
+    for y in range(NY)
+    for x in range(NX)
+]
+
+
+def exchange(pieces):
+    return lax.all_to_all(
+        pieces, "ctx", 0, 0, axis_index_groups=X_GROUPS, tiled=True
+    )
 
 
 def ring(step):
@@ -84,7 +95,7 @@
     n = len(shifts)
     place, x_ref, blocks = refs[0], refs[1], refs[2 : 2 + n]
     acc_in, max_in, sum_in = refs[2 + n : 5 + n]
-    outs, (key_scr, value_scr, safe_scr) = refs[5 + n : -3], refs[-3:]
+    outs, (key_scr, value_scr) = refs[5 + n : -2], refs[-2:]
     z, y = place[0], place[1]
     allowed = []
     for shift in shifts:
@@ -92,30 +103,20 @@
         allowed += [z + before >= 1, z + before == 2]
     any_allowed = functools.reduce(jnp.logical_or, allowed)
 
-    def put(c, key, value, one):
-        key_scr[c * ROWS : (c + 1) * ROWS, :] = key
-        value_scr[c * ROWS : (c + 1) * ROWS, :HD] = value
-        value_scr[c * ROWS : (c + 1) * ROWS, HD:] = one
-
     @pl.when(any_allowed)
     def _():
-        for c in range(2 * n - 2, -1, -2):
-
-            @pl.when(allowed[c])
-            def _(c=c):
-                safe_scr[...] = blocks[c // 2][:ROWS, :HD]
-
-        one = jnp.ones((ROWS, HD), jnp.bfloat16)
-        for c in range(2 * n):
+        safe = blocks[n - 1][:ROWS, :HD]
+        for b in range(n - 2, -1, -1):
+            safe = jnp.where(allowed[2 * b], blocks[b][:ROWS, :HD], safe)
+        for c, seen in enumerate(allowed):
             block, at = blocks[c // 2], c % 2 * ROWS
-
-            @pl.when(allowed[c])
-            def _(c=c, block=block, at=at):
-                put(c, block[at : at + ROWS, :HD], block[at : at + ROWS, HD:], one)
-
-            @pl.when(jnp.logical_not(allowed[c]))
-            def _(c=c):
-                put(c, safe_scr[...], jnp.zeros_like(one), jnp.zeros_like(one))
+            rows = slice(c * ROWS, (c + 1) * ROWS)
+            value = block[at : at + ROWS, HD:]
+            key_scr[rows, :] = jnp.where(seen, block[at : at + ROWS, :HD], safe)
+            value_scr[rows, :HD] = jnp.where(seen, value, jnp.zeros_like(value))
+            value_scr[rows, HD:] = jnp.where(
+                seen, jnp.ones_like(value), jnp.zeros_like(value)
+            )
 
         def finish(cols, scores):
             old = max_in[:, cols]
@@ -180,7 +181,7 @@
         out_shape=STATE,
         in_specs=[SMEM] + [VMEM] * (n + 4),
         out_specs=[VMEM] * 3,
-        scratch_shapes=scratch(n) + [pltpu.VMEM((ROWS, HD), jnp.bfloat16)],
+        scratch_shapes=scratch(n),
         input_output_aliases={n + 2: 0, n + 3: 1, n + 4: 2},
         compiler_params=PARAMS,
         cost_estimate=cost(n),
@@ -196,7 +197,7 @@
         out_shape=[jax.ShapeDtypeStruct((ROWS, GROUP * HD), jnp.bfloat16)],
         in_specs=[SMEM] + [VMEM] * (n + 4),
         out_specs=[VMEM],
-        scratch_shapes=scratch(n) + [pltpu.VMEM((ROWS, HD), jnp.bfloat16)],
+        scratch_shapes=scratch(n),
         compiler_params=PARAMS,
         cost_estimate=cost(n),
         name="last_blocks",
@@ -209,19 +210,15 @@
     z, y = me // (NY * NX), (me // NX) % NY
     place = jnp.stack([z, y]).astype(jnp.int32)
     by_head = jnp.concatenate(
-        [
-            queries.reshape(rows, KVH, GROUP * HD),
-            keys.reshape(rows, KVH, HD),
-            values.reshape(rows, KVH, HD),
-        ],
-        axis=2,
+        [keys.reshape(rows, KVH, HD), values.reshape(rows, KVH, HD)], axis=2
     ).transpose(1, 0, 2)
-    x = lax.all_to_all(by_head, "ctx", 0, 0, axis_index_groups=X_GROUPS, tiled=True)
-    x = x.reshape(ROWS, (GROUP + 2) * HD)
-    kv = lax.all_gather(
-        x[:, GROUP * HD :], "ctx", axis=0, tiled=True, axis_index_groups=Z_GROUPS
-    )
-    x = x[:, : GROUP * HD]
+    own = exchange(by_head).reshape(ROWS, 2 * HD)
+    other = lax.ppermute(own, "ctx", Z_SWAP)
+    x = exchange(queries.reshape(rows, KVH, GROUP * HD).transpose(1, 0, 2))
+    x = x.reshape(ROWS, GROUP * HD)
+    kv = jnp.concatenate(
+        [jnp.where(z == 0, own, other), jnp.where(z == 0, other, own)], axis=0
+    )
     got = {}
     got[1] = lax.ppermute(kv, "ctx", ring(1))
     got[-1] = lax.ppermute(kv, "ctx", ring(-1))
@@ -233,14 +230,7 @@
             got[-step - 1] = lax.ppermute(got[-step], "ctx", ring(-1))
         state = more_blocks([(at, got[at]) for at in shifts], place, x, state)
     out = last_blocks([(NY // 2, got[NY // 2])], place, x, state)
-    out = lax.all_to_all(
-        out.reshape(NX, rows, GROUP * HD),
-        "ctx",
-        0,
-        0,
-        axis_index_groups=X_GROUPS,
-        tiled=True,
-    )
+    out = exchange(out.reshape(NX, rows, GROUP * HD))
     return out.transpose(1, 0, 2).reshape(rows, QH * HD)
 
 

time: 85.2 us -> 83.8 us (0.984)
  the two profiles are of different devices: /device:TPU:96 before, /device:TPU:32 now
where the time goes in v5:
time: 83.8 us; the launch traced here: 83.3 us
  starting transfers between devices  37.5 us (45%)
  blocking collectives  21.9 us (26%)
  Pallas kernels  17.5 us (21%)
  local copies, waits for them, and re-layouts  3.43 us (4%)
  waiting for transfers between devices  2.61 us (3%)
    all_to_all x2, blocking collectives, exchange(): lax.all_to_all(pieces, 'ctx', 0, 0, axis_index_groups=X_GROUPS, tiled=True)  21.9 us
    pallas_call x3, Pallas kernels, more_blocks(): pl.pallas_call(functools.partial(more_kernel, shifts, False), out_shape=S...  12.7 us
    ppermute x1, starting transfers between devices, local(): other = lax.ppermute(own, 'ctx', Z_SWAP)  10.9 us
    ppermute x2, starting transfers between devices, local(): got[-step - 1] = lax.ppermute(got[-step], 'ctx', ring(-1))  9.6 us
    ppermute x3, starting transfers between devices, local(): got[step + 1] = lax.ppermute(got[step], 'ctx', ring(1))  6.43 us
    ppermute x1, starting transfers between devices, local(): got[-1] = lax.ppermute(kv, 'ctx', ring(-1))  4.47 us
    all_to_all x1, starting transfers between devices, exchange(): lax.all_to_all(pieces, 'ctx', 0, 0, axis_index_groups=X_GROUPS, tiled=True)  3.47 us
    ppermute x1, starting transfers between devices, local(): got[1] = lax.ppermute(kv, 'ctx', ring(1))  2.59 us
  transfers between devices with their start and end apart: 9, of which 2 were waited for; matrix products, arithmetic and copies ran while one was open for 1% of the time, Pallas kernels for 18%

profile of v5, /device:TPU:32, one launch (start us, length us, event | category | flops | bytes accessed | tf_op | source)
XLA Modules:
  0.0 83.3 jit_solution(15289133141479536244)
XLA Ops:
  0.0 0.0 copy-start
  0.0 0.8 %copy-done = bf16[64,512]{1,0:T(8,128)(2,1)S(1)} copy-done((bf16[64,512]{1,0:T(8,128)(2,1)S(1)}, bf16[64,512]{1,0:T(8,128)(2,1)}, u32[]{:S(2)}) %copy-start) | copy-done | bytes 65560
  0.8 0.0 copy-start.1
  0.8 0.9 %copy_bitcast_fusion = (bf16[64,4,128]{2,0,1:T(8,128)(2,1)S(1)}, bf16[64,4,128]{2,0,1:T(8,128)(2,1)S(1)}) fusion(bf16[64,512]{1,0:T(8,128)(2,1)S(1)} %copy-done, bf16[64,512]{1,0:T(8,128)(2,1)} %param.5), kind=kLoop, calls=%fused_computation.5 | loop fusion | bytes 262144 | tf_op jit(solution)/shard_map/reshape | solution.py:213
  1.8 10.1 %all_to_all.15 = bf16[4,64,256]{2,1,0:T(8,128)(2,1)S(1)} all-to-all(bf16[4,64,256]{2,1,0:T(8,128)(2,1)S(1)} %maximum_bitcast_fusion), channel_id=1, replica_groups={{0,1,2,3},{4,5,6,7},{8,9,10,11},{12,13,14,15},{16,17,18,19},{20,21,22,2..., dimensions={0} | all-to-all | bytes 262144 | tf_op jit(solution)/shard_map/all_to_all | solution.py:36
  11.9 10.9 %collective-permute-start = (bf16[256,256]{1,0:T(8,128)(2,1)S(1)}, bf16[256,256]{1,0:T(8,128)(2,1)S(1)}, u32[]{:S(2)}, u32[]{:S(2)}) collective-permute-start(bf16[256,256]{1,0:T(8,128)(2,1)S(1)} %bitcast.36), channel_id=1, source_target_pairs={{0,32},{1,33},{2,34},{3,35},{4,36},{5,37},{6,38},{7,39},{8,40},{9,... | collective-permute-start | bytes 393224 | tf_op jit(solution)/shard_map/ppermute | solution.py:216
  22.8 0.0 copy-done.1
  22.8 0.8 %copy.24 = bf16[8,4,8,1024]{3,2,0,1:T(8,128)(2,1)} copy(bf16[8,4,8,1024]{3,2,1,0:T(8,128)(2,1)S(1)} %bitcast.37) | data formatting | bytes 1048576 | tf_op jit(solution)/shard_map/reshape | solution.py:217
  23.6 3.5 %all-to-all-start = ((bf16[4,64,1024]{2,1,0:T(8,128)(2,1)}), bf16[4,64,1024]{2,1,0:T(8,128)(2,1)S(1)}, u32[]{:S(2)}, u32[]{:S(2)}) async-start(bf16[4,64,1024]{2,1,0:T(8,128)(2,1)} %bitcast.28), calls=%async_computation | async-start | bytes 1048576 | tf_op jit(solution)/shard_map/all_to_all | solution.py:36
  27.1 0.0 collective-permute-done
  27.2 2.6 %collective-permute-start.1 = (bf16[512,256]{1,0:T(8,128)(2,1)S(1)}, bf16[512,256]{1,0:T(8,128)(2,1)S(1)}, u32[]{:S(2)}, u32[]{:S(2)}) collective-permute-start(bf16[512,256]{1,0:T(8,128)(2,1)S(1)} %pad_maximum_fusion.kv_ref), channel_id=1, source_target_pairs={{0,4},{1,5},{2,6},{3,7},{4,8},{5,9},{6,10},{7,11},{8,12},{9,13},{1... | collective-permute-start | bytes 786440 | tf_op jit(solution)/shard_map/ppermute | solution.py:223
  29.8 4.5 %collective-permute-start.4 = (bf16[512,256]{1,0:T(8,128)(2,1)S(1)}, bf16[512,256]{1,0:T(8,128)(2,1)S(1)}, u32[]{:S(2)}, u32[]{:S(2)}) collective-permute-start(bf16[512,256]{1,0:T(8,128)(2,1)S(1)} %pad_maximum_fusion.kv_ref), channel_id=1, source_target_pairs={{0,28},{1,29},{2,30},{3,31},{4,0},{5,1},{6,2},{7,3},{8,4},{9,5},{1... | collective-permute-start | bytes 786440 | tf_op jit(solution)/shard_map/ppermute | solution.py:224
  34.3 0.1 pad_add_fusion.place.refs_0_
  34.4 0.8 all-to-all-done
  35.1 2.4 %own_block.1 = (f32[256,1024]{1,0:T(8,128)S(1)}, f32[256,1024]{1,0:T(8,128)S(1)}, f32[256,1024]{1,0:T(8,128)S(1)}) custom-call(s32[2]{0:T(128)S(1)} %pad_add_fusion.place.refs_0_, bf16[256,1024]{1,0:T(8,128)(2,1)S(1)} %bitcast.29, bf16[512,256]{1,0:T(8,128)(2,1)S(1)} %pad_maximum_fusion.kv_ref), custom_call_target="tpu_custom_call" | custom-call | flops 536870912 | bytes 8388608 | tf_op jit(solution)/shard_map/own_block/pallas_call | solution.py:164
  37.5 0.0 collective-permute-done.1.refs_2_
  37.5 2.6 %collective-permute-start.2 = (bf16[512,256]{1,0:T(8,128)(2,1)S(1)}, bf16[512,256]{1,0:T(8,128)(2,1)S(1)}, u32[]{:S(2)}, u32[]{:S(2)}) collective-permute-start(bf16[512,256]{1,0:T(8,128)(2,1)S(1)} %collective-permute-done.1.refs_2_), channel_id=1, source_target_pairs={{0,4},{1,5},{2,6},{3,7},{4,8},{5,9},{6,10},{7,11},{8,12},{9,13},{1... | collective-permute-start | bytes 786440 | tf_op jit(solution)/shard_map/ppermute | solution.py:228
  40.1 0.0 collective-permute-done.4.refs_2_
  40.1 4.5 %collective-permute-start.6 = (bf16[512,256]{1,0:T(8,128)(2,1)S(1)}, bf16[512,256]{1,0:T(8,128)(2,1)S(1)}, u32[]{:S(2)}, u32[]{:S(2)}) collective-permute-start(bf16[512,256]{1,0:T(8,128)(2,1)S(1)} %collective-permute-done.4.refs_2_), channel_id=1, source_target_pairs={{0,28},{1,29},{2,30},{3,31},{4,0},{5,1},{6,2},{7,3},{8,4},{9,5},{1... | collective-permute-start | bytes 786440 | tf_op jit(solution)/shard_map/ppermute | solution.py:230
  44.6 2.8 %more_blocks.3 = (f32[256,1024]{1,0:T(8,128)S(1)}, f32[256,1024]{1,0:T(8,128)S(1)}, f32[256,1024]{1,0:T(8,128)S(1)}) custom-call(s32[2]{0:T(128)S(1)} %pad_add_fusion.place.refs_0_, bf16[256,1024]{1,0:T(8,128)(2,1)S(1)} %bitcast.30, bf16[512,256]{1,0:T(8,128)(2,1)S(1)} %collective-permute-done.1.refs_2_, ...), custom_call_target="tpu_custom_call", output_to_operand_aliasing={{0}: (3, {}), {1}: (4, {}), {2}: (5, {})} | custom-call | flops 536870912 | bytes 8388608 | tf_op jit(solution)/shard_map/more_blocks/pallas_call | solution.py:179
  47.4 0.0 collective-permute-done.2.refs_3_
  47.4 1.9 %collective-permute-start.3 = (bf16[512,256]{1,0:T(8,128)(2,1)S(1)}, bf16[512,256]{1,0:T(8,128)(2,1)S(1)}, u32[]{:S(2)}, u32[]{:S(2)}) collective-permute-start(bf16[512,256]{1,0:T(8,128)(2,1)S(1)} %collective-permute-done.2.refs_3_), channel_id=1, source_target_pairs={{0,4},{1,5},{2,6},{3,7},{4,8},{5,9},{6,10},{7,11},{8,12},{9,13},{1... | collective-permute-start | bytes 786440 | tf_op jit(solution)/shard_map/ppermute | solution.py:228
  49.3 0.0 collective-permute-done.6.refs_2_
  49.3 5.1 %collective-permute-start.7 = (bf16[512,256]{1,0:T(8,128)(2,1)S(1)}, bf16[512,256]{1,0:T(8,128)(2,1)S(1)}, u32[]{:S(2)}, u32[]{:S(2)}) collective-permute-start(bf16[512,256]{1,0:T(8,128)(2,1)S(1)} %collective-permute-done.6.refs_2_), channel_id=1, source_target_pairs={{0,28},{1,29},{2,30},{3,31},{4,0},{5,1},{6,2},{7,3},{8,4},{9,5},{1... | collective-permute-start | bytes 786440 | tf_op jit(solution)/shard_map/ppermute | solution.py:230
  54.5 4.2 %more_blocks.4 = (f32[256,1024]{1,0:T(8,128)S(1)}, f32[256,1024]{1,0:T(8,128)S(1)}, f32[256,1024]{1,0:T(8,128)S(1)}) custom-call(s32[2]{0:T(128)S(1)} %pad_add_fusion.place.refs_0_, bf16[256,1024]{1,0:T(8,128)(2,1)S(1)} %bitcast.31, bf16[512,256]{1,0:T(8,128)(2,1)S(1)} %collective-permute-done.4.refs_2_, ...), custom_call_target="tpu_custom_call", output_to_operand_aliasing={{0}: (4, {}), {1}: (5, {}), {2}: (6, {})} | custom-call | flops 1073741824 | bytes 8388608 | tf_op jit(solution)/shard_map/more_blocks/pallas_call | solution.py:179
  58.7 0.0 collective-permute-done.3.refs_3_
  58.7 1.9 %collective-permute-start.5 = (bf16[512,256]{1,0:T(8,128)(2,1)S(1)}, bf16[512,256]{1,0:T(8,128)(2,1)S(1)}, u32[]{:S(2)}, u32[]{:S(2)}) collective-permute-start(bf16[512,256]{1,0:T(8,128)(2,1)S(1)} %collective-permute-done.3.refs_3_), channel_id=1, source_target_pairs={{0,4},{1,5},{2,6},{3,7},{4,8},{5,9},{6,10},{7,11},{8,12},{9,13},{1... | collective-permute-start | bytes 786440 | tf_op jit(solution)/shard_map/ppermute | solution.py:228
  60.6 0.0 collective-permute-done.7.refs_4_
  60.6 5.7 %more_blocks.5 = (f32[256,1024]{1,0:T(8,128)S(1)}, f32[256,1024]{1,0:T(8,128)S(1)}, f32[256,1024]{1,0:T(8,128)S(1)}) custom-call(s32[2]{0:T(128)S(1)} %pad_add_fusion.place.refs_0_, bf16[256,1024]{1,0:T(8,128)(2,1)S(1)} %bitcast.32, bf16[512,256]{1,0:T(8,128)(2,1)S(1)} %collective-permute-done.6.refs_2_, ...), custom_call_target="tpu_custom_call", output_to_operand_aliasing={{0}: (5, {}), {1}: (6, {}), {2}: (7, {})} | custom-call | flops 1610612736 | bytes 8388608 | tf_op jit(solution)/shard_map/more_blocks/pallas_call | solution.py:179
  66.4 1.8 %collective-permute-done.5.refs_2_ = bf16[512,256]{1,0:T(8,128)(2,1)S(1)} collective-permute-done((bf16[512,256]{1,0:T(8,128)(2,1)S(1)}, bf16[512,256]{1,0:T(8,128)(2,1)S(1)}, u32[]{:S(2)}, u32[]{:S(2)}) %collective-permute-start.5) | collective-permute-done | bytes 262176 | tf_op jit(solution)/shard_map/ppermute | solution.py:228
  68.2 2.4 %last_blocks.1 = bf16[256,1024]{1,0:T(8,128)(2,1)S(1)} custom-call(s32[2]{0:T(128)S(1)} %pad_add_fusion.place.refs_0_, bf16[256,1024]{1,0:T(8,128)(2,1)S(1)} %bitcast.33, bf16[512,256]{1,0:T(8,128)(2,1)S(1)} %collective-permute-done.5.refs_2_, f32[256,1024]{1,0:T(8,128)S(1)} %get-tuple-element.50.refs_3_, f32[256,1024]{1,0:T(8,128)S(1)} %get-tuple-element.51.refs_4_, ...), custom_call_target="tpu_custom_call" | custom-call | flops 536870912 | bytes 8388608 | tf_op jit(solution)/shard_map/last_blocks/pallas_call | solution.py:195
  70.6 11.8 %all_to_all.16 = bf16[4,64,1024]{2,1,0:T(8,128)(2,1)S(1)} all-to-all(bf16[4,64,1024]{2,1,0:T(8,128)(2,1)S(1)} %bitcast.34), channel_id=1, replica_groups={{0,1,2,3},{4,5,6,7},{8,9,10,11},{12,13,14,15},{16,17,18,19},{20,21,22,2..., dimensions={0} | all-to-all | bytes 1048576 | tf_op jit(solution)/shard_map/all_to_all | solution.py:36
  82.4 0.8 %copy.20 = bf16[4,8,8,1024]{3,2,0,1:T(8,128)(2,1)} copy(bf16[4,8,8,1024]{3,2,1,0:T(8,128)(2,1)S(1)} %bitcast.35) | data formatting | bytes 1048576 | tf_op jit(solution)/shard_map/reshape | solution.py:234
  (3 shorter events, 0.1 us)
Async XLA Ops:
  0.0 0.8 %copy-start = (bf16[64,512]{1,0:T(8,128)(2,1)S(1)}, bf16[64,512]{1,0:T(8,128)(2,1)}, u32[]{:S(2)}) copy-start(bf16[64,512]{1,0:T(8,128)(2,1)} %param.4) | copy-start | bytes 196612
  0.8 21.9 %copy-start.1 = (bf16[64,4096]{1,0:T(8,128)(2,1)S(1)}, bf16[64,4096]{1,0:T(8,128)(2,1)}, u32[]{:S(2)}) copy-start(bf16[64,4096]{1,0:T(8,128)(2,1)} %param.3) | copy-start | bytes 1572868
  11.9 15.3 %collective-permute-start = (bf16[256,256]{1,0:T(8,128)(2,1)S(1)}, bf16[256,256]{1,0:T(8,128)(2,1)S(1)}, u32[]{:S(2)}, u32[]{:S(2)}) collective-permute-start(bf16[256,256]{1,0:T(8,128)(2,1)S(1)} %bitcast.36), channel_id=1, source_target_pairs={{0,32},{1,33},{2,34},{3,35},{4,36},{5,37},{6,38},{7,39},{8,40},{9,... | collective-permute-start | bytes 393224 | tf_op jit(solution)/shard_map/ppermute | solution.py:216
  23.6 11.5 %all-to-all-start = ((bf16[4,64,1024]{2,1,0:T(8,128)(2,1)}), bf16[4,64,1024]{2,1,0:T(8,128)(2,1)S(1)}, u32[]{:S(2)}, u32[]{:S(2)}) async-start(bf16[4,64,1024]{2,1,0:T(8,128)(2,1)} %bitcast.28), calls=%async_computation | async-start | bytes 1048576 | tf_op jit(solution)/shard_map/all_to_all | solution.py:36
  27.2 10.3 %collective-permute-start.1 = (bf16[512,256]{1,0:T(8,128)(2,1)S(1)}, bf16[512,256]{1,0:T(8,128)(2,1)S(1)}, u32[]{:S(2)}, u32[]{:S(2)}) collective-permute-start(bf16[512,256]{1,0:T(8,128)(2,1)S(1)} %pad_maximum_fusion.kv_ref), channel_id=1, source_target_pairs={{0,4},{1,5},{2,6},{3,7},{4,8},{5,9},{6,10},{7,11},{8,12},{9,13},{1... | collective-permute-start | bytes 786440 | tf_op jit(solution)/shard_map/ppermute | solution.py:223
  29.8 10.3 %collective-permute-start.4 = (bf16[512,256]{1,0:T(8,128)(2,1)S(1)}, bf16[512,256]{1,0:T(8,128)(2,1)S(1)}, u32[]{:S(2)}, u32[]{:S(2)}) collective-permute-start(bf16[512,256]{1,0:T(8,128)(2,1)S(1)} %pad_maximum_fusion.kv_ref), channel_id=1, source_target_pairs={{0,28},{1,29},{2,30},{3,31},{4,0},{5,1},{6,2},{7,3},{8,4},{9,5},{1... | collective-permute-start | bytes 786440 | tf_op jit(solution)/shard_map/ppermute | solution.py:224
  37.5 9.8 %collective-permute-start.2 = (bf16[512,256]{1,0:T(8,128)(2,1)S(1)}, bf16[512,256]{1,0:T(8,128)(2,1)S(1)}, u32[]{:S(2)}, u32[]{:S(2)}) collective-permute-start(bf16[512,256]{1,0:T(8,128)(2,1)S(1)} %collective-permute-done.1.refs_2_), channel_id=1, source_target_pairs={{0,4},{1,5},{2,6},{3,7},{4,8},{5,9},{6,10},{7,11},{8,12},{9,13},{1... | collective-permute-start | bytes 786440 | tf_op jit(solution)/shard_map/ppermute | solution.py:228
  40.1 9.2 %collective-permute-start.6 = (bf16[512,256]{1,0:T(8,128)(2,1)S(1)}, bf16[512,256]{1,0:T(8,128)(2,1)S(1)}, u32[]{:S(2)}, u32[]{:S(2)}) collective-permute-start(bf16[512,256]{1,0:T(8,128)(2,1)S(1)} %collective-permute-done.4.refs_2_), channel_id=1, source_target_pairs={{0,28},{1,29},{2,30},{3,31},{4,0},{5,1},{6,2},{7,3},{8,4},{9,5},{1... | collective-permute-start | bytes 786440 | tf_op jit(solution)/shard_map/ppermute | solution.py:230
  47.4 11.3 %collective-permute-start.3 = (bf16[512,256]{1,0:T(8,128)(2,1)S(1)}, bf16[512,256]{1,0:T(8,128)(2,1)S(1)}, u32[]{:S(2)}, u32[]{:S(2)}) collective-permute-start(bf16[512,256]{1,0:T(8,128)(2,1)S(1)} %collective-permute-done.2.refs_3_), channel_id=1, source_target_pairs={{0,4},{1,5},{2,6},{3,7},{4,8},{5,9},{6,10},{7,11},{8,12},{9,13},{1... | collective-permute-start | bytes 786440 | tf_op jit(solution)/shard_map/ppermute | solution.py:228
  49.3 11.3 %collective-permute-start.7 = (bf16[512,256]{1,0:T(8,128)(2,1)S(1)}, bf16[512,256]{1,0:T(8,128)(2,1)S(1)}, u32[]{:S(2)}, u32[]{:S(2)}) collective-permute-start(bf16[512,256]{1,0:T(8,128)(2,1)S(1)} %collective-permute-done.6.refs_2_), channel_id=1, source_target_pairs={{0,28},{1,29},{2,30},{3,31},{4,0},{5,1},{6,2},{7,3},{8,4},{9,5},{1... | collective-permute-start | bytes 786440 | tf_op jit(solution)/shard_map/ppermute | solution.py:230
  58.7 9.5 %collective-permute-start.5 = (bf16[512,256]{1,0:T(8,128)(2,1)S(1)}, bf16[512,256]{1,0:T(8,128)(2,1)S(1)}, u32[]{:S(2)}, u32[]{:S(2)}) collective-permute-start(bf16[512,256]{1,0:T(8,128)(2,1)S(1)} %collective-permute-done.3.refs_3_), channel_id=1, source_target_pairs={{0,4},{1,5},{2,6},{3,7},{4,8},{5,9},{6,10},{7,11},{8,12},{9,13},{1... | collective-permute-start | bytes 786440 | tf_op jit(solution)/shard_map/ppermute | solution.py:228

commit v6 on v5

--- a/solution.py
+++ b/solution.py
@@ -32,6 +32,11 @@
 ]
 
 
+def place_of():
+    me = lax.axis_index("ctx")
+    return me // (NY * NX), lax.rem(me // NX, NY)
+
+
 def exchange(pieces):
     return lax.all_to_all(
         pieces, "ctx", 0, 0, axis_index_groups=X_GROUPS, tiled=True
@@ -72,14 +77,14 @@
     return both[:, :HD], both[:, HD:]
 
 
-def own_kernel(place, x_ref, kv_ref, acc_ref, max_ref, sum_ref, key_scr, value_scr):
+def own_kernel(x_ref, kv_ref, acc_ref, max_ref, sum_ref, key_scr, value_scr):
     value_scr[:, HD:] = jnp.ones((2 * ROWS, HD), jnp.bfloat16)
     key_scr[...] = kv_ref[:, :HD]
     value_scr[:, :HD] = kv_ref[:, HD:]
     shape = (ROWS, 2 * ROWS)
     row = lax.broadcasted_iota(jnp.int32, shape, 0)
     col = lax.broadcasted_iota(jnp.int32, shape, 1)
-    seen = col <= row + place[0] * ROWS
+    seen = col <= row + place_of()[0] * ROWS
 
     def finish(cols, scores):
         scores = jnp.where(seen, scores, NEG)
@@ -93,10 +98,10 @@
 
 def more_kernel(shifts, last, *refs):
     n = len(shifts)
-    place, x_ref, blocks = refs[0], refs[1], refs[2 : 2 + n]
-    acc_in, max_in, sum_in = refs[2 + n : 5 + n]
-    outs, (key_scr, value_scr) = refs[5 + n : -2], refs[-2:]
-    z, y = place[0], place[1]
+    x_ref, blocks = refs[0], refs[1 : 1 + n]
+    acc_in, max_in, sum_in = refs[1 + n : 4 + n]
+    outs, (key_scr, value_scr) = refs[4 + n : -2], refs[-2:]
+    z, y = place_of()
     allowed = []
     for shift in shifts:
         before = (lax.rem(y - shift + NY, NY) < y).astype(jnp.int32)
@@ -141,7 +146,6 @@
 
 
 VMEM = pl.BlockSpec(memory_space=pltpu.VMEM)
-SMEM = pl.BlockSpec(memory_space=pltpu.SMEM)
 STATE = [jax.ShapeDtypeStruct((ROWS, GROUP * HD), jnp.float32)] * 3
 PARAMS = pltpu.CompilerParams(vmem_limit_bytes=32 << 20)
 
@@ -160,55 +164,53 @@
     ]
 
 
-def own_block(place, x, kv):
+def own_block(x, kv):
     return pl.pallas_call(
         own_kernel,
         out_shape=STATE,
-        in_specs=[SMEM, VMEM, VMEM],
+        in_specs=[VMEM, VMEM],
         out_specs=[VMEM] * 3,
         scratch_shapes=scratch(1),
         compiler_params=PARAMS,
         cost_estimate=cost(1),
         name="own_block",
-    )(place, x, kv)
-
-
-def more_blocks(arrived, place, x, state):
+    )(x, kv)
+
+
+def more_blocks(arrived, x, state):
     shifts = tuple(shift for shift, _ in arrived)
     n = len(arrived)
     return pl.pallas_call(
         functools.partial(more_kernel, shifts, False),
         out_shape=STATE,
-        in_specs=[SMEM] + [VMEM] * (n + 4),
+        in_specs=[VMEM] * (n + 4),
         out_specs=[VMEM] * 3,
         scratch_shapes=scratch(n),
-        input_output_aliases={n + 2: 0, n + 3: 1, n + 4: 2},
+        input_output_aliases={n + 1: 0, n + 2: 1, n + 3: 2},
         compiler_params=PARAMS,
         cost_estimate=cost(n),
         name="more_blocks",
-    )(place, x, *[block for _, block in arrived], *state)
-
-
-def last_blocks(arrived, place, x, state):
+    )(x, *[block for _, block in arrived], *state)
+
+
+def last_blocks(arrived, x, state):
     shifts = tuple(shift for shift, _ in arrived)
     n = len(arrived)
     return pl.pallas_call(
         functools.partial(more_kernel, shifts, True),
         out_shape=[jax.ShapeDtypeStruct((ROWS, GROUP * HD), jnp.bfloat16)],
-        in_specs=[SMEM] + [VMEM] * (n + 4),
+        in_specs=[VMEM] * (n + 4),
         out_specs=[VMEM],
         scratch_shapes=scratch(n),
         compiler_params=PARAMS,
         cost_estimate=cost(n),
         name="last_blocks",
-    )(place, x, *[block for _, block in arrived], *state)[0]
+    )(x, *[block for _, block in arrived], *state)[0]
 
 
 def local(queries, keys, values):
     rows = queries.shape[0]
-    me = lax.axis_index("ctx")
-    z, y = me // (NY * NX), (me // NX) % NY
-    place = jnp.stack([z, y]).astype(jnp.int32)
+    z, _ = place_of()
     by_head = jnp.concatenate(
         [keys.reshape(rows, KVH, HD), values.reshape(rows, KVH, HD)], axis=2
     ).transpose(1, 0, 2)
@@ -222,14 +224,14 @@
     got = {}
     got[1] = lax.ppermute(kv, "ctx", ring(1))
     got[-1] = lax.ppermute(kv, "ctx", ring(-1))
-    state = own_block(place, x, kv)
-    for step, shifts in ((1, (1,)), (2, (-1, 2)), (3, (-2, 3, -3))):
+    state = own_block(x, kv)
+    for step, shifts in ((1, (1,)), (2, (-1,)), (3, (2, -2, 3, -3))):
         got[step], state = lax.optimization_barrier((got[step], state))
         got[step + 1] = lax.ppermute(got[step], "ctx", ring(1))
         if step < NY // 2 - 1:
             got[-step - 1] = lax.ppermute(got[-step], "ctx", ring(-1))
-        state = more_blocks([(at, got[at]) for at in shifts], place, x, state)
-    out = last_blocks([(NY // 2, got[NY // 2])], place, x, state)
+        state = more_blocks([(at, got[at]) for at in shifts], x, state)
+    out = last_blocks([(NY // 2, got[NY // 2])], x, state)
     out = exchange(out.reshape(NX, rows, GROUP * HD))
     return out.transpose(1, 0, 2).reshape(rows, QH * HD)
 

time: 83.8 us -> 80.8 us (0.964)
  Pallas kernels: 17.5 us -> 11.7 us
  waiting for transfers between devices: 2.61 us -> 5.07 us
    pallas_call x3, Pallas kernels: 12.7 us -> 8.14 us  [more_blocks(): pl.pallas_call(functools.partial(more_kernel, shifts, False), out_shape=S...]
    ppermute x3, waiting for transfers between devices: 1.82 us -> 4.17 us  [local(): got[step + 1] = lax.ppermute(got[step], 'ctx', ring(1))]
  transfers between devices with their start and end apart: 9 -> 9, of which waited for: 2 -> 4; matrix products, arithmetic and copies ran while one was open for 1% -> 1% of each run, Pallas kernels for 18% -> 12%
where the time goes in v6:
time: 80.8 us; the launch traced here: 80.3 us
  starting transfers between devices  37.4 us (46%)
  blocking collectives  22.3 us (28%)
  Pallas kernels  11.7 us (14%)
  waiting for transfers between devices  5.07 us (6%)
  local copies, waits for them, and re-layouts  3.43 us (4%)
    all_to_all x2, blocking collectives, exchange(): lax.all_to_all(pieces, 'ctx', 0, 0, axis_index_groups=X_GROUPS, tiled=True)  22.3 us
    ppermute x1, starting transfers between devices, local(): other = lax.ppermute(own, 'ctx', Z_SWAP)  10.9 us
    ppermute x2, starting transfers between devices, local(): got[-step - 1] = lax.ppermute(got[-step], 'ctx', ring(-1))  9.6 us
    pallas_call x3, Pallas kernels, more_blocks(): pl.pallas_call(functools.partial(more_kernel, shifts, False), out_shape=S...  8.14 us
    ppermute x3, starting transfers between devices, local(): got[step + 1] = lax.ppermute(got[step], 'ctx', ring(1))  6.4 us
    ppermute x1, starting transfers between devices, local(): got[-1] = lax.ppermute(kv, 'ctx', ring(-1))  4.47 us
    ppermute x3, waiting for transfers between devices, local(): got[step + 1] = lax.ppermute(got[step], 'ctx', ring(1))  4.17 us
    all_to_all x1, starting transfers between devices, exchange(): lax.all_to_all(pieces, 'ctx', 0, 0, axis_index_groups=X_GROUPS, tiled=True)  3.47 us
  transfers between devices with their start and end apart: 9, of which 4 were waited for; matrix products, arithmetic and copies ran while one was open for 1% of the time, Pallas kernels for 12%

profile of v6, /device:TPU:32, one launch (start us, length us, event | category | flops | bytes accessed | tf_op | source)
XLA Modules:
  0.0 80.3 jit_solution(16852551311180146274)
XLA Ops:
  0.0 0.0 copy-start
  0.0 0.8 %copy-done = bf16[64,512]{1,0:T(8,128)(2,1)S(1)} copy-done((bf16[64,512]{1,0:T(8,128)(2,1)S(1)}, bf16[64,512]{1,0:T(8,128)(2,1)}, u32[]{:S(2)}) %copy-start) | copy-done | bytes 65560
  0.8 0.0 copy-start.1
  0.8 0.9 %copy_bitcast_fusion = (bf16[64,4,128]{2,0,1:T(8,128)(2,1)S(1)}, bf16[64,4,128]{2,0,1:T(8,128)(2,1)S(1)}) fusion(bf16[64,512]{1,0:T(8,128)(2,1)S(1)} %copy-done, bf16[64,512]{1,0:T(8,128)(2,1)} %param.5), kind=kLoop, calls=%fused_computation.5 | loop fusion | bytes 262144 | tf_op jit(solution)/shard_map/reshape | solution.py:215
  1.8 10.1 %all_to_all.15 = bf16[4,64,256]{2,1,0:T(8,128)(2,1)S(1)} all-to-all(bf16[4,64,256]{2,1,0:T(8,128)(2,1)S(1)} %maximum_bitcast_fusion), channel_id=1, replica_groups={{0,1,2,3},{4,5,6,7},{8,9,10,11},{12,13,14,15},{16,17,18,19},{20,21,22,2..., dimensions={0} | all-to-all | bytes 262144 | tf_op jit(solution)/shard_map/all_to_all | solution.py:41
  11.9 10.9 %collective-permute-start = (bf16[256,256]{1,0:T(8,128)(2,1)S(1)}, bf16[256,256]{1,0:T(8,128)(2,1)S(1)}, u32[]{:S(2)}, u32[]{:S(2)}) collective-permute-start(bf16[256,256]{1,0:T(8,128)(2,1)S(1)} %bitcast.34), channel_id=1, source_target_pairs={{0,32},{1,33},{2,34},{3,35},{4,36},{5,37},{6,38},{7,39},{8,40},{9,... | collective-permute-start | bytes 393224 | tf_op jit(solution)/shard_map/ppermute | solution.py:218
  22.8 0.0 copy-done.1
  22.8 0.8 %copy.24 = bf16[8,4,8,1024]{3,2,0,1:T(8,128)(2,1)} copy(bf16[8,4,8,1024]{3,2,1,0:T(8,128)(2,1)S(1)} %bitcast.35) | data formatting | bytes 1048576 | tf_op jit(solution)/shard_map/reshape | solution.py:219
  23.6 3.5 %all-to-all-start = ((bf16[4,64,1024]{2,1,0:T(8,128)(2,1)}), bf16[4,64,1024]{2,1,0:T(8,128)(2,1)S(1)}, u32[]{:S(2)}, u32[]{:S(2)}) async-start(bf16[4,64,1024]{2,1,0:T(8,128)(2,1)} %bitcast.26), calls=%async_computation | async-start | bytes 1048576 | tf_op jit(solution)/shard_map/all_to_all | solution.py:41
  27.1 0.0 collective-permute-done
  27.2 2.6 %collective-permute-start.1 = (bf16[512,256]{1,0:T(8,128)(2,1)S(1)}, bf16[512,256]{1,0:T(8,128)(2,1)S(1)}, u32[]{:S(2)}, u32[]{:S(2)}) collective-permute-start(bf16[512,256]{1,0:T(8,128)(2,1)S(1)} %pad_maximum_fusion.kv_ref), channel_id=1, source_target_pairs={{0,4},{1,5},{2,6},{3,7},{4,8},{5,9},{6,10},{7,11},{8,12},{9,13},{1... | collective-permute-start | bytes 786440 | tf_op jit(solution)/shard_map/ppermute | solution.py:225
  29.8 4.5 %collective-permute-start.4 = (bf16[512,256]{1,0:T(8,128)(2,1)S(1)}, bf16[512,256]{1,0:T(8,128)(2,1)S(1)}, u32[]{:S(2)}, u32[]{:S(2)}) collective-permute-start(bf16[512,256]{1,0:T(8,128)(2,1)S(1)} %pad_maximum_fusion.kv_ref), channel_id=1, source_target_pairs={{0,28},{1,29},{2,30},{3,31},{4,0},{5,1},{6,2},{7,3},{8,4},{9,5},{1... | collective-permute-start | bytes 786440 | tf_op jit(solution)/shard_map/ppermute | solution.py:226
  34.3 0.9 %all-to-all-done = bf16[4,64,1024]{2,1,0:T(8,128)(2,1)S(1)} async-done(((bf16[4,64,1024]{2,1,0:T(8,128)(2,1)}), bf16[4,64,1024]{2,1,0:T(8,128)(2,1)S(1)}, u32[]{:S(2)}, u32[]{:S(2)}) %all-to-all-start) | async-done | bytes 524320 | tf_op jit(solution)/shard_map/all_to_all | solution.py:41
  35.1 1.8 %own_block.1 = (f32[256,1024]{1,0:T(8,128)S(1)}, f32[256,1024]{1,0:T(8,128)S(1)}, f32[256,1024]{1,0:T(8,128)S(1)}) custom-call(bf16[256,1024]{1,0:T(8,128)(2,1)S(1)} %bitcast.27, bf16[512,256]{1,0:T(8,128)(2,1)S(1)} %pad_maximum_fusion.kv_ref), custom_call_target="tpu_custom_call" | custom-call | flops 536870912 | bytes 8388608 | tf_op jit(solution)/shard_map/own_block/pallas_call | solution.py:168
  37.0 0.0 collective-permute-done.1.refs_1_
  37.0 2.6 %collective-permute-start.2 = (bf16[512,256]{1,0:T(8,128)(2,1)S(1)}, bf16[512,256]{1,0:T(8,128)(2,1)S(1)}, u32[]{:S(2)}, u32[]{:S(2)}) collective-permute-start(bf16[512,256]{1,0:T(8,128)(2,1)S(1)} %collective-permute-done.1.refs_1_), channel_id=1, source_target_pairs={{0,4},{1,5},{2,6},{3,7},{4,8},{5,9},{6,10},{7,11},{8,12},{9,13},{1... | collective-permute-start | bytes 786440 | tf_op jit(solution)/shard_map/ppermute | solution.py:230
  39.6 0.0 collective-permute-done.4.refs_1_
  39.6 4.5 %collective-permute-start.6 = (bf16[512,256]{1,0:T(8,128)(2,1)S(1)}, bf16[512,256]{1,0:T(8,128)(2,1)S(1)}, u32[]{:S(2)}, u32[]{:S(2)}) collective-permute-start(bf16[512,256]{1,0:T(8,128)(2,1)S(1)} %collective-permute-done.4.refs_1_), channel_id=1, source_target_pairs={{0,28},{1,29},{2,30},{3,31},{4,0},{5,1},{6,2},{7,3},{8,4},{9,5},{1... | collective-permute-start | bytes 786440 | tf_op jit(solution)/shard_map/ppermute | solution.py:232
  44.1 2.1 %more_blocks.3 = (f32[256,1024]{1,0:T(8,128)S(1)}, f32[256,1024]{1,0:T(8,128)S(1)}, f32[256,1024]{1,0:T(8,128)S(1)}) custom-call(bf16[256,1024]{1,0:T(8,128)(2,1)S(1)} %bitcast.28, bf16[512,256]{1,0:T(8,128)(2,1)S(1)} %collective-permute-done.1.refs_1_, ...), custom_call_target="tpu_custom_call", output_to_operand_aliasing={{0}: (2, {}), {1}: (3, {}), {2}: (4, {})} | custom-call | flops 536870912 | bytes 8388608 | tf_op jit(solution)/shard_map/more_blocks/pallas_call | solution.py:183
  46.2 0.3 collective-permute-done.2.refs_1_
  46.5 1.9 %collective-permute-start.3 = (bf16[512,256]{1,0:T(8,128)(2,1)S(1)}, bf16[512,256]{1,0:T(8,128)(2,1)S(1)}, u32[]{:S(2)}, u32[]{:S(2)}) collective-permute-start(bf16[512,256]{1,0:T(8,128)(2,1)S(1)} %collective-permute-done.2.refs_1_), channel_id=1, source_target_pairs={{0,4},{1,5},{2,6},{3,7},{4,8},{5,9},{6,10},{7,11},{8,12},{9,13},{1... | collective-permute-start | bytes 786440 | tf_op jit(solution)/shard_map/ppermute | solution.py:230
  48.4 0.0 collective-permute-done.6.refs_2_
  48.4 5.1 %collective-permute-start.7 = (bf16[512,256]{1,0:T(8,128)(2,1)S(1)}, bf16[512,256]{1,0:T(8,128)(2,1)S(1)}, u32[]{:S(2)}, u32[]{:S(2)}) collective-permute-start(bf16[512,256]{1,0:T(8,128)(2,1)S(1)} %collective-permute-done.6.refs_2_), channel_id=1, source_target_pairs={{0,28},{1,29},{2,30},{3,31},{4,0},{5,1},{6,2},{7,3},{8,4},{9,5},{1... | collective-permute-start | bytes 786440 | tf_op jit(solution)/shard_map/ppermute | solution.py:232
  53.6 2.4 %collective-permute-done.3.refs_3_ = bf16[512,256]{1,0:T(8,128)(2,1)S(1)} collective-permute-done((bf16[512,256]{1,0:T(8,128)(2,1)S(1)}, bf16[512,256]{1,0:T(8,128)(2,1)S(1)}, u32[]{:S(2)}, u32[]{:S(2)}) %collective-permute-start.3) | collective-permute-done | bytes 262176 | tf_op jit(solution)/shard_map/ppermute | solution.py:230
  55.9 1.9 %collective-permute-start.5 = (bf16[512,256]{1,0:T(8,128)(2,1)S(1)}, bf16[512,256]{1,0:T(8,128)(2,1)S(1)}, u32[]{:S(2)}, u32[]{:S(2)}) collective-permute-start(bf16[512,256]{1,0:T(8,128)(2,1)S(1)} %collective-permute-done.3.refs_3_), channel_id=1, source_target_pairs={{0,4},{1,5},{2,6},{3,7},{4,8},{5,9},{6,10},{7,11},{8,12},{9,13},{1... | collective-permute-start | bytes 786440 | tf_op jit(solution)/shard_map/ppermute | solution.py:230
  57.9 0.0 collective-permute-done.7.refs_4_
  57.9 6.0 %more_blocks.5 = (f32[256,1024]{1,0:T(8,128)S(1)}, f32[256,1024]{1,0:T(8,128)S(1)}, f32[256,1024]{1,0:T(8,128)S(1)}) custom-call(bf16[256,1024]{1,0:T(8,128)(2,1)S(1)} %bitcast.30, bf16[512,256]{1,0:T(8,128)(2,1)S(1)} %collective-permute-done.2.refs_1_, ...), custom_call_target="tpu_custom_call", output_to_operand_aliasing={{0}: (5, {}), {1}: (6, {}), {2}: (7, {})} | custom-call | flops 2147483648 | bytes 8388608 | tf_op jit(solution)/shard_map/more_blocks/pallas_call | solution.py:183
  63.9 1.5 %collective-permute-done.5.refs_1_ = bf16[512,256]{1,0:T(8,128)(2,1)S(1)} collective-permute-done((bf16[512,256]{1,0:T(8,128)(2,1)S(1)}, bf16[512,256]{1,0:T(8,128)(2,1)S(1)}, u32[]{:S(2)}, u32[]{:S(2)}) %collective-permute-start.5) | collective-permute-done | bytes 262176 | tf_op jit(solution)/shard_map/ppermute | solution.py:230
  65.4 1.8 %last_blocks.1 = bf16[256,1024]{1,0:T(8,128)(2,1)S(1)} custom-call(bf16[256,1024]{1,0:T(8,128)(2,1)S(1)} %bitcast.31, bf16[512,256]{1,0:T(8,128)(2,1)S(1)} %collective-permute-done.5.refs_1_, f32[256,1024]{1,0:T(8,128)S(1)} %get-tuple-element.50.refs_2_, f32[256,1024]{1,0:T(8,128)S(1)} %get-tuple-element.51.refs_3_, f32[256,1024]{1,0:T(8,128)S(1)} %get-tuple-element.52.refs_4_), custom_call_target="tpu_custom_call" | custom-call | flops 536870912 | bytes 8388608 | tf_op jit(solution)/shard_map/last_blocks/pallas_call | solution.py:199
  67.2 12.3 %all_to_all.16 = bf16[4,64,1024]{2,1,0:T(8,128)(2,1)S(1)} all-to-all(bf16[4,64,1024]{2,1,0:T(8,128)(2,1)S(1)} %bitcast.32), channel_id=1, replica_groups={{0,1,2,3},{4,5,6,7},{8,9,10,11},{12,13,14,15},{16,17,18,19},{20,21,22,2..., dimensions={0} | all-to-all | bytes 1048576 | tf_op jit(solution)/shard_map/all_to_all | solution.py:41
  79.5 0.8 %copy.20 = bf16[4,8,8,1024]{3,2,0,1:T(8,128)(2,1)} copy(bf16[4,8,8,1024]{3,2,1,0:T(8,128)(2,1)S(1)} %bitcast.33) | data formatting | bytes 1048576 | tf_op jit(solution)/shard_map/reshape | solution.py:236
  (4 shorter events, 0.1 us)
Async XLA Ops:
  0.0 0.8 %copy-start = (bf16[64,512]{1,0:T(8,128)(2,1)S(1)}, bf16[64,512]{1,0:T(8,128)(2,1)}, u32[]{:S(2)}) copy-start(bf16[64,512]{1,0:T(8,128)(2,1)} %param.4) | copy-start | bytes 196612
  0.8 21.9 %copy-start.1 = (bf16[64,4096]{1,0:T(8,128)(2,1)S(1)}, bf16[64,4096]{1,0:T(8,128)(2,1)}, u32[]{:S(2)}) copy-start(bf16[64,4096]{1,0:T(8,128)(2,1)} %param.3) | copy-start | bytes 1572868
  11.9 15.3 %collective-permute-start = (bf16[256,256]{1,0:T(8,128)(2,1)S(1)}, bf16[256,256]{1,0:T(8,128)(2,1)S(1)}, u32[]{:S(2)}, u32[]{:S(2)}) collective-permute-start(bf16[256,256]{1,0:T(8,128)(2,1)S(1)} %bitcast.34), channel_id=1, source_target_pairs={{0,32},{1,33},{2,34},{3,35},{4,36},{5,37},{6,38},{7,39},{8,40},{9,... | collective-permute-start | bytes 393224 | tf_op jit(solution)/shard_map/ppermute | solution.py:218
  23.6 11.5 %all-to-all-start = ((bf16[4,64,1024]{2,1,0:T(8,128)(2,1)}), bf16[4,64,1024]{2,1,0:T(8,128)(2,1)S(1)}, u32[]{:S(2)}, u32[]{:S(2)}) async-start(bf16[4,64,1024]{2,1,0:T(8,128)(2,1)} %bitcast.26), calls=%async_computation | async-start | bytes 1048576 | tf_op jit(solution)/shard_map/all_to_all | solution.py:41
  27.2 9.8 %collective-permute-start.1 = (bf16[512,256]{1,0:T(8,128)(2,1)S(1)}, bf16[512,256]{1,0:T(8,128)(2,1)S(1)}, u32[]{:S(2)}, u32[]{:S(2)}) collective-permute-start(bf16[512,256]{1,0:T(8,128)(2,1)S(1)} %pad_maximum_fusion.kv_ref), channel_id=1, source_target_pairs={{0,4},{1,5},{2,6},{3,7},{4,8},{5,9},{6,10},{7,11},{8,12},{9,13},{1... | collective-permute-start | bytes 786440 | tf_op jit(solution)/shard_map/ppermute | solution.py:225
  29.8 9.8 %collective-permute-start.4 = (bf16[512,256]{1,0:T(8,128)(2,1)S(1)}, bf16[512,256]{1,0:T(8,128)(2,1)S(1)}, u32[]{:S(2)}, u32[]{:S(2)}) collective-permute-start(bf16[512,256]{1,0:T(8,128)(2,1)S(1)} %pad_maximum_fusion.kv_ref), channel_id=1, source_target_pairs={{0,28},{1,29},{2,30},{3,31},{4,0},{5,1},{6,2},{7,3},{8,4},{9,5},{1... | collective-permute-start | bytes 786440 | tf_op jit(solution)/shard_map/ppermute | solution.py:226
  37.0 9.5 %collective-permute-start.2 = (bf16[512,256]{1,0:T(8,128)(2,1)S(1)}, bf16[512,256]{1,0:T(8,128)(2,1)S(1)}, u32[]{:S(2)}, u32[]{:S(2)}) collective-permute-start(bf16[512,256]{1,0:T(8,128)(2,1)S(1)} %collective-permute-done.1.refs_1_), channel_id=1, source_target_pairs={{0,4},{1,5},{2,6},{3,7},{4,8},{5,9},{6,10},{7,11},{8,12},{9,13},{1... | collective-permute-start | bytes 786440 | tf_op jit(solution)/shard_map/ppermute | solution.py:230
  39.6 8.8 %collective-permute-start.6 = (bf16[512,256]{1,0:T(8,128)(2,1)S(1)}, bf16[512,256]{1,0:T(8,128)(2,1)S(1)}, u32[]{:S(2)}, u32[]{:S(2)}) collective-permute-start(bf16[512,256]{1,0:T(8,128)(2,1)S(1)} %collective-permute-done.4.refs_1_), channel_id=1, source_target_pairs={{0,28},{1,29},{2,30},{3,31},{4,0},{5,1},{6,2},{7,3},{8,4},{9,5},{1... | collective-permute-start | bytes 786440 | tf_op jit(solution)/shard_map/ppermute | solution.py:232
  46.5 9.5 %collective-permute-start.3 = (bf16[512,256]{1,0:T(8,128)(2,1)S(1)}, bf16[512,256]{1,0:T(8,128)(2,1)S(1)}, u32[]{:S(2)}, u32[]{:S(2)}) collective-permute-start(bf16[512,256]{1,0:T(8,128)(2,1)S(1)} %collective-permute-done.2.refs_1_), channel_id=1, source_target_pairs={{0,4},{1,5},{2,6},{3,7},{4,8},{5,9},{6,10},{7,11},{8,12},{9,13},{1... | collective-permute-start | bytes 786440 | tf_op jit(solution)/shard_map/ppermute | solution.py:230
  48.4 9.5 %collective-permute-start.7 = (bf16[512,256]{1,0:T(8,128)(2,1)S(1)}, bf16[512,256]{1,0:T(8,128)(2,1)S(1)}, u32[]{:S(2)}, u32[]{:S(2)}) collective-permute-start(bf16[512,256]{1,0:T(8,128)(2,1)S(1)} %collective-permute-done.6.refs_2_), channel_id=1, source_target_pairs={{0,28},{1,29},{2,30},{3,31},{4,0},{5,1},{6,2},{7,3},{8,4},{9,5},{1... | collective-permute-start | bytes 786440 | tf_op jit(solution)/shard_map/ppermute | solution.py:232
  55.9 9.5 %collective-permute-start.5 = (bf16[512,256]{1,0:T(8,128)(2,1)S(1)}, bf16[512,256]{1,0:T(8,128)(2,1)S(1)}, u32[]{:S(2)}, u32[]{:S(2)}) collective-permute-start(bf16[512,256]{1,0:T(8,128)(2,1)S(1)} %collective-permute-done.3.refs_3_), channel_id=1, source_target_pairs={{0,4},{1,5},{2,6},{3,7},{4,8},{5,9},{6,10},{7,11},{8,12},{9,13},{1... | collective-permute-start | bytes 786440 | tf_op jit(solution)/shard_map/ppermute | solution.py:230

commit v7 on v6

v7 whole, which is shorter than its diff:
```python
import functools
import math

import jax
import jax.numpy as jnp
from jax import lax
from jax.experimental import pallas as pl
from jax.experimental.pallas import tpu as pltpu
from jax.sharding import PartitionSpec as P

QH = 32
KVH = 4
HD = 128
GROUP = QH // KVH
NZ, NY, NX = 2, 8, 4
ROWS = 256
SCALE = math.log2(math.e) / math.sqrt(HD)
NEG = -1e30
QK = (((1,), (1,)), ((), ()))


def index(z, y, x):
    return z * (NY * NX) + y * NX + x


X_GROUPS = [[index(z, y, x) for x in range(NX)] for z in range(NZ) for y in range(NY)]
Z_SWAP = [
    (index(z, y, x), index(1 - z, y, x))
    for z in range(NZ)
    for y in range(NY)
    for x in range(NX)
]


def place_of():
    me = lax.axis_index("ctx")
    return me // (NY * NX), lax.rem(me // NX, NY)


def exchange(pieces):
    return lax.all_to_all(
        pieces, "ctx", 0, 0, axis_index_groups=X_GROUPS, tiled=True
    )


def ring(direction, step, halves=(0, 1)):
    pairs = []
    for z in halves:
        for y in range(NY):
            origin = (y - direction * (step - 1)) % NY
            last = NY // 2 if direction == 1 else NY // 2 - 1
            reached = [(origin + direction * k) % NY for k in range(step, last + 1)]
            if z == 1 or any(origin < there for there in reached):
                target = (y + direction) % NY
                pairs += [(index(z, y, x), index(z, target, x)) for x in range(NX)]
    return pairs


def per_head(n, x_ref, key_scr, finish):
    def scores_of(j):
        return lax.dot_general(
            x_ref[:, j * HD : (j + 1) * HD],
            key_scr[:n, :],
            QK,
            preferred_element_type=jnp.float32,
        )

    scores = scores_of(0)
    for j in range(GROUP):
        ahead = scores_of(j + 1) if j + 1 < GROUP else None
        finish(slice(j * HD, (j + 1) * HD), scores)
        scores = ahead


def weigh(n, weights, value_scr):
    both = jnp.dot(
        weights.astype(jnp.bfloat16),
        value_scr[:n, :],
        preferred_element_type=jnp.float32,
    )
    return both[:, :HD], both[:, HD:]


def own_kernel(x_ref, kv_ref, acc_ref, max_ref, sum_ref, key_scr, value_scr):
    value_scr[:, HD:] = jnp.ones((2 * ROWS, HD), jnp.bfloat16)
    key_scr[...] = kv_ref[:, :HD]
    value_scr[:, :HD] = kv_ref[:, HD:]
    shape = (ROWS, 2 * ROWS)
    row = lax.broadcasted_iota(jnp.int32, shape, 0)
    col = lax.broadcasted_iota(jnp.int32, shape, 1)
    seen = col <= row + place_of()[0] * ROWS

    def finish(cols, scores):
        scores = jnp.where(seen, scores, NEG)
        peak = jnp.max(scores, axis=1, keepdims=True) * SCALE
        weights = jnp.exp2(scores * SCALE - peak)
        acc_ref[:, cols], sum_ref[:, cols] = weigh(2 * ROWS, weights, value_scr)
        max_ref[:, cols] = jnp.broadcast_to(peak, (ROWS, HD))

    per_head(2 * ROWS, x_ref, key_scr, finish)


def more_kernel(shifts, last, *refs):
    n = len(shifts)
    x_ref, firsts, seconds = refs[0], refs[1 : 1 + n], refs[1 + n : 1 + 2 * n]
    acc_in, max_in, sum_in = refs[1 + 2 * n : 4 + 2 * n]
    outs, (key_scr, value_scr) = refs[4 + 2 * n : -2], refs[-2:]
    z, y = place_of()
    before = [lax.rem(y - shift + NY, NY) < y for shift in shifts]

    def put(c, seen, key, value, safe):
        rows = slice(c * ROWS, (c + 1) * ROWS)
        zeros, ones = jnp.zeros_like(value), jnp.ones_like(value)
        key_scr[rows, :] = key if seen is None else jnp.where(seen, key, safe)
        value_scr[rows, :HD] = value if seen is None else jnp.where(seen, value, zeros)
        value_scr[rows, HD:] = ones if seen is None else jnp.where(seen, ones, zeros)

    def attend(keys):
        def finish(cols, scores):
            old = max_in[:, cols]
            peak = jnp.maximum(old, jnp.max(scores, axis=1, keepdims=True) * SCALE)
            keep = jnp.exp2(old - peak)
            weights = jnp.exp2(scores * SCALE - jnp.tile(peak, (1, keys // HD)))
            acc, total = weigh(keys, weights, value_scr)
            acc = acc_in[:, cols] * keep + acc
            total = sum_in[:, cols] * keep + total
            if last:
                outs[0][:, cols] = (acc / total).astype(jnp.bfloat16)
            else:
                outs[0][:, cols], outs[1][:, cols], outs[2][:, cols] = acc, peak, total

        per_head(keys, x_ref, key_scr, finish)

    @pl.when(z == 1)
    def _():
        for b in range(n):
            key = seconds[b][:ROWS, :HD]
            put(2 * b, None, key, seconds[b][:ROWS, HD:], None)
            put(2 * b + 1, before[b], seconds[b][ROWS:, :HD], seconds[b][ROWS:, HD:], key)
        attend(2 * ROWS * n)

    some = functools.reduce(jnp.logical_or, before)

    @pl.when(jnp.logical_and(z == 0, some))
    def _():
        safe = firsts[n - 1][:ROWS, :HD]
        for b in range(n - 2, -1, -1):
            safe = jnp.where(before[b], firsts[b][:ROWS, :HD], safe)
        for b in range(n):
            put(b, before[b], firsts[b][:ROWS, :HD], firsts[b][:ROWS, HD:], safe)
        attend(ROWS * n)

    if last:

        @pl.when(jnp.logical_and(z == 0, jnp.logical_not(some)))
        def _():
            outs[0][...] = (acc_in[...] / sum_in[...]).astype(jnp.bfloat16)


VMEM = pl.BlockSpec(memory_space=pltpu.VMEM)
STATE = [jax.ShapeDtypeStruct((ROWS, GROUP * HD), jnp.float32)] * 3
PARAMS = pltpu.CompilerParams(vmem_limit_bytes=32 << 20)


def cost(blocks):
    pairs = ROWS * GROUP * 2 * ROWS * blocks
    return pl.CostEstimate(
        flops=4 * pairs * HD, bytes_accessed=8 << 20, transcendentals=pairs
    )


def scratch(blocks):
    return [
        pltpu.VMEM((2 * ROWS * blocks, HD), jnp.bfloat16),
        pltpu.VMEM((2 * ROWS * blocks, 2 * HD), jnp.bfloat16),
    ]


def own_block(x, kv):
    return pl.pallas_call(
        own_kernel,
        out_shape=STATE,
        in_specs=[VMEM, VMEM],
        out_specs=[VMEM] * 3,
        scratch_shapes=scratch(1),
        compiler_params=PARAMS,
        cost_estimate=cost(1),
        name="own_block",
    )(x, kv)


def absorb(arrived, x, state, last=False):
    shifts, firsts, seconds = zip(*arrived)
    n = len(shifts)
    at = 1 + 2 * n
    out = [jax.ShapeDtypeStruct((ROWS, GROUP * HD), jnp.bfloat16)] if last else STATE
    return pl.pallas_call(
        functools.partial(more_kernel, shifts, last),
        out_shape=out,
        in_specs=[VMEM] * (2 * n + 4),
        out_specs=[VMEM] * len(out),
        scratch_shapes=scratch(n),
        input_output_aliases={} if last else {at: 0, at + 1: 1, at + 2: 2},
        compiler_params=PARAMS,
        cost_estimate=cost(n),
        name="last_blocks" if last else "more_blocks",
    )(x, *firsts, *seconds, *state)


def local(queries, keys, values):
    rows = queries.shape[0]
    z, _ = place_of()
    by_head = jnp.concatenate(
        [keys.reshape(rows, KVH, HD), values.reshape(rows, KVH, HD)], axis=2
    ).transpose(1, 0, 2)
    own = exchange(by_head).reshape(ROWS, 2 * HD)
    other = lax.ppermute(own, "ctx", Z_SWAP)
    x = exchange(queries.reshape(rows, KVH, GROUP * HD).transpose(1, 0, 2))
    x = x.reshape(ROWS, GROUP * HD)
    kv = jnp.concatenate(
        [jnp.where(z == 0, own, other), jnp.where(z == 0, other, own)], axis=0
    )
    got = {}
    got[1] = lax.ppermute(kv, "ctx", ring(1, 1))
    got[-1] = lax.ppermute(kv, "ctx", ring(-1, 1))
    state = own_block(x, kv)
    for step, shifts in ((1, (1,)), (2, (-1,)), (3, (2, -2, 3, -3))):
        got[step], state = lax.optimization_barrier((got[step], state))
        if step < NY // 2 - 1:
            got[step + 1] = lax.ppermute(got[step], "ctx", ring(1, step + 1))
            got[-step - 1] = lax.ppermute(got[-step], "ctx", ring(-1, step + 1))
        else:
            last = (
                step + 1,
                lax.ppermute(got[step][:ROWS], "ctx", ring(1, step + 1, (0,))),
                lax.ppermute(got[step], "ctx", ring(1, step + 1, (1,))),
            )
        state = absorb([(at, got[at], got[at]) for at in shifts], x, state)
    (out,) = absorb([last], x, state, last=True)
    out = exchange(out.reshape(NX, rows, GROUP * HD))
    return out.transpose(1, 0, 2).reshape(rows, QH * HD)


def solution(mesh):
    spec = P(("dp", "ctx"), None)
    return jax.shard_map(
        local, mesh=mesh, in_specs=(spec,) * 3, out_specs=spec, check_vma=False
    )
```

time: 80.8 us -> 79.4 us (0.983)
  waiting for transfers between devices: 5.07 us -> 18.6 us
  starting transfers between devices: 37.4 us -> 26.1 us
  Pallas kernels: 11.7 us -> 8.21 us
    ppermute x7 -> x8, starting transfers between devices: 23.1 us -> 11.7 us  [the longest x2 4.5 us: local(): got[step + 1] = lax.ppermute(got[step], 'ctx', ring(1, step + 1))]
    ppermute x7 -> x8, waiting for transfers between devices: 4.18 us -> 13.9 us  [the longest x2 11.4 us: local(): got[step + 1] = lax.ppermute(got[step], 'ctx', ring(1, step + 1))]
    all_to_all x1, waiting for transfers between devices: 0.89 us -> 4.68 us  [exchange(): lax.all_to_all(pieces, 'ctx', 0, 0, axis_index_groups=X_GROUPS, tiled=True)]
    pallas_call x4, Pallas kernels: 9.91 us -> 6.37 us  [absorb(): pl.pallas_call(functools.partial(more_kernel, shifts, last), out_shape=ou...]
  transfers between devices with their start and end apart: 9 -> 10, of which waited for: 4 -> 4; matrix products, arithmetic and copies ran while one was open for 1% -> 1% of each run, Pallas kernels for 12% -> 9%
where the time goes in v7:
time: 79.4 us; the launch traced here: 79 us
  starting transfers between devices  26.1 us (33%)
  blocking collectives  22.3 us (28%)
  waiting for transfers between devices  18.6 us (23%)
  Pallas kernels  8.21 us (10%)
  local copies, waits for them, and re-layouts  3.44 us (4%)
    all_to_all x2, blocking collectives, exchange(): lax.all_to_all(pieces, 'ctx', 0, 0, axis_index_groups=X_GROUPS, tiled=True)  22.3 us
    ppermute x2, waiting for transfers between devices, local(): got[step + 1] = lax.ppermute(got[step], 'ctx', ring(1, step + 1))  11.4 us
    ppermute x1, starting transfers between devices, local(): other = lax.ppermute(own, 'ctx', Z_SWAP)  10.9 us
    pallas_call x4, Pallas kernels, absorb(): pl.pallas_call(functools.partial(more_kernel, shifts, last), out_shape=ou...  6.37 us
    all_to_all x1, waiting for transfers between devices, exchange(): lax.all_to_all(pieces, 'ctx', 0, 0, axis_index_groups=X_GROUPS, tiled=True)  4.68 us
    ppermute x2, starting transfers between devices, local(): got[step + 1] = lax.ppermute(got[step], 'ctx', ring(1, step + 1))  4.5 us
    all_to_all x1, starting transfers between devices, exchange(): lax.all_to_all(pieces, 'ctx', 0, 0, axis_index_groups=X_GROUPS, tiled=True)  3.47 us
    ppermute x1, starting transfers between devices, local(): got[1] = lax.ppermute(kv, 'ctx', ring(1, 1))  2.59 us
  transfers between devices with their start and end apart: 10, of which 4 were waited for; matrix products, arithmetic and copies ran while one was open for 1% of the time, Pallas kernels for 9%

profile of v7, /device:TPU:32, one launch (start us, length us, event | category | flops | bytes accessed | tf_op | source)
XLA Modules:
  0.0 79.0 jit_solution(11894101671801435172)
XLA Ops:
  0.0 0.0 copy-start
  0.0 0.8 %copy-done = bf16[64,512]{1,0:T(8,128)(2,1)S(1)} copy-done((bf16[64,512]{1,0:T(8,128)(2,1)S(1)}, bf16[64,512]{1,0:T(8,128)(2,1)}, u32[]{:S(2)}) %copy-start) | copy-done | bytes 65560
  0.8 0.0 copy-start.1
  0.8 0.9 %copy_bitcast_fusion = (bf16[64,4,128]{2,0,1:T(8,128)(2,1)S(1)}, bf16[64,4,128]{2,0,1:T(8,128)(2,1)S(1)}) fusion(bf16[64,512]{1,0:T(8,128)(2,1)S(1)} %copy-done, bf16[64,512]{1,0:T(8,128)(2,1)} %param.5), kind=kLoop, calls=%fused_computation.5 | loop fusion | bytes 262144 | tf_op jit(solution)/shard_map/reshape | solution.py:214
  1.8 10.1 %all_to_all.15 = bf16[4,64,256]{2,1,0:T(8,128)(2,1)S(1)} all-to-all(bf16[4,64,256]{2,1,0:T(8,128)(2,1)S(1)} %maximum_bitcast_fusion), channel_id=1, replica_groups={{0,1,2,3},{4,5,6,7},{8,9,10,11},{12,13,14,15},{16,17,18,19},{20,21,22,2..., dimensions={0} | all-to-all | bytes 262144 | tf_op jit(solution)/shard_map/all_to_all | solution.py:41
  11.9 10.9 %collective-permute-start = (bf16[256,256]{1,0:T(8,128)(2,1)S(1)}, bf16[256,256]{1,0:T(8,128)(2,1)S(1)}, u32[]{:S(2)}, u32[]{:S(2)}) collective-permute-start(bf16[256,256]{1,0:T(8,128)(2,1)S(1)} %bitcast.34), channel_id=1, source_target_pairs={{0,32},{1,33},{2,34},{3,35},{4,36},{5,37},{6,38},{7,39},{8,40},{9,... | collective-permute-start | bytes 393224 | tf_op jit(solution)/shard_map/ppermute | solution.py:217
  22.8 0.0 copy-done.1
  22.8 0.8 %copy.24 = bf16[8,4,8,1024]{3,2,0,1:T(8,128)(2,1)} copy(bf16[8,4,8,1024]{3,2,1,0:T(8,128)(2,1)S(1)} %bitcast.35) | data formatting | bytes 1048576 | tf_op jit(solution)/shard_map/reshape | solution.py:218
  23.6 3.5 %all-to-all-start = ((bf16[4,64,1024]{2,1,0:T(8,128)(2,1)}), bf16[4,64,1024]{2,1,0:T(8,128)(2,1)S(1)}, u32[]{:S(2)}, u32[]{:S(2)}) async-start(bf16[4,64,1024]{2,1,0:T(8,128)(2,1)} %bitcast.26), calls=%async_computation | async-start | bytes 1048576 | tf_op jit(solution)/shard_map/all_to_all | solution.py:41
  27.1 0.0 collective-permute-done
  27.2 2.6 %collective-permute-start.1 = (bf16[512,256]{1,0:T(8,128)(2,1)S(1)}, bf16[512,256]{1,0:T(8,128)(2,1)S(1)}, u32[]{:S(2)}, u32[]{:S(2)}) collective-permute-start(bf16[512,256]{1,0:T(8,128)(2,1)S(1)} %pad_maximum_fusion.kv_ref), channel_id=1, source_target_pairs={{0,4},{1,5},{2,6},{3,7},{4,8},{5,9},{6,10},{7,11},{8,12},{9,13},{1... | collective-permute-start | bytes 786440 | tf_op jit(solution)/shard_map/ppermute | solution.py:224
  29.8 0.7 collective-permute-start.4
  30.5 4.7 %all-to-all-done = bf16[4,64,1024]{2,1,0:T(8,128)(2,1)S(1)} async-done(((bf16[4,64,1024]{2,1,0:T(8,128)(2,1)}), bf16[4,64,1024]{2,1,0:T(8,128)(2,1)S(1)}, u32[]{:S(2)}, u32[]{:S(2)}) %all-to-all-start) | async-done | bytes 524320 | tf_op jit(solution)/shard_map/all_to_all | solution.py:41
  35.1 1.8 %own_block.1 = (f32[256,1024]{1,0:T(8,128)S(1)}, f32[256,1024]{1,0:T(8,128)S(1)}, f32[256,1024]{1,0:T(8,128)S(1)}) custom-call(bf16[256,1024]{1,0:T(8,128)(2,1)S(1)} %bitcast.27, bf16[512,256]{1,0:T(8,128)(2,1)S(1)} %pad_maximum_fusion.kv_ref), custom_call_target="tpu_custom_call" | custom-call | flops 536870912 | bytes 8388608 | tf_op jit(solution)/shard_map/own_block/pallas_call | solution.py:180
  37.0 0.0 collective-permute-done.1.refs_1_.refs_2_
  37.0 2.6 %collective-permute-start.2 = (bf16[512,256]{1,0:T(8,128)(2,1)S(1)}, bf16[512,256]{1,0:T(8,128)(2,1)S(1)}, u32[]{:S(2)}, u32[]{:S(2)}) collective-permute-start(bf16[512,256]{1,0:T(8,128)(2,1)S(1)} %collective-permute-done.1.refs_1_.refs_2_), channel_id=1, source_target_pairs={{4,8},{5,9},{6,10},{7,11},{8,12},{9,13},{10,14},{11,15},{12,16},{1... | collective-permute-start | bytes 786440 | tf_op jit(solution)/shard_map/ppermute | solution.py:230
  39.6 0.0 collective-permute-done.4.refs_1_.refs_2_
  39.6 0.7 collective-permute-start.7
  40.3 1.6 %more_blocks.3 = (f32[256,1024]{1,0:T(8,128)S(1)}, f32[256,1024]{1,0:T(8,128)S(1)}, f32[256,1024]{1,0:T(8,128)S(1)}) custom-call(bf16[256,1024]{1,0:T(8,128)(2,1)S(1)} %bitcast.28, bf16[512,256]{1,0:T(8,128)(2,1)S(1)} %collective-permute-done.1.refs_1_.refs_2_, ...), custom_call_target="tpu_custom_call", output_to_operand_aliasing={{0}: (3, {}), {1}: (4, {}), {2}: (5, {})} | custom-call | flops 536870912 | bytes 8388608 | tf_op jit(solution)/shard_map/more_blocks/pallas_call | solution.py:197
  41.9 4.6 %collective-permute-done.2.refs_1_.refs_5_ = bf16[512,256]{1,0:T(8,128)(2,1)S(1)} collective-permute-done((bf16[512,256]{1,0:T(8,128)(2,1)S(1)}, bf16[512,256]{1,0:T(8,128)(2,1)S(1)}, u32[]{:S(2)}, u32[]{:S(2)}) %collective-permute-start.2) | collective-permute-done | bytes 262176 | tf_op jit(solution)/shard_map/ppermute | solution.py:230
  46.5 1.9 %collective-permute-start.3 = (bf16[512,256]{1,0:T(8,128)(2,1)S(1)}, bf16[512,256]{1,0:T(8,128)(2,1)S(1)}, u32[]{:S(2)}, u32[]{:S(2)}) collective-permute-start(bf16[512,256]{1,0:T(8,128)(2,1)S(1)} %collective-permute-done.2.refs_1_.refs_5_), channel_id=1, source_target_pairs={{8,12},{9,13},{10,14},{11,15},{12,16},{13,17},{14,18},{15,19},{16,... | collective-permute-start | bytes 786440 | tf_op jit(solution)/shard_map/ppermute | solution.py:230
  48.4 0.0 collective-permute-done.7.refs_2_.refs_6_
  48.4 0.7 collective-permute-start.8
  49.1 6.8 %collective-permute-done.3.refs_3_.refs_7_ = bf16[512,256]{1,0:T(8,128)(2,1)S(1)} collective-permute-done((bf16[512,256]{1,0:T(8,128)(2,1)S(1)}, bf16[512,256]{1,0:T(8,128)(2,1)S(1)}, u32[]{:S(2)}, u32[]{:S(2)}) %collective-permute-start.3) | collective-permute-done | bytes 262176 | tf_op jit(solution)/shard_map/ppermute | solution.py:230
  55.9 0.7 collective-permute-start.6
  56.6 1.9 %collective-permute-start.5 = (bf16[256,256]{1,0:T(8,128)(2,1)S(1)}, bf16[256,256]{1,0:T(8,128)(2,1)S(1)}, u32[]{:S(2)}, u32[]{:S(2)}) collective-permute-start(bf16[256,256]{1,0:T(8,128)(2,1)S(1)} %slice.3), channel_id=1, source_target_pairs={{12,16},{13,17},{14,18},{15,19},{16,20},{17,21},{18,22},{19,23},{2... | collective-permute-start | bytes 393224 | tf_op jit(solution)/shard_map/ppermute | solution.py:235
  58.6 0.0 collective-permute-done.8.refs_4_.refs_8_
  58.6 3.6 %more_blocks.5 = (f32[256,1024]{1,0:T(8,128)S(1)}, f32[256,1024]{1,0:T(8,128)S(1)}, f32[256,1024]{1,0:T(8,128)S(1)}) custom-call(bf16[256,1024]{1,0:T(8,128)(2,1)S(1)} %bitcast.30, bf16[512,256]{1,0:T(8,128)(2,1)S(1)} %collective-permute-done.2.refs_1_.refs_5_, ...), custom_call_target="tpu_custom_call", output_to_operand_aliasing={{0}: (9, {}), {1}: (10, {}), {2}: (11, {})} | custom-call | flops 2147483648 | bytes 8388608 | tf_op jit(solution)/shard_map/more_blocks/pallas_call | solution.py:197
  62.2 2.5 %collective-permute-done.5.refs_1_ = bf16[256,256]{1,0:T(8,128)(2,1)S(1)} collective-permute-done((bf16[256,256]{1,0:T(8,128)(2,1)S(1)}, bf16[256,256]{1,0:T(8,128)(2,1)S(1)}, u32[]{:S(2)}, u32[]{:S(2)}) %collective-permute-start.5) | collective-permute-done | bytes 131104 | tf_op jit(solution)/shard_map/ppermute | solution.py:235
  64.7 0.0 collective-permute-done.6.refs_2_
  64.7 1.1 %last_blocks.1 = bf16[256,1024]{1,0:T(8,128)(2,1)S(1)} custom-call(bf16[256,1024]{1,0:T(8,128)(2,1)S(1)} %bitcast.31, bf16[256,256]{1,0:T(8,128)(2,1)S(1)} %collective-permute-done.5.refs_1_, bf16[512,256]{1,0:T(8,128)(2,1)S(1)} %collective-permute-done.6.refs_2_, f32[256,1024]{1,0:T(8,128)S(1)} %get-tuple-element.50.refs_3_, ...), custom_call_target="tpu_custom_call" | custom-call | flops 536870912 | bytes 8388608 | tf_op jit(solution)/shard_map/last_blocks/pallas_call | solution.py:197
  65.9 12.3 %all_to_all.16 = bf16[4,64,1024]{2,1,0:T(8,128)(2,1)S(1)} all-to-all(bf16[4,64,1024]{2,1,0:T(8,128)(2,1)S(1)} %bitcast.32), channel_id=1, replica_groups={{0,1,2,3},{4,5,6,7},{8,9,10,11},{12,13,14,15},{16,17,18,19},{20,21,22,2..., dimensions={0} | all-to-all | bytes 1048576 | tf_op jit(solution)/shard_map/all_to_all | solution.py:41
  78.1 0.8 %copy.20 = bf16[4,8,8,1024]{3,2,0,1:T(8,128)(2,1)} copy(bf16[4,8,8,1024]{3,2,1,0:T(8,128)(2,1)S(1)} %bitcast.33) | data formatting | bytes 1048576 | tf_op jit(solution)/shard_map/reshape | solution.py:241
  (5 shorter events, 0.1 us)
Async XLA Ops:
  0.0 0.8 %copy-start = (bf16[64,512]{1,0:T(8,128)(2,1)S(1)}, bf16[64,512]{1,0:T(8,128)(2,1)}, u32[]{:S(2)}) copy-start(bf16[64,512]{1,0:T(8,128)(2,1)} %param.4) | copy-start | bytes 196612
  0.8 21.9 %copy-start.1 = (bf16[64,4096]{1,0:T(8,128)(2,1)S(1)}, bf16[64,4096]{1,0:T(8,128)(2,1)}, u32[]{:S(2)}) copy-start(bf16[64,4096]{1,0:T(8,128)(2,1)} %param.3) | copy-start | bytes 1572868
  11.9 15.3 %collective-permute-start = (bf16[256,256]{1,0:T(8,128)(2,1)S(1)}, bf16[256,256]{1,0:T(8,128)(2,1)S(1)}, u32[]{:S(2)}, u32[]{:S(2)}) collective-permute-start(bf16[256,256]{1,0:T(8,128)(2,1)S(1)} %bitcast.34), channel_id=1, source_target_pairs={{0,32},{1,33},{2,34},{3,35},{4,36},{5,37},{6,38},{7,39},{8,40},{9,... | collective-permute-start | bytes 393224 | tf_op jit(solution)/shard_map/ppermute | solution.py:217
  23.6 11.5 %all-to-all-start = ((bf16[4,64,1024]{2,1,0:T(8,128)(2,1)}), bf16[4,64,1024]{2,1,0:T(8,128)(2,1)S(1)}, u32[]{:S(2)}, u32[]{:S(2)}) async-start(bf16[4,64,1024]{2,1,0:T(8,128)(2,1)} %bitcast.26), calls=%async_computation | async-start | bytes 1048576 | tf_op jit(solution)/shard_map/all_to_all | solution.py:41
  27.2 9.8 %collective-permute-start.1 = (bf16[512,256]{1,0:T(8,128)(2,1)S(1)}, bf16[512,256]{1,0:T(8,128)(2,1)S(1)}, u32[]{:S(2)}, u32[]{:S(2)}) collective-permute-start(bf16[512,256]{1,0:T(8,128)(2,1)S(1)} %pad_maximum_fusion.kv_ref), channel_id=1, source_target_pairs={{0,4},{1,5},{2,6},{3,7},{4,8},{5,9},{6,10},{7,11},{8,12},{9,13},{1... | collective-permute-start | bytes 786440 | tf_op jit(solution)/shard_map/ppermute | solution.py:224
  29.8 9.8 %collective-permute-start.4 = (bf16[512,256]{1,0:T(8,128)(2,1)S(1)}, bf16[512,256]{1,0:T(8,128)(2,1)S(1)}, u32[]{:S(2)}, u32[]{:S(2)}) collective-permute-start(bf16[512,256]{1,0:T(8,128)(2,1)S(1)} %pad_maximum_fusion.kv_ref), channel_id=1, source_target_pairs={{0,28},{1,29},{2,30},{3,31},{4,0},{5,1},{6,2},{7,3},{8,4},{9,5},{1... | collective-permute-start | bytes 786440 | tf_op jit(solution)/shard_map/ppermute | solution.py:225
  37.0 9.5 %collective-permute-start.2 = (bf16[512,256]{1,0:T(8,128)(2,1)S(1)}, bf16[512,256]{1,0:T(8,128)(2,1)S(1)}, u32[]{:S(2)}, u32[]{:S(2)}) collective-permute-start(bf16[512,256]{1,0:T(8,128)(2,1)S(1)} %collective-permute-done.1.refs_1_.refs_2_), channel_id=1, source_target_pairs={{4,8},{5,9},{6,10},{7,11},{8,12},{9,13},{10,14},{11,15},{12,16},{1... | collective-permute-start | bytes 786440 | tf_op jit(solution)/shard_map/ppermute | solution.py:230
  39.6 8.8 %collective-permute-start.7 = (bf16[512,256]{1,0:T(8,128)(2,1)S(1)}, bf16[512,256]{1,0:T(8,128)(2,1)S(1)}, u32[]{:S(2)}, u32[]{:S(2)}) collective-permute-start(bf16[512,256]{1,0:T(8,128)(2,1)S(1)} %collective-permute-done.4.refs_1_.refs_2_), channel_id=1, source_target_pairs={{0,28},{1,29},{2,30},{3,31},{4,0},{5,1},{6,2},{7,3},{28,24},{29,25... | collective-permute-start | bytes 786440 | tf_op jit(solution)/shard_map/ppermute | solution.py:231
  46.5 9.5 %collective-permute-start.3 = (bf16[512,256]{1,0:T(8,128)(2,1)S(1)}, bf16[512,256]{1,0:T(8,128)(2,1)S(1)}, u32[]{:S(2)}, u32[]{:S(2)}) collective-permute-start(bf16[512,256]{1,0:T(8,128)(2,1)S(1)} %collective-permute-done.2.refs_1_.refs_5_), channel_id=1, source_target_pairs={{8,12},{9,13},{10,14},{11,15},{12,16},{13,17},{14,18},{15,19},{16,... | collective-permute-start | bytes 786440 | tf_op jit(solution)/shard_map/ppermute | solution.py:230
  48.4 10.2 %collective-permute-start.8 = (bf16[512,256]{1,0:T(8,128)(2,1)S(1)}, bf16[512,256]{1,0:T(8,128)(2,1)S(1)}, u32[]{:S(2)}, u32[]{:S(2)}) collective-permute-start(bf16[512,256]{1,0:T(8,128)(2,1)S(1)} %collective-permute-done.7.refs_2_.refs_6_), channel_id=1, source_target_pairs={{0,28},{1,29},{2,30},{3,31},{24,20},{25,21},{26,22},{27,23},{28,24... | collective-permute-start | bytes 786440 | tf_op jit(solution)/shard_map/ppermute | solution.py:231
  55.9 8.8 %collective-permute-start.6 = (bf16[512,256]{1,0:T(8,128)(2,1)S(1)}, bf16[512,256]{1,0:T(8,128)(2,1)S(1)}, u32[]{:S(2)}, u32[]{:S(2)}) collective-permute-start(bf16[512,256]{1,0:T(8,128)(2,1)S(1)} %collective-permute-done.3.refs_3_.refs_7_), channel_id=1, source_target_pairs={{32,36},{33,37},{34,38},{35,39},{36,40},{37,41},{38,42},{39,43},{4... | collective-permute-start | bytes 786440 | tf_op jit(solution)/shard_map/ppermute | solution.py:236
  56.6 8.1 %collective-permute-start.5 = (bf16[256,256]{1,0:T(8,128)(2,1)S(1)}, bf16[256,256]{1,0:T(8,128)(2,1)S(1)}, u32[]{:S(2)}, u32[]{:S(2)}) collective-permute-start(bf16[256,256]{1,0:T(8,128)(2,1)S(1)} %slice.3), channel_id=1, source_target_pairs={{12,16},{13,17},{14,18},{15,19},{16,20},{17,21},{18,22},{19,23},{2... | collective-permute-start | bytes 393224 | tf_op jit(solution)/shard_map/ppermute | solution.py:235

commit v8 on v7

--- a/solution.py
+++ b/solution.py
@@ -220,23 +220,25 @@
     kv = jnp.concatenate(
         [jnp.where(z == 0, own, other), jnp.where(z == 0, other, own)], axis=0
     )
-    got = {}
-    got[1] = lax.ppermute(kv, "ctx", ring(1, 1))
-    got[-1] = lax.ppermute(kv, "ctx", ring(-1, 1))
+    def send_up(first, second, step):
+        return (
+            lax.ppermute(first, "ctx", ring(1, step, (0,))),
+            lax.ppermute(second, "ctx", ring(1, step, (1,))),
+        )
+
+    got = {1: send_up(kv[:ROWS], kv, 1)}
+    down = lax.ppermute(kv, "ctx", ring(-1, 1))
+    got[-1] = (down, down)
     state = own_block(x, kv)
     for step, shifts in ((1, (1,)), (2, (-1,)), (3, (2, -2, 3, -3))):
-        got[step], state = lax.optimization_barrier((got[step], state))
+        up, state = lax.optimization_barrier((got[step], state))
+        got[step] = up
+        got[step + 1] = send_up(*up, step + 1)
         if step < NY // 2 - 1:
-            got[step + 1] = lax.ppermute(got[step], "ctx", ring(1, step + 1))
-            got[-step - 1] = lax.ppermute(got[-step], "ctx", ring(-1, step + 1))
-        else:
-            last = (
-                step + 1,
-                lax.ppermute(got[step][:ROWS], "ctx", ring(1, step + 1, (0,))),
-                lax.ppermute(got[step], "ctx", ring(1, step + 1, (1,))),
-            )
-        state = absorb([(at, got[at], got[at]) for at in shifts], x, state)
-    (out,) = absorb([last], x, state, last=True)
+            down = lax.ppermute(down, "ctx", ring(-1, step + 1))
+            got[-step - 1] = (down, down)
+        state = absorb([(at, *got[at]) for at in shifts], x, state)
+    (out,) = absorb([(NY // 2, *got[NY // 2])], x, state, last=True)
     out = exchange(out.reshape(NX, rows, GROUP * HD))
     return out.transpose(1, 0, 2).reshape(rows, QH * HD)
 

time: 79.4 us -> 79.4 us (level)
  waiting for transfers between devices: 18.6 us -> 16.4 us
  starting transfers between devices: 26.1 us -> 28.2 us
    ppermute x8 -> x11, starting transfers between devices: 11.7 us -> 13.8 us  [the longest x4 9.08 us: send_up(): lax.ppermute(first, 'ctx', ring(1, step, (0,)))]
    ppermute x8 -> x11, waiting for transfers between devices: 13.9 us -> 12.4 us  [the longest x4 12.4 us: send_up(): lax.ppermute(first, 'ctx', ring(1, step, (0,)))]
  transfers between devices with their start and end apart: 10 -> 13, of which waited for: 4 -> 4; matrix products, arithmetic and copies ran while one was open for 1% -> 1% of each run, Pallas kernels for 9% -> 9%
where the time goes in v8:
time: 79.4 us; the launch traced here: 78.9 us
  starting transfers between devices  28.2 us (36%)
  blocking collectives  22.3 us (28%)
  waiting for transfers between devices  16.4 us (21%)
  Pallas kernels  8.22 us (10%)
  local copies, waits for them, and re-layouts  3.43 us (4%)
    all_to_all x2, blocking collectives, exchange(): lax.all_to_all(pieces, 'ctx', 0, 0, axis_index_groups=X_GROUPS, tiled=True)  22.3 us
    ppermute x4, waiting for transfers between devices, send_up(): lax.ppermute(first, 'ctx', ring(1, step, (0,)))  12.4 us
    ppermute x1, starting transfers between devices, local(): other = lax.ppermute(own, 'ctx', Z_SWAP)  10.9 us
    ppermute x4, starting transfers between devices, send_up(): lax.ppermute(first, 'ctx', ring(1, step, (0,)))  9.08 us
    pallas_call x4, Pallas kernels, absorb(): pl.pallas_call(functools.partial(more_kernel, shifts, last), out_shape=ou...  6.38 us
    all_to_all x1, waiting for transfers between devices, exchange(): lax.all_to_all(pieces, 'ctx', 0, 0, axis_index_groups=X_GROUPS, tiled=True)  3.99 us
    all_to_all x1, starting transfers between devices, exchange(): lax.all_to_all(pieces, 'ctx', 0, 0, axis_index_groups=X_GROUPS, tiled=True)  3.47 us
    ppermute x4, starting transfers between devices, send_up(): lax.ppermute(second, 'ctx', ring(1, step, (1,)))  2.69 us
  transfers between devices with their start and end apart: 13, of which 4 were waited for; matrix products, arithmetic and copies ran while one was open for 1% of the time, Pallas kernels for 9%

profile of v8, /device:TPU:32, one launch (start us, length us, event | category | flops | bytes accessed | tf_op | source)
XLA Modules:
  0.0 78.9 jit_solution(6325378013050318400)
XLA Ops:
  0.0 0.0 copy-start
  0.0 0.8 %copy-done = bf16[64,512]{1,0:T(8,128)(2,1)S(1)} copy-done((bf16[64,512]{1,0:T(8,128)(2,1)S(1)}, bf16[64,512]{1,0:T(8,128)(2,1)}, u32[]{:S(2)}) %copy-start) | copy-done | bytes 65560
  0.8 0.0 copy-start.1
  0.8 0.9 %copy_bitcast_fusion = (bf16[64,4,128]{2,0,1:T(8,128)(2,1)S(1)}, bf16[64,4,128]{2,0,1:T(8,128)(2,1)S(1)}) fusion(bf16[64,512]{1,0:T(8,128)(2,1)S(1)} %copy-done, bf16[64,512]{1,0:T(8,128)(2,1)} %param.5), kind=kLoop, calls=%fused_computation.5 | loop fusion | bytes 262144 | tf_op jit(solution)/shard_map/reshape | solution.py:214
  1.8 10.1 %all_to_all.15 = bf16[4,64,256]{2,1,0:T(8,128)(2,1)S(1)} all-to-all(bf16[4,64,256]{2,1,0:T(8,128)(2,1)S(1)} %maximum_bitcast_fusion), channel_id=1, replica_groups={{0,1,2,3},{4,5,6,7},{8,9,10,11},{12,13,14,15},{16,17,18,19},{20,21,22,2..., dimensions={0} | all-to-all | bytes 262144 | tf_op jit(solution)/shard_map/all_to_all | solution.py:41
  11.9 10.9 %collective-permute-start = (bf16[256,256]{1,0:T(8,128)(2,1)S(1)}, bf16[256,256]{1,0:T(8,128)(2,1)S(1)}, u32[]{:S(2)}, u32[]{:S(2)}) collective-permute-start(bf16[256,256]{1,0:T(8,128)(2,1)S(1)} %bitcast.34), channel_id=1, source_target_pairs={{0,32},{1,33},{2,34},{3,35},{4,36},{5,37},{6,38},{7,39},{8,40},{9,... | collective-permute-start | bytes 393224 | tf_op jit(solution)/shard_map/ppermute | solution.py:217
  22.8 0.0 copy-done.1
  22.8 0.8 %copy.24 = bf16[8,4,8,1024]{3,2,0,1:T(8,128)(2,1)} copy(bf16[8,4,8,1024]{3,2,1,0:T(8,128)(2,1)S(1)} %bitcast.35) | data formatting | bytes 1048576 | tf_op jit(solution)/shard_map/reshape | solution.py:218
  23.6 3.5 %all-to-all-start = ((bf16[4,64,1024]{2,1,0:T(8,128)(2,1)}), bf16[4,64,1024]{2,1,0:T(8,128)(2,1)S(1)}, u32[]{:S(2)}, u32[]{:S(2)}) async-start(bf16[4,64,1024]{2,1,0:T(8,128)(2,1)} %bitcast.26), calls=%async_computation | async-start | bytes 1048576 | tf_op jit(solution)/shard_map/all_to_all | solution.py:41
  27.1 0.0 collective-permute-done
  27.2 0.7 collective-permute-start.2
  27.9 0.7 collective-permute-start.7
  28.6 2.6 %collective-permute-start.1 = (bf16[256,256]{1,0:T(8,128)(2,1)S(1)}, bf16[256,256]{1,0:T(8,128)(2,1)S(1)}, u32[]{:S(2)}, u32[]{:S(2)}) collective-permute-start(bf16[256,256]{1,0:T(8,128)(2,1)S(1)} %get-tuple-element.60), channel_id=1, source_target_pairs={{0,4},{1,5},{2,6},{3,7},{4,8},{5,9},{6,10},{7,11},{8,12},{9,13},{1... | collective-permute-start | bytes 393224 | tf_op jit(solution)/shard_map/ppermute | solution.py:225
  31.2 4.0 %all-to-all-done = bf16[4,64,1024]{2,1,0:T(8,128)(2,1)S(1)} async-done(((bf16[4,64,1024]{2,1,0:T(8,128)(2,1)}), bf16[4,64,1024]{2,1,0:T(8,128)(2,1)S(1)}, u32[]{:S(2)}, u32[]{:S(2)}) %all-to-all-start) | async-done | bytes 524320 | tf_op jit(solution)/shard_map/all_to_all | solution.py:41
  35.1 1.8 %own_block.1 = (f32[256,1024]{1,0:T(8,128)S(1)}, f32[256,1024]{1,0:T(8,128)S(1)}, f32[256,1024]{1,0:T(8,128)S(1)}) custom-call(bf16[256,1024]{1,0:T(8,128)(2,1)S(1)} %bitcast.27, bf16[512,256]{1,0:T(8,128)(2,1)S(1)} %pad_maximum_fusion.kv_ref), custom_call_target="tpu_custom_call" | custom-call | flops 536870912 | bytes 8388608 | tf_op jit(solution)/shard_map/own_block/pallas_call | solution.py:180
  37.0 0.0 collective-permute-done.1.refs_1_
  37.0 0.0 collective-permute-done.2.refs_2_
  37.0 0.7 collective-permute-start.4
  37.7 0.0 collective-permute-done.7.refs_1_.refs_2_
  37.7 0.7 collective-permute-start.10
  38.4 2.6 %collective-permute-start.3 = (bf16[256,256]{1,0:T(8,128)(2,1)S(1)}, bf16[256,256]{1,0:T(8,128)(2,1)S(1)}, u32[]{:S(2)}, u32[]{:S(2)}) collective-permute-start(bf16[256,256]{1,0:T(8,128)(2,1)S(1)} %collective-permute-done.1.refs_1_), channel_id=1, source_target_pairs={{4,8},{5,9},{6,10},{7,11},{8,12},{9,13},{10,14},{11,15},{12,16},{1... | collective-permute-start | bytes 393224 | tf_op jit(solution)/shard_map/ppermute | solution.py:225
  41.0 1.6 %more_blocks.3 = (f32[256,1024]{1,0:T(8,128)S(1)}, f32[256,1024]{1,0:T(8,128)S(1)}, f32[256,1024]{1,0:T(8,128)S(1)}) custom-call(bf16[256,1024]{1,0:T(8,128)(2,1)S(1)} %bitcast.28, bf16[256,256]{1,0:T(8,128)(2,1)S(1)} %collective-permute-done.1.refs_1_, ...), custom_call_target="tpu_custom_call", output_to_operand_aliasing={{0}: (3, {}), {1}: (4, {}), {2}: (5, {})} | custom-call | flops 536870912 | bytes 8388608 | tf_op jit(solution)/shard_map/more_blocks/pallas_call | solution.py:197
  42.6 3.9 %collective-permute-done.3.refs_1_ = bf16[256,256]{1,0:T(8,128)(2,1)S(1)} collective-permute-done((bf16[256,256]{1,0:T(8,128)(2,1)S(1)}, bf16[256,256]{1,0:T(8,128)(2,1)S(1)}, u32[]{:S(2)}, u32[]{:S(2)}) %collective-permute-start.3) | collective-permute-done | bytes 131104 | tf_op jit(solution)/shard_map/ppermute | solution.py:225
  46.5 0.0 collective-permute-done.4.refs_5_
  46.5 0.7 collective-permute-start.6
  47.1 0.0 collective-permute-done.10.refs_2_.refs_6_
  47.2 0.7 collective-permute-start.11
  47.8 2.0 %collective-permute-start.5 = (bf16[256,256]{1,0:T(8,128)(2,1)S(1)}, bf16[256,256]{1,0:T(8,128)(2,1)S(1)}, u32[]{:S(2)}, u32[]{:S(2)}) collective-permute-start(bf16[256,256]{1,0:T(8,128)(2,1)S(1)} %collective-permute-done.3.refs_1_), channel_id=1, source_target_pairs={{8,12},{9,13},{10,14},{11,15},{12,16},{13,17},{14,18},{15,19},{16,... | collective-permute-start | bytes 393224 | tf_op jit(solution)/shard_map/ppermute | solution.py:225
  49.9 6.0 %collective-permute-done.5.refs_3_ = bf16[256,256]{1,0:T(8,128)(2,1)S(1)} collective-permute-done((bf16[256,256]{1,0:T(8,128)(2,1)S(1)}, bf16[256,256]{1,0:T(8,128)(2,1)S(1)}, u32[]{:S(2)}, u32[]{:S(2)}) %collective-permute-start.5) | collective-permute-done | bytes 131104 | tf_op jit(solution)/shard_map/ppermute | solution.py:225
  55.9 0.0 collective-permute-done.6.refs_7_
  55.9 0.7 collective-permute-start.9
  56.6 1.9 %collective-permute-start.8 = (bf16[256,256]{1,0:T(8,128)(2,1)S(1)}, bf16[256,256]{1,0:T(8,128)(2,1)S(1)}, u32[]{:S(2)}, u32[]{:S(2)}) collective-permute-start(bf16[256,256]{1,0:T(8,128)(2,1)S(1)} %collective-permute-done.5.refs_3_), channel_id=1, source_target_pairs={{12,16},{13,17},{14,18},{15,19},{16,20},{17,21},{18,22},{19,23},{2... | collective-permute-start | bytes 393224 | tf_op jit(solution)/shard_map/ppermute | solution.py:225
  58.5 0.0 collective-permute-done.11.refs_4_.refs_8_
  58.5 3.6 %more_blocks.5 = (f32[256,1024]{1,0:T(8,128)S(1)}, f32[256,1024]{1,0:T(8,128)S(1)}, f32[256,1024]{1,0:T(8,128)S(1)}) custom-call(bf16[256,1024]{1,0:T(8,128)(2,1)S(1)} %bitcast.30, bf16[256,256]{1,0:T(8,128)(2,1)S(1)} %collective-permute-done.3.refs_1_, ...), custom_call_target="tpu_custom_call", output_to_operand_aliasing={{0}: (9, {}), {1}: (10, {}), {2}: (11, {})} | custom-call | flops 2147483648 | bytes 8388608 | tf_op jit(solution)/shard_map/more_blocks/pallas_call | solution.py:197
  62.2 2.5 %collective-permute-done.8.refs_1_ = bf16[256,256]{1,0:T(8,128)(2,1)S(1)} collective-permute-done((bf16[256,256]{1,0:T(8,128)(2,1)S(1)}, bf16[256,256]{1,0:T(8,128)(2,1)S(1)}, u32[]{:S(2)}, u32[]{:S(2)}) %collective-permute-start.8) | collective-permute-done | bytes 131104 | tf_op jit(solution)/shard_map/ppermute | solution.py:225
  64.7 0.0 collective-permute-done.9.refs_2_
  64.7 1.1 %last_blocks.1 = bf16[256,1024]{1,0:T(8,128)(2,1)S(1)} custom-call(bf16[256,1024]{1,0:T(8,128)(2,1)S(1)} %bitcast.31, bf16[256,256]{1,0:T(8,128)(2,1)S(1)} %collective-permute-done.8.refs_1_, bf16[512,256]{1,0:T(8,128)(2,1)S(1)} %collective-permute-done.9.refs_2_, f32[256,1024]{1,0:T(8,128)S(1)} %get-tuple-element.56.refs_3_, ...), custom_call_target="tpu_custom_call" | custom-call | flops 536870912 | bytes 8388608 | tf_op jit(solution)/shard_map/last_blocks/pallas_call | solution.py:197
  65.8 12.2 %all_to_all.16 = bf16[4,64,1024]{2,1,0:T(8,128)(2,1)S(1)} all-to-all(bf16[4,64,1024]{2,1,0:T(8,128)(2,1)S(1)} %bitcast.32), channel_id=1, replica_groups={{0,1,2,3},{4,5,6,7},{8,9,10,11},{12,13,14,15},{16,17,18,19},{20,21,22,2..., dimensions={0} | all-to-all | bytes 1048576 | tf_op jit(solution)/shard_map/all_to_all | solution.py:41
  78.0 0.8 %copy.20 = bf16[4,8,8,1024]{3,2,0,1:T(8,128)(2,1)} copy(bf16[4,8,8,1024]{3,2,1,0:T(8,128)(2,1)S(1)} %bitcast.33) | data formatting | bytes 1048576 | tf_op jit(solution)/shard_map/reshape | solution.py:243
  (4 shorter events, 0.1 us)
Async XLA Ops:
  0.0 0.8 %copy-start = (bf16[64,512]{1,0:T(8,128)(2,1)S(1)}, bf16[64,512]{1,0:T(8,128)(2,1)}, u32[]{:S(2)}) copy-start(bf16[64,512]{1,0:T(8,128)(2,1)} %param.4) | copy-start | bytes 196612
  0.8 21.9 %copy-start.1 = (bf16[64,4096]{1,0:T(8,128)(2,1)S(1)}, bf16[64,4096]{1,0:T(8,128)(2,1)}, u32[]{:S(2)}) copy-start(bf16[64,4096]{1,0:T(8,128)(2,1)} %param.3) | copy-start | bytes 1572868
  11.9 15.3 %collective-permute-start = (bf16[256,256]{1,0:T(8,128)(2,1)S(1)}, bf16[256,256]{1,0:T(8,128)(2,1)S(1)}, u32[]{:S(2)}, u32[]{:S(2)}) collective-permute-start(bf16[256,256]{1,0:T(8,128)(2,1)S(1)} %bitcast.34), channel_id=1, source_target_pairs={{0,32},{1,33},{2,34},{3,35},{4,36},{5,37},{6,38},{7,39},{8,40},{9,... | collective-permute-start | bytes 393224 | tf_op jit(solution)/shard_map/ppermute | solution.py:217
  23.6 11.5 %all-to-all-start = ((bf16[4,64,1024]{2,1,0:T(8,128)(2,1)}), bf16[4,64,1024]{2,1,0:T(8,128)(2,1)S(1)}, u32[]{:S(2)}, u32[]{:S(2)}) async-start(bf16[4,64,1024]{2,1,0:T(8,128)(2,1)} %bitcast.26), calls=%async_computation | async-start | bytes 1048576 | tf_op jit(solution)/shard_map/all_to_all | solution.py:41
  27.2 9.8 %collective-permute-start.2 = (bf16[512,256]{1,0:T(8,128)(2,1)S(1)}, bf16[512,256]{1,0:T(8,128)(2,1)S(1)}, u32[]{:S(2)}, u32[]{:S(2)}) collective-permute-start(bf16[512,256]{1,0:T(8,128)(2,1)S(1)} %pad_maximum_fusion.kv_ref), channel_id=1, source_target_pairs={{32,36},{33,37},{34,38},{35,39},{36,40},{37,41},{38,42},{39,43},{4... | collective-permute-start | bytes 786440 | tf_op jit(solution)/shard_map/ppermute | solution.py:226
  27.9 9.8 %collective-permute-start.7 = (bf16[512,256]{1,0:T(8,128)(2,1)S(1)}, bf16[512,256]{1,0:T(8,128)(2,1)S(1)}, u32[]{:S(2)}, u32[]{:S(2)}) collective-permute-start(bf16[512,256]{1,0:T(8,128)(2,1)S(1)} %pad_maximum_fusion.kv_ref), channel_id=1, source_target_pairs={{0,28},{1,29},{2,30},{3,31},{4,0},{5,1},{6,2},{7,3},{8,4},{9,5},{1... | collective-permute-start | bytes 786440 | tf_op jit(solution)/shard_map/ppermute | solution.py:230
  28.6 8.4 %collective-permute-start.1 = (bf16[256,256]{1,0:T(8,128)(2,1)S(1)}, bf16[256,256]{1,0:T(8,128)(2,1)S(1)}, u32[]{:S(2)}, u32[]{:S(2)}) collective-permute-start(bf16[256,256]{1,0:T(8,128)(2,1)S(1)} %get-tuple-element.60), channel_id=1, source_target_pairs={{0,4},{1,5},{2,6},{3,7},{4,8},{5,9},{6,10},{7,11},{8,12},{9,13},{1... | collective-permute-start | bytes 393224 | tf_op jit(solution)/shard_map/ppermute | solution.py:225
  37.0 9.5 %collective-permute-start.4 = (bf16[512,256]{1,0:T(8,128)(2,1)S(1)}, bf16[512,256]{1,0:T(8,128)(2,1)S(1)}, u32[]{:S(2)}, u32[]{:S(2)}) collective-permute-start(bf16[512,256]{1,0:T(8,128)(2,1)S(1)} %collective-permute-done.2.refs_2_), channel_id=1, source_target_pairs={{32,36},{33,37},{34,38},{35,39},{36,40},{37,41},{38,42},{39,43},{4... | collective-permute-start | bytes 786440 | tf_op jit(solution)/shard_map/ppermute | solution.py:226
  37.7 9.4 %collective-permute-start.10 = (bf16[512,256]{1,0:T(8,128)(2,1)S(1)}, bf16[512,256]{1,0:T(8,128)(2,1)S(1)}, u32[]{:S(2)}, u32[]{:S(2)}) collective-permute-start(bf16[512,256]{1,0:T(8,128)(2,1)S(1)} %collective-permute-done.7.refs_1_.refs_2_), channel_id=1, source_target_pairs={{0,28},{1,29},{2,30},{3,31},{4,0},{5,1},{6,2},{7,3},{28,24},{29,25... | collective-permute-start | bytes 786440 | tf_op jit(solution)/shard_map/ppermute | solution.py:238
  38.4 8.1 %collective-permute-start.3 = (bf16[256,256]{1,0:T(8,128)(2,1)S(1)}, bf16[256,256]{1,0:T(8,128)(2,1)S(1)}, u32[]{:S(2)}, u32[]{:S(2)}) collective-permute-start(bf16[256,256]{1,0:T(8,128)(2,1)S(1)} %collective-permute-done.1.refs_1_), channel_id=1, source_target_pairs={{4,8},{5,9},{6,10},{7,11},{8,12},{9,13},{10,14},{11,15},{12,16},{1... | collective-permute-start | bytes 393224 | tf_op jit(solution)/shard_map/ppermute | solution.py:225
  46.5 9.4 %collective-permute-start.6 = (bf16[512,256]{1,0:T(8,128)(2,1)S(1)}, bf16[512,256]{1,0:T(8,128)(2,1)S(1)}, u32[]{:S(2)}, u32[]{:S(2)}) collective-permute-start(bf16[512,256]{1,0:T(8,128)(2,1)S(1)} %collective-permute-done.4.refs_5_), channel_id=1, source_target_pairs={{32,36},{33,37},{34,38},{35,39},{36,40},{37,41},{38,42},{39,43},{4... | collective-permute-start | bytes 786440 | tf_op jit(solution)/shard_map/ppermute | solution.py:226
  47.2 11.4 %collective-permute-start.11 = (bf16[512,256]{1,0:T(8,128)(2,1)S(1)}, bf16[512,256]{1,0:T(8,128)(2,1)S(1)}, u32[]{:S(2)}, u32[]{:S(2)}) collective-permute-start(bf16[512,256]{1,0:T(8,128)(2,1)S(1)} %collective-permute-done.10.refs_2_.refs_6_), channel_id=1, source_target_pairs={{0,28},{1,29},{2,30},{3,31},{24,20},{25,21},{26,22},{27,23},{28,24... | collective-permute-start | bytes 786440 | tf_op jit(solution)/shard_map/ppermute | solution.py:238
  47.8 8.1 %collective-permute-start.5 = (bf16[256,256]{1,0:T(8,128)(2,1)S(1)}, bf16[256,256]{1,0:T(8,128)(2,1)S(1)}, u32[]{:S(2)}, u32[]{:S(2)}) collective-permute-start(bf16[256,256]{1,0:T(8,128)(2,1)S(1)} %collective-permute-done.3.refs_1_), channel_id=1, source_target_pairs={{8,12},{9,13},{10,14},{11,15},{12,16},{13,17},{14,18},{15,19},{16,... | collective-permute-start | bytes 393224 | tf_op jit(solution)/shard_map/ppermute | solution.py:225
  55.9 8.8 %collective-permute-start.9 = (bf16[512,256]{1,0:T(8,128)(2,1)S(1)}, bf16[512,256]{1,0:T(8,128)(2,1)S(1)}, u32[]{:S(2)}, u32[]{:S(2)}) collective-permute-start(bf16[512,256]{1,0:T(8,128)(2,1)S(1)} %collective-permute-done.6.refs_7_), channel_id=1, source_target_pairs={{32,36},{33,37},{34,38},{35,39},{36,40},{37,41},{38,42},{39,43},{4... | collective-permute-start | bytes 786440 | tf_op jit(solution)/shard_map/ppermute | solution.py:226
  56.6 8.1 %collective-permute-start.8 = (bf16[256,256]{1,0:T(8,128)(2,1)S(1)}, bf16[256,256]{1,0:T(8,128)(2,1)S(1)}, u32[]{:S(2)}, u32[]{:S(2)}) collective-permute-start(bf16[256,256]{1,0:T(8,128)(2,1)S(1)} %collective-permute-done.5.refs_3_), channel_id=1, source_target_pairs={{12,16},{13,17},{14,18},{15,19},{16,20},{17,21},{18,22},{19,23},{2... | collective-permute-start | bytes 393224 | tf_op jit(solution)/shard_map/ppermute | solution.py:225

commit v9 on v8

--- a/solution.py
+++ b/solution.py
@@ -7,6 +7,7 @@
 from jax.experimental import pallas as pl
 from jax.experimental.pallas import tpu as pltpu
 from jax.sharding import PartitionSpec as P
+
 
 QH = 32
 KVH = 4
@@ -207,7 +208,7 @@
     )(x, *firsts, *seconds, *state)
 
 
-def local(queries, keys, values):
+def attention(queries, keys, values):
     rows = queries.shape[0]
     z, _ = place_of()
     by_head = jnp.concatenate(
@@ -220,11 +221,11 @@
     kv = jnp.concatenate(
         [jnp.where(z == 0, own, other), jnp.where(z == 0, other, own)], axis=0
     )
+
     def send_up(first, second, step):
-        return (
-            lax.ppermute(first, "ctx", ring(1, step, (0,))),
-            lax.ppermute(second, "ctx", ring(1, step, (1,))),
-        )
+        first = lax.ppermute(first, "ctx", ring(1, step, (0,)))
+        second = lax.ppermute(second, "ctx", ring(1, step, (1,)))
+        return first, second
 
     got = {1: send_up(kv[:ROWS], kv, 1)}
     down = lax.ppermute(kv, "ctx", ring(-1, 1))
@@ -246,5 +247,5 @@
 def solution(mesh):
     spec = P(("dp", "ctx"), None)
     return jax.shard_map(
-        local, mesh=mesh, in_specs=(spec,) * 3, out_specs=spec, check_vma=False
-    )
+        attention, mesh=mesh, in_specs=(spec,) * 3, out_specs=spec, check_vma=False
+    )

time: 79.4 us -> 79.4 us (level)
  no operation moved by 1% of the time
where the time goes in v9:
time: 79.4 us; the launch traced here: 78.9 us
  starting transfers between devices  28.2 us (36%)
  blocking collectives  22.3 us (28%)
  waiting for transfers between devices  16.4 us (21%)
  Pallas kernels  8.22 us (10%)
  local copies, waits for them, and re-layouts  3.43 us (4%)
    all_to_all x2, blocking collectives, exchange(): lax.all_to_all(pieces, 'ctx', 0, 0, axis_index_groups=X_GROUPS, tiled=True)  22.3 us
    ppermute x4, waiting for transfers between devices, send_up(): first = lax.ppermute(first, 'ctx', ring(1, step, (0,)))  12.4 us
    ppermute x1, starting transfers between devices, attention(): other = lax.ppermute(own, 'ctx', Z_SWAP)  10.9 us
    ppermute x4, starting transfers between devices, send_up(): first = lax.ppermute(first, 'ctx', ring(1, step, (0,)))  9.08 us
    pallas_call x4, Pallas kernels, absorb(): pl.pallas_call(functools.partial(more_kernel, shifts, last), out_shape=ou...  6.38 us
    all_to_all x1, waiting for transfers between devices, exchange(): lax.all_to_all(pieces, 'ctx', 0, 0, axis_index_groups=X_GROUPS, tiled=True)  3.99 us
    all_to_all x1, starting transfers between devices, exchange(): lax.all_to_all(pieces, 'ctx', 0, 0, axis_index_groups=X_GROUPS, tiled=True)  3.47 us
    ppermute x4, starting transfers between devices, send_up(): second = lax.ppermute(second, 'ctx', ring(1, step, (1,)))  2.69 us
  transfers between devices with their start and end apart: 13, of which 4 were waited for; matrix products, arithmetic and copies ran while one was open for 1% of the time, Pallas kernels for 9%

profile of v9, /device:TPU:32, one launch (start us, length us, event | category | flops | bytes accessed | tf_op | source)
XLA Modules:
  0.0 78.9 jit_solution(6325378013050318400)
XLA Ops:
  0.0 0.0 copy-start
  0.0 0.8 %copy-done = bf16[64,512]{1,0:T(8,128)(2,1)S(1)} copy-done((bf16[64,512]{1,0:T(8,128)(2,1)S(1)}, bf16[64,512]{1,0:T(8,128)(2,1)}, u32[]{:S(2)}) %copy-start) | copy-done | bytes 65560
  0.8 0.0 copy-start.1
  0.8 0.9 %copy_bitcast_fusion = (bf16[64,4,128]{2,0,1:T(8,128)(2,1)S(1)}, bf16[64,4,128]{2,0,1:T(8,128)(2,1)S(1)}) fusion(bf16[64,512]{1,0:T(8,128)(2,1)S(1)} %copy-done, bf16[64,512]{1,0:T(8,128)(2,1)} %param.5), kind=kLoop, calls=%fused_computation.5 | loop fusion | bytes 262144 | tf_op jit(solution)/shard_map/reshape | solution.py:215
  1.8 10.1 %all_to_all.15 = bf16[4,64,256]{2,1,0:T(8,128)(2,1)S(1)} all-to-all(bf16[4,64,256]{2,1,0:T(8,128)(2,1)S(1)} %maximum_bitcast_fusion), channel_id=1, replica_groups={{0,1,2,3},{4,5,6,7},{8,9,10,11},{12,13,14,15},{16,17,18,19},{20,21,22,2..., dimensions={0} | all-to-all | bytes 262144 | tf_op jit(solution)/shard_map/all_to_all | solution.py:42
  11.9 10.9 %collective-permute-start = (bf16[256,256]{1,0:T(8,128)(2,1)S(1)}, bf16[256,256]{1,0:T(8,128)(2,1)S(1)}, u32[]{:S(2)}, u32[]{:S(2)}) collective-permute-start(bf16[256,256]{1,0:T(8,128)(2,1)S(1)} %bitcast.34), channel_id=1, source_target_pairs={{0,32},{1,33},{2,34},{3,35},{4,36},{5,37},{6,38},{7,39},{8,40},{9,... | collective-permute-start | bytes 393224 | tf_op jit(solution)/shard_map/ppermute | solution.py:218
  22.8 0.0 copy-done.1
  22.8 0.8 %copy.24 = bf16[8,4,8,1024]{3,2,0,1:T(8,128)(2,1)} copy(bf16[8,4,8,1024]{3,2,1,0:T(8,128)(2,1)S(1)} %bitcast.35) | data formatting | bytes 1048576 | tf_op jit(solution)/shard_map/reshape | solution.py:219
  23.6 3.5 %all-to-all-start = ((bf16[4,64,1024]{2,1,0:T(8,128)(2,1)}), bf16[4,64,1024]{2,1,0:T(8,128)(2,1)S(1)}, u32[]{:S(2)}, u32[]{:S(2)}) async-start(bf16[4,64,1024]{2,1,0:T(8,128)(2,1)} %bitcast.26), calls=%async_computation | async-start | bytes 1048576 | tf_op jit(solution)/shard_map/all_to_all | solution.py:42
  27.1 0.0 collective-permute-done
  27.2 0.7 collective-permute-start.2
  27.9 0.7 collective-permute-start.7
  28.6 2.6 %collective-permute-start.1 = (bf16[256,256]{1,0:T(8,128)(2,1)S(1)}, bf16[256,256]{1,0:T(8,128)(2,1)S(1)}, u32[]{:S(2)}, u32[]{:S(2)}) collective-permute-start(bf16[256,256]{1,0:T(8,128)(2,1)S(1)} %get-tuple-element.60), channel_id=1, source_target_pairs={{0,4},{1,5},{2,6},{3,7},{4,8},{5,9},{6,10},{7,11},{8,12},{9,13},{1... | collective-permute-start | bytes 393224 | tf_op jit(solution)/shard_map/ppermute | solution.py:226
  31.2 4.0 %all-to-all-done = bf16[4,64,1024]{2,1,0:T(8,128)(2,1)S(1)} async-done(((bf16[4,64,1024]{2,1,0:T(8,128)(2,1)}), bf16[4,64,1024]{2,1,0:T(8,128)(2,1)S(1)}, u32[]{:S(2)}, u32[]{:S(2)}) %all-to-all-start) | async-done | bytes 524320 | tf_op jit(solution)/shard_map/all_to_all | solution.py:42
  35.1 1.8 %own_block.1 = (f32[256,1024]{1,0:T(8,128)S(1)}, f32[256,1024]{1,0:T(8,128)S(1)}, f32[256,1024]{1,0:T(8,128)S(1)}) custom-call(bf16[256,1024]{1,0:T(8,128)(2,1)S(1)} %bitcast.27, bf16[512,256]{1,0:T(8,128)(2,1)S(1)} %pad_maximum_fusion.kv_ref), custom_call_target="tpu_custom_call" | custom-call | flops 536870912 | bytes 8388608 | tf_op jit(solution)/shard_map/own_block/pallas_call | solution.py:181
  37.0 0.0 collective-permute-done.1.refs_1_
  37.0 0.0 collective-permute-done.2.refs_2_
  37.0 0.7 collective-permute-start.4
  37.7 0.0 collective-permute-done.7.refs_1_.refs_2_
  37.7 0.7 collective-permute-start.10
  38.4 2.6 %collective-permute-start.3 = (bf16[256,256]{1,0:T(8,128)(2,1)S(1)}, bf16[256,256]{1,0:T(8,128)(2,1)S(1)}, u32[]{:S(2)}, u32[]{:S(2)}) collective-permute-start(bf16[256,256]{1,0:T(8,128)(2,1)S(1)} %collective-permute-done.1.refs_1_), channel_id=1, source_target_pairs={{4,8},{5,9},{6,10},{7,11},{8,12},{9,13},{10,14},{11,15},{12,16},{1... | collective-permute-start | bytes 393224 | tf_op jit(solution)/shard_map/ppermute | solution.py:226
  41.0 1.6 %more_blocks.3 = (f32[256,1024]{1,0:T(8,128)S(1)}, f32[256,1024]{1,0:T(8,128)S(1)}, f32[256,1024]{1,0:T(8,128)S(1)}) custom-call(bf16[256,1024]{1,0:T(8,128)(2,1)S(1)} %bitcast.28, bf16[256,256]{1,0:T(8,128)(2,1)S(1)} %collective-permute-done.1.refs_1_, ...), custom_call_target="tpu_custom_call", output_to_operand_aliasing={{0}: (3, {}), {1}: (4, {}), {2}: (5, {})} | custom-call | flops 536870912 | bytes 8388608 | tf_op jit(solution)/shard_map/more_blocks/pallas_call | solution.py:198
  42.6 3.9 %collective-permute-done.3.refs_1_ = bf16[256,256]{1,0:T(8,128)(2,1)S(1)} collective-permute-done((bf16[256,256]{1,0:T(8,128)(2,1)S(1)}, bf16[256,256]{1,0:T(8,128)(2,1)S(1)}, u32[]{:S(2)}, u32[]{:S(2)}) %collective-permute-start.3) | collective-permute-done | bytes 131104 | tf_op jit(solution)/shard_map/ppermute | solution.py:226
  46.5 0.0 collective-permute-done.4.refs_5_
  46.5 0.7 collective-permute-start.6
  47.1 0.0 collective-permute-done.10.refs_2_.refs_6_
  47.2 0.7 collective-permute-start.11
  47.8 2.0 %collective-permute-start.5 = (bf16[256,256]{1,0:T(8,128)(2,1)S(1)}, bf16[256,256]{1,0:T(8,128)(2,1)S(1)}, u32[]{:S(2)}, u32[]{:S(2)}) collective-permute-start(bf16[256,256]{1,0:T(8,128)(2,1)S(1)} %collective-permute-done.3.refs_1_), channel_id=1, source_target_pairs={{8,12},{9,13},{10,14},{11,15},{12,16},{13,17},{14,18},{15,19},{16,... | collective-permute-start | bytes 393224 | tf_op jit(solution)/shard_map/ppermute | solution.py:226
  49.9 6.0 %collective-permute-done.5.refs_3_ = bf16[256,256]{1,0:T(8,128)(2,1)S(1)} collective-permute-done((bf16[256,256]{1,0:T(8,128)(2,1)S(1)}, bf16[256,256]{1,0:T(8,128)(2,1)S(1)}, u32[]{:S(2)}, u32[]{:S(2)}) %collective-permute-start.5) | collective-permute-done | bytes 131104 | tf_op jit(solution)/shard_map/ppermute | solution.py:226
  55.9 0.0 collective-permute-done.6.refs_7_
  55.9 0.7 collective-permute-start.9
  56.6 1.9 %collective-permute-start.8 = (bf16[256,256]{1,0:T(8,128)(2,1)S(1)}, bf16[256,256]{1,0:T(8,128)(2,1)S(1)}, u32[]{:S(2)}, u32[]{:S(2)}) collective-permute-start(bf16[256,256]{1,0:T(8,128)(2,1)S(1)} %collective-permute-done.5.refs_3_), channel_id=1, source_target_pairs={{12,16},{13,17},{14,18},{15,19},{16,20},{17,21},{18,22},{19,23},{2... | collective-permute-start | bytes 393224 | tf_op jit(solution)/shard_map/ppermute | solution.py:226
  58.5 0.0 collective-permute-done.11.refs_4_.refs_8_
  58.5 3.6 %more_blocks.5 = (f32[256,1024]{1,0:T(8,128)S(1)}, f32[256,1024]{1,0:T(8,128)S(1)}, f32[256,1024]{1,0:T(8,128)S(1)}) custom-call(bf16[256,1024]{1,0:T(8,128)(2,1)S(1)} %bitcast.30, bf16[256,256]{1,0:T(8,128)(2,1)S(1)} %collective-permute-done.3.refs_1_, ...), custom_call_target="tpu_custom_call", output_to_operand_aliasing={{0}: (9, {}), {1}: (10, {}), {2}: (11, {})} | custom-call | flops 2147483648 | bytes 8388608 | tf_op jit(solution)/shard_map/more_blocks/pallas_call | solution.py:198
  62.2 2.5 %collective-permute-done.8.refs_1_ = bf16[256,256]{1,0:T(8,128)(2,1)S(1)} collective-permute-done((bf16[256,256]{1,0:T(8,128)(2,1)S(1)}, bf16[256,256]{1,0:T(8,128)(2,1)S(1)}, u32[]{:S(2)}, u32[]{:S(2)}) %collective-permute-start.8) | collective-permute-done | bytes 131104 | tf_op jit(solution)/shard_map/ppermute | solution.py:226
  64.7 0.0 collective-permute-done.9.refs_2_
  64.7 1.1 %last_blocks.1 = bf16[256,1024]{1,0:T(8,128)(2,1)S(1)} custom-call(bf16[256,1024]{1,0:T(8,128)(2,1)S(1)} %bitcast.31, bf16[256,256]{1,0:T(8,128)(2,1)S(1)} %collective-permute-done.8.refs_1_, bf16[512,256]{1,0:T(8,128)(2,1)S(1)} %collective-permute-done.9.refs_2_, f32[256,1024]{1,0:T(8,128)S(1)} %get-tuple-element.56.refs_3_, ...), custom_call_target="tpu_custom_call" | custom-call | flops 536870912 | bytes 8388608 | tf_op jit(solution)/shard_map/last_blocks/pallas_call | solution.py:198
  65.8 12.2 %all_to_all.16 = bf16[4,64,1024]{2,1,0:T(8,128)(2,1)S(1)} all-to-all(bf16[4,64,1024]{2,1,0:T(8,128)(2,1)S(1)} %bitcast.32), channel_id=1, replica_groups={{0,1,2,3},{4,5,6,7},{8,9,10,11},{12,13,14,15},{16,17,18,19},{20,21,22,2..., dimensions={0} | all-to-all | bytes 1048576 | tf_op jit(solution)/shard_map/all_to_all | solution.py:42
  78.0 0.8 %copy.20 = bf16[4,8,8,1024]{3,2,0,1:T(8,128)(2,1)} copy(bf16[4,8,8,1024]{3,2,1,0:T(8,128)(2,1)S(1)} %bitcast.33) | data formatting | bytes 1048576 | tf_op jit(solution)/shard_map/reshape | solution.py:244
  (4 shorter events, 0.1 us)
Async XLA Ops:
  0.0 0.8 %copy-start = (bf16[64,512]{1,0:T(8,128)(2,1)S(1)}, bf16[64,512]{1,0:T(8,128)(2,1)}, u32[]{:S(2)}) copy-start(bf16[64,512]{1,0:T(8,128)(2,1)} %param.4) | copy-start | bytes 196612
  0.8 21.9 %copy-start.1 = (bf16[64,4096]{1,0:T(8,128)(2,1)S(1)}, bf16[64,4096]{1,0:T(8,128)(2,1)}, u32[]{:S(2)}) copy-start(bf16[64,4096]{1,0:T(8,128)(2,1)} %param.3) | copy-start | bytes 1572868
  11.9 15.3 %collective-permute-start = (bf16[256,256]{1,0:T(8,128)(2,1)S(1)}, bf16[256,256]{1,0:T(8,128)(2,1)S(1)}, u32[]{:S(2)}, u32[]{:S(2)}) collective-permute-start(bf16[256,256]{1,0:T(8,128)(2,1)S(1)} %bitcast.34), channel_id=1, source_target_pairs={{0,32},{1,33},{2,34},{3,35},{4,36},{5,37},{6,38},{7,39},{8,40},{9,... | collective-permute-start | bytes 393224 | tf_op jit(solution)/shard_map/ppermute | solution.py:218
  23.6 11.5 %all-to-all-start = ((bf16[4,64,1024]{2,1,0:T(8,128)(2,1)}), bf16[4,64,1024]{2,1,0:T(8,128)(2,1)S(1)}, u32[]{:S(2)}, u32[]{:S(2)}) async-start(bf16[4,64,1024]{2,1,0:T(8,128)(2,1)} %bitcast.26), calls=%async_computation | async-start | bytes 1048576 | tf_op jit(solution)/shard_map/all_to_all | solution.py:42
  27.2 9.8 %collective-permute-start.2 = (bf16[512,256]{1,0:T(8,128)(2,1)S(1)}, bf16[512,256]{1,0:T(8,128)(2,1)S(1)}, u32[]{:S(2)}, u32[]{:S(2)}) collective-permute-start(bf16[512,256]{1,0:T(8,128)(2,1)S(1)} %pad_maximum_fusion.kv_ref), channel_id=1, source_target_pairs={{32,36},{33,37},{34,38},{35,39},{36,40},{37,41},{38,42},{39,43},{4... | collective-permute-start | bytes 786440 | tf_op jit(solution)/shard_map/ppermute | solution.py:227
  27.9 9.8 %collective-permute-start.7 = (bf16[512,256]{1,0:T(8,128)(2,1)S(1)}, bf16[512,256]{1,0:T(8,128)(2,1)S(1)}, u32[]{:S(2)}, u32[]{:S(2)}) collective-permute-start(bf16[512,256]{1,0:T(8,128)(2,1)S(1)} %pad_maximum_fusion.kv_ref), channel_id=1, source_target_pairs={{0,28},{1,29},{2,30},{3,31},{4,0},{5,1},{6,2},{7,3},{8,4},{9,5},{1... | collective-permute-start | bytes 786440 | tf_op jit(solution)/shard_map/ppermute | solution.py:231
  28.6 8.4 %collective-permute-start.1 = (bf16[256,256]{1,0:T(8,128)(2,1)S(1)}, bf16[256,256]{1,0:T(8,128)(2,1)S(1)}, u32[]{:S(2)}, u32[]{:S(2)}) collective-permute-start(bf16[256,256]{1,0:T(8,128)(2,1)S(1)} %get-tuple-element.60), channel_id=1, source_target_pairs={{0,4},{1,5},{2,6},{3,7},{4,8},{5,9},{6,10},{7,11},{8,12},{9,13},{1... | collective-permute-start | bytes 393224 | tf_op jit(solution)/shard_map/ppermute | solution.py:226
  37.0 9.5 %collective-permute-start.4 = (bf16[512,256]{1,0:T(8,128)(2,1)S(1)}, bf16[512,256]{1,0:T(8,128)(2,1)S(1)}, u32[]{:S(2)}, u32[]{:S(2)}) collective-permute-start(bf16[512,256]{1,0:T(8,128)(2,1)S(1)} %collective-permute-done.2.refs_2_), channel_id=1, source_target_pairs={{32,36},{33,37},{34,38},{35,39},{36,40},{37,41},{38,42},{39,43},{4... | collective-permute-start | bytes 786440 | tf_op jit(solution)/shard_map/ppermute | solution.py:227
  37.7 9.4 %collective-permute-start.10 = (bf16[512,256]{1,0:T(8,128)(2,1)S(1)}, bf16[512,256]{1,0:T(8,128)(2,1)S(1)}, u32[]{:S(2)}, u32[]{:S(2)}) collective-permute-start(bf16[512,256]{1,0:T(8,128)(2,1)S(1)} %collective-permute-done.7.refs_1_.refs_2_), channel_id=1, source_target_pairs={{0,28},{1,29},{2,30},{3,31},{4,0},{5,1},{6,2},{7,3},{28,24},{29,25... | collective-permute-start | bytes 786440 | tf_op jit(solution)/shard_map/ppermute | solution.py:239
  38.4 8.1 %collective-permute-start.3 = (bf16[256,256]{1,0:T(8,128)(2,1)S(1)}, bf16[256,256]{1,0:T(8,128)(2,1)S(1)}, u32[]{:S(2)}, u32[]{:S(2)}) collective-permute-start(bf16[256,256]{1,0:T(8,128)(2,1)S(1)} %collective-permute-done.1.refs_1_), channel_id=1, source_target_pairs={{4,8},{5,9},{6,10},{7,11},{8,12},{9,13},{10,14},{11,15},{12,16},{1... | collective-permute-start | bytes 393224 | tf_op jit(solution)/shard_map/ppermute | solution.py:226
  46.5 9.4 %collective-permute-start.6 = (bf16[512,256]{1,0:T(8,128)(2,1)S(1)}, bf16[512,256]{1,0:T(8,128)(2,1)S(1)}, u32[]{:S(2)}, u32[]{:S(2)}) collective-permute-start(bf16[512,256]{1,0:T(8,128)(2,1)S(1)} %collective-permute-done.4.refs_5_), channel_id=1, source_target_pairs={{32,36},{33,37},{34,38},{35,39},{36,40},{37,41},{38,42},{39,43},{4... | collective-permute-start | bytes 786440 | tf_op jit(solution)/shard_map/ppermute | solution.py:227
  47.2 11.4 %collective-permute-start.11 = (bf16[512,256]{1,0:T(8,128)(2,1)S(1)}, bf16[512,256]{1,0:T(8,128)(2,1)S(1)}, u32[]{:S(2)}, u32[]{:S(2)}) collective-permute-start(bf16[512,256]{1,0:T(8,128)(2,1)S(1)} %collective-permute-done.10.refs_2_.refs_6_), channel_id=1, source_target_pairs={{0,28},{1,29},{2,30},{3,31},{24,20},{25,21},{26,22},{27,23},{28,24... | collective-permute-start | bytes 786440 | tf_op jit(solution)/shard_map/ppermute | solution.py:239
  47.8 8.1 %collective-permute-start.5 = (bf16[256,256]{1,0:T(8,128)(2,1)S(1)}, bf16[256,256]{1,0:T(8,128)(2,1)S(1)}, u32[]{:S(2)}, u32[]{:S(2)}) collective-permute-start(bf16[256,256]{1,0:T(8,128)(2,1)S(1)} %collective-permute-done.3.refs_1_), channel_id=1, source_target_pairs={{8,12},{9,13},{10,14},{11,15},{12,16},{13,17},{14,18},{15,19},{16,... | collective-permute-start | bytes 393224 | tf_op jit(solution)/shard_map/ppermute | solution.py:226
  55.9 8.8 %collective-permute-start.9 = (bf16[512,256]{1,0:T(8,128)(2,1)S(1)}, bf16[512,256]{1,0:T(8,128)(2,1)S(1)}, u32[]{:S(2)}, u32[]{:S(2)}) collective-permute-start(bf16[512,256]{1,0:T(8,128)(2,1)S(1)} %collective-permute-done.6.refs_7_), channel_id=1, source_target_pairs={{32,36},{33,37},{34,38},{35,39},{36,40},{37,41},{38,42},{39,43},{4... | collective-permute-start | bytes 786440 | tf_op jit(solution)/shard_map/ppermute | solution.py:227
  56.6 8.1 %collective-permute-start.8 = (bf16[256,256]{1,0:T(8,128)(2,1)S(1)}, bf16[256,256]{1,0:T(8,128)(2,1)S(1)}, u32[]{:S(2)}, u32[]{:S(2)}) collective-permute-start(bf16[256,256]{1,0:T(8,128)(2,1)S(1)} %collective-permute-done.5.refs_3_), channel_id=1, source_target_pairs={{12,16},{13,17},{14,18},{15,19},{16,20},{17,21},{18,22},{19,23},{2... | collective-permute-start | bytes 393224 | tf_op jit(solution)/shard_map/ppermute | solution.py:226
